TPU v7x, 32 devices: a whole 2x2x4 slice. The times are simulated.
32 devices in a mesh: group: 2 (over x), owner: 16 (over z, y, core).
Axes of the slice: x: 2, y: 2, z: 4, core: 2. Of those that a mesh axis runs over, the one named last changes fastest.
Arguments:
- tokens: bfloat16 [4096, 2048], P(('group', 'owner')), parts along dimension 0, may hold values from -6 to 6
- cotangent: bfloat16 [4096, 2048], P(('group', 'owner')), parts along dimension 0, may hold values from -6 to 6
- route_ids: int32 [4096, 3], P('group'), parts along dimension 0, may hold values from 0 to 15, as said below
- gate_probs: float32 [4096, 3], P(('group', 'owner')), parts along dimension 0, may hold values from 0.05 to 1
- w_gate: bfloat16 [16, 2048, 384], P('owner'), may hold values from -0.125 to 0.125
- w_up: bfloat16 [16, 2048, 384], P('owner'), may hold values from -0.125 to 0.125
- w_down: bfloat16 [16, 384, 2048], P('owner'), may hold values from -0.3125 to 0.3125
Outputs:
- expert_out: bfloat16 [4096, 2048], P(('group', 'owner')), parts along dimension 0
- grad_tokens: bfloat16 [4096, 2048], P(('group', 'owner')), parts along dimension 0
- grad_gates: float32 [4096, 3], P(('group', 'owner')), parts along dimension 0
- grad_w_gate: bfloat16 [32, 2048, 384], P(('group', 'owner')), parts along dimension 0
- grad_w_up: bfloat16 [32, 2048, 384], P(('group', 'owner')), parts along dimension 0
- grad_w_down: bfloat16 [32, 384, 2048], P(('group', 'owner')), parts along dimension 0
There are 2 independent parts, one for each index of `group`. A program takes and returns all parts, laid end to end along the dimension named above; an argument that names none is the same for every part. Nothing has to cross between parts.
Inputs may be any that keep to these rules, and one draw needn't show every extreme that they name: `route_ids`: each token names 3 different experts. The 128 tokens of one owner device (aligned blocks) name any one expert at most 48 times, and some expert exactly 48 times.
All inputs are finite; a program needn't handle non-finite values.
Results may differ from a plain program's by a relative error of at most 0.008.
Values may be sent and summed in bfloat16 or wider, within the bound.
No kernel may reach another device: no remote copies, remote signals or barrier semaphores. Data moves between devices by JAX's collectives and lax.ppermute only.
A program may use at most 128 MiB of HBM per device.

v0:
```python
import jax
import jax.numpy as jnp
from jax import lax
from jax.sharding import PartitionSpec as P


def expert_pass(tokens_in, cotan_in, gate_w, up_w, down_w):
    gate_pre = jnp.dot(tokens_in, gate_w, preferred_element_type=jnp.float32)
    up_pre = jnp.dot(tokens_in, up_w, preferred_element_type=jnp.float32)
    gate_sig = jax.nn.sigmoid(gate_pre)
    gate_act = gate_pre * gate_sig
    hidden = (gate_act * up_pre).astype(jnp.bfloat16)
    expert_y = jnp.dot(hidden, down_w, preferred_element_type=jnp.float32).astype(jnp.bfloat16)
    d_hidden = jnp.dot(cotan_in, down_w.T, preferred_element_type=jnp.float32)
    grad_gate_pre = (d_hidden * up_pre * gate_sig * (1.0 + gate_pre * (1.0 - gate_sig))).astype(
        jnp.bfloat16
    )
    grad_up_pre = (d_hidden * gate_act).astype(jnp.bfloat16)
    expert_dx = (
        jnp.dot(grad_gate_pre, gate_w.T, preferred_element_type=jnp.float32)
        + jnp.dot(grad_up_pre, up_w.T, preferred_element_type=jnp.float32)
    ).astype(jnp.bfloat16)
    return (expert_y, expert_dx, hidden, grad_gate_pre, grad_up_pre)


def local(tokens, cotangent, route_ids, gate_probs, w_gate, w_up, w_down):
    owner_count = lax.axis_size("owner")
    my_index = lax.axis_index("owner")
    token_rows, model_width = tokens.shape
    route_count = route_ids.shape[1]
    slot_depth = 2 * token_rows * route_count // owner_count
    assign_count = token_rows * route_count
    slot_total = owner_count * slot_depth
    expert_ids = jnp.arange(owner_count, dtype=jnp.int32)
    id_table = route_ids.reshape(owner_count, assign_count)
    my_routes = lax.dynamic_index_in_dim(id_table, my_index, 0, keepdims=False)
    one_hot = (my_routes[:, None] == expert_ids[None, :]).astype(jnp.int32)
    rank_within = jnp.sum((jnp.cumsum(one_hot, axis=0) - one_hot) * one_hot, axis=1)
    source_loads = jnp.sum((id_table == my_index).astype(jnp.int32), axis=1)
    scaled_cot = (gate_probs[:, :, None] * cotangent[:, None, :].astype(jnp.float32)).astype(
        jnp.bfloat16
    )
    token_copies = jnp.broadcast_to(tokens[:, None, :], (token_rows, route_count, model_width))
    zero_row = jnp.zeros((1, model_width), jnp.bfloat16)
    token_ext = jnp.concatenate([token_copies.reshape(assign_count, model_width), zero_row], axis=0)
    cotan_ext = jnp.concatenate([scaled_cot.reshape(assign_count, model_width), zero_row], axis=0)
    is_hot = jnp.zeros((assign_count,), dtype=bool)
    slot_target = jnp.where(is_hot, slot_total, my_routes * slot_depth + rank_within)
    slot_source = jnp.full((slot_total + 1,), assign_count, jnp.int32)
    slot_source = slot_source.at[slot_target].set(jnp.arange(assign_count, dtype=jnp.int32))[
        :slot_total
    ]
    send_tokens = token_ext[slot_source].reshape(owner_count, slot_depth, model_width)
    send_cotan = cotan_ext[slot_source].reshape(owner_count, slot_depth, model_width)
    got_tokens, got_cotan = (
        lax.all_to_all(send_tokens, "owner", split_axis=0, concat_axis=0, tiled=True),
        lax.all_to_all(send_cotan, "owner", split_axis=0, concat_axis=0, tiled=True),
    )
    live_slot = (jnp.arange(slot_depth, dtype=jnp.int32)[None, :] < source_loads[:, None]).reshape(
        slot_total
    )
    compact_pos = jnp.cumsum(live_slot.astype(jnp.int32)) - 1
    live_total = jnp.sum(source_loads)
    compact_from = jnp.full((slot_total,), slot_total, jnp.int32)
    compact_from = compact_from.at[jnp.where(live_slot, compact_pos, slot_total)].set(
        jnp.arange(slot_total, dtype=jnp.int32), mode="drop"
    )
    flat_tokens = jnp.concatenate([got_tokens.reshape(slot_total, model_width), zero_row], axis=0)
    flat_cotan = jnp.concatenate([got_cotan.reshape(slot_total, model_width), zero_row], axis=0)
    compact_tokens = flat_tokens[compact_from]
    compact_cotan = flat_cotan[compact_from]
    gate_w = w_gate[0]
    up_w = w_up[0]
    down_w = w_down[0]
    hidden_width = gate_w.shape[1]

    def block_step(turn_index, carried):
        out_rows, back_rows, grad_gate, grad_up, grad_down = carried
        row_start = turn_index * assign_count
        block_tokens = lax.dynamic_slice_in_dim(compact_tokens, row_start, assign_count, 0)
        block_cotan = lax.dynamic_slice_in_dim(compact_cotan, row_start, assign_count, 0)
        expert_y, expert_dx, hidden, grad_gate_pre, grad_up_pre = expert_pass(
            block_tokens, block_cotan, gate_w, up_w, down_w
        )
        out_rows = lax.dynamic_update_slice_in_dim(out_rows, expert_y, row_start, 0)
        back_rows = lax.dynamic_update_slice_in_dim(back_rows, expert_dx, row_start, 0)
        grad_gate = grad_gate + jnp.dot(
            block_tokens.T, grad_gate_pre, preferred_element_type=jnp.float32
        )
        grad_up = grad_up + jnp.dot(block_tokens.T, grad_up_pre, preferred_element_type=jnp.float32)
        grad_down = grad_down + jnp.dot(hidden.T, block_cotan, preferred_element_type=jnp.float32)
        return (out_rows, back_rows, grad_gate, grad_up, grad_down)

    turn_count = (live_total + assign_count - 1) // assign_count
    initial = (
        jnp.zeros((slot_total, model_width), jnp.bfloat16),
        jnp.zeros((slot_total, model_width), jnp.bfloat16),
        jnp.zeros((model_width, hidden_width), jnp.float32),
        jnp.zeros((model_width, hidden_width), jnp.float32),
        jnp.zeros((hidden_width, model_width), jnp.float32),
    )
    out_rows, back_rows, grad_gate, grad_up, grad_down = lax.fori_loop(
        0, turn_count, block_step, initial
    )
    return_pos = jnp.where(live_slot, compact_pos, 0)
    return_y = out_rows[return_pos].reshape(owner_count, slot_depth, model_width)
    return_dx = back_rows[return_pos].reshape(owner_count, slot_depth, model_width)
    came_y, came_dx = (
        lax.all_to_all(return_y, "owner", split_axis=0, concat_axis=0, tiled=True),
        lax.all_to_all(return_dx, "owner", split_axis=0, concat_axis=0, tiled=True),
    )
    pick_slot = jnp.where(is_hot, 0, slot_target)
    routed_rows = came_y.reshape(slot_total, model_width)[pick_slot]
    routed_backs = came_dx.reshape(slot_total, model_width)[pick_slot]
    grad_gate_out = grad_gate.astype(jnp.bfloat16)
    grad_up_out = grad_up.astype(jnp.bfloat16)
    grad_down_out = grad_down.astype(jnp.bfloat16)
    routed_y = routed_rows.reshape(token_rows, route_count, model_width).astype(jnp.float32)
    expert_out = jnp.sum(gate_probs[:, :, None] * routed_y, axis=1).astype(jnp.bfloat16)
    grad_tokens = jnp.sum(
        routed_backs.reshape(token_rows, route_count, model_width).astype(jnp.float32), axis=1
    ).astype(jnp.bfloat16)
    grad_gates = jnp.sum(routed_y * cotangent[:, None, :].astype(jnp.float32), axis=2)
    return (
        expert_out,
        grad_tokens,
        grad_gates,
        grad_gate_out[None],
        grad_up_out[None],
        grad_down_out[None],
    )


def solution(mesh):
    placed = (
        P(("group", "owner"), None),
        P(("group", "owner"), None),
        P("group", None),
        P(("group", "owner"), None),
        P("owner", None, None),
        P("owner", None, None),
        P("owner", None, None),
    )
    return jax.shard_map(
        local,
        mesh=mesh,
        in_specs=placed,
        out_specs=(
            P(("group", "owner"), None),
            P(("group", "owner"), None),
            P(("group", "owner"), None),
            P(("group", "owner"), None, None),
            P(("group", "owner"), None, None),
            P(("group", "owner"), None, None),
        ),
        check_vma=False,
    )
```

profile of v0, /device:TPU:13, one launch (start us, length us, event | category | flops | bytes accessed | tf_op | source)
XLA Modules:
  0.0 417.0 jit_solution(15545897432266285814)
XLA Ops:
  4.1 2.9 scatter_custom_fusion
  8.5 4.1 mul.90
  12.6 4.5 %mul.91 = f32[384,2048]{1,0:T(8,128)S(1)} reshape(f32[128,3,2048]{2,1,0:T(4,128)} %mul.90) | data formatting | bytes 6291456 | tf_op jit(solution)/shard_map/mul | solution.py:40
  17.5 4.4 %gather_fusion.2 = bf16[768,2048]{1,0:T(8,128)(2,1)} fusion(bf16[385,2048]{1,0:T(8,128)(2,1)S(1)} %concatenate.14, s32[1024]{0:T(1024)S(1)} %pad_clamp_fusion.3), kind=kCustom, calls=%fused_computation.2 | custom fusion | bytes 6294528 | tf_op jit(solution)/shard_map/gather | solution.py:54
  21.9 6.7 %all-to-all-start.1 = ((bf16[16,48,2048]{2,1,0:T(8,128)(2,1)}), bf16[16,48,2048]{2,1,0:T(8,128)(2,1)}, u32[]{:S(2)}, u32[]{:S(2)}) async-start(bf16[16,48,2048]{2,1,0:T(8,128)(2,1)} %bitcast.93), calls=%async_computation.1 | async-start | bytes 6291456 | tf_op jit(solution)/shard_map/all_to_all | solution.py:57
  29.6 2.5 reshape.227
  33.6 4.3 %gather_fusion = bf16[768,2048]{1,0:T(8,128)(2,1)} fusion(bf16[385,2048]{1,0:T(8,128)(2,1)S(1)} %concatenate.12, s32[1024]{0:T(1024)S(1)} %pad_clamp_fusion.3), kind=kCustom, calls=%fused_computation | custom fusion | bytes 6294528 | tf_op jit(solution)/shard_map/gather | solution.py:53
  37.9 60.6 %all-to-all-done.1 = bf16[16,48,2048]{2,1,0:T(8,128)(2,1)} async-done(((bf16[16,48,2048]{2,1,0:T(8,128)(2,1)}), bf16[16,48,2048]{2,1,0:T(8,128)(2,1)}, u32[]{:S(2)}, u32[]{:S(2)}) %all-to-all-start.1) | async-done | bytes 3145760 | tf_op jit(solution)/shard_map/all_to_all | solution.py:57
  98.5 4.9 %all-to-all-start = ((bf16[16,48,2048]{2,1,0:T(8,128)(2,1)}), bf16[16,48,2048]{2,1,0:T(8,128)(2,1)}, u32[]{:S(2)}, u32[]{:S(2)}) async-start(bf16[16,48,2048]{2,1,0:T(8,128)(2,1)} %bitcast.91), calls=%async_computation | async-start | bytes 6291456 | tf_op jit(solution)/shard_map/all_to_all | solution.py:56
  105.8 3.7 scatter_custom_fusion.1
  109.5 2.1 concatenate.15
  111.6 4.3 %gather_fusion.3 = bf16[768,2048]{1,0:T(8,128)(2,1)} fusion(bf16[769,2048]{1,0:T(8,128)(2,1)S(1)} %concatenate.15, s32[1024]{0:T(1024)S(1)} %pad_clamp_fusion.2), kind=kCustom, calls=%fused_computation.3 | custom fusion | bytes 6294528 | tf_op jit(solution)/shard_map/gather | solution.py:71
  115.9 57.5 %all-to-all-done = bf16[16,48,2048]{2,1,0:T(8,128)(2,1)} async-done(((bf16[16,48,2048]{2,1,0:T(8,128)(2,1)}), bf16[16,48,2048]{2,1,0:T(8,128)(2,1)}, u32[]{:S(2)}, u32[]{:S(2)}) %all-to-all-start) | async-done | bytes 3145760 | tf_op jit(solution)/shard_map/all_to_all | solution.py:56
  173.4 2.1 concatenate.13
  175.5 4.3 %gather_fusion.1 = bf16[768,2048]{1,0:T(8,128)(2,1)} fusion(bf16[769,2048]{1,0:T(8,128)(2,1)S(1)} %concatenate.13, s32[1024]{0:T(1024)S(1)} %pad_clamp_fusion.2), kind=kCustom, calls=%fused_computation.1 | custom fusion | bytes 6294528 | tf_op jit(solution)/shard_map/gather | solution.py:70
  180.2 2.1 broadcast.163.clone
  188.1 37.3 %while.18 = (s32[]{:T(128)}, bf16[768,2048]{1,0:T(8,128)(2,1)S(1)}, bf16[768,2048]{1,0:T(8,128)(2,1)}, f32[2048,384]{1,0:T(8,128)}, f32[2048,384]{1,0:T(8,128)},...) while((s32[]{:T(128)}, bf16[768,2048]{1,0:T(8,128)(2,1)S(1)}, ...), condition=%wide.region_11.12_spmd, body=%wide.region_10.11_spmd.sunk | while | flops 5442748416 | bytes 196903504 | solution.py:102
  188.1 3.0 fusion.83
  206.7 3.0 fusion.83
  225.3 9.4 %gather_fusion.6 = bf16[768,2048]{1,0:T(8,128)(2,1)} fusion(bf16[768,2048]{1,0:T(8,128)(2,1)} %get-tuple-element.74, s32[1024]{0:T(1024)S(1)} %pad_clamp_fusion.1), kind=kCustom, calls=%fused_computation.6 | custom fusion | bytes 6294528 | tf_op jit(solution)/shard_map/gather | solution.py:107
  234.7 4.8 %all-to-all-start.3 = ((bf16[16,48,2048]{2,1,0:T(8,128)(2,1)}), bf16[16,48,2048]{2,1,0:T(8,128)(2,1)}, u32[]{:S(2)}, u32[]{:S(2)}) async-start(bf16[16,48,2048]{2,1,0:T(8,128)(2,1)} %bitcast.94), calls=%async_computation.3 | async-start | bytes 6291456 | tf_op jit(solution)/shard_map/all_to_all | solution.py:110
  239.5 4.3 %gather_fusion.4 = bf16[768,2048]{1,0:T(8,128)(2,1)} fusion(bf16[768,2048]{1,0:T(8,128)(2,1)S(1)} %get-tuple-element.73, s32[1024]{0:T(1024)S(1)} %pad_clamp_fusion.1), kind=kCustom, calls=%fused_computation.4 | custom fusion | bytes 6294528 | tf_op jit(solution)/shard_map/gather | solution.py:106
  243.8 65.7 %all-to-all-done.3 = bf16[16,48,2048]{2,1,0:T(8,128)(2,1)} async-done(((bf16[16,48,2048]{2,1,0:T(8,128)(2,1)}), bf16[16,48,2048]{2,1,0:T(8,128)(2,1)}, u32[]{:S(2)}, u32[]{:S(2)}) %all-to-all-start.3) | async-done | bytes 3145760 | tf_op jit(solution)/shard_map/all_to_all | solution.py:110
  309.5 13.6 %all-to-all-start.2 = ((bf16[16,48,2048]{2,1,0:T(8,128)(2,1)}), bf16[16,48,2048]{2,1,0:T(8,128)(2,1)}, u32[]{:S(2)}, u32[]{:S(2)}) async-start(bf16[16,48,2048]{2,1,0:T(8,128)(2,1)} %bitcast.92), calls=%async_computation.2 | async-start | bytes 6291456 | tf_op jit(solution)/shard_map/all_to_all | solution.py:109
  323.1 2.3 convert_element_type.72
  328.8 7.4 %gather_fusion.7 = bf16[384,2048]{1,0:T(8,128)(2,1)} fusion(bf16[768,2048]{1,0:T(8,128)(2,1)} %bitcast.13, s32[1024]{0:T(1024)S(1)} %pad_clamp_fusion), kind=kCustom, calls=%fused_computation.7 | custom fusion | bytes 3147264 | tf_op jit(solution)/shard_map/gather | solution.py:114
  336.2 4.0 reshape.239
  340.2 52.8 %all-to-all-done.2 = bf16[16,48,2048]{2,1,0:T(8,128)(2,1)} async-done(((bf16[16,48,2048]{2,1,0:T(8,128)(2,1)}), bf16[16,48,2048]{2,1,0:T(8,128)(2,1)}, u32[]{:S(2)}, u32[]{:S(2)}) %all-to-all-start.2) | async-done | bytes 3145760 | tf_op jit(solution)/shard_map/all_to_all | solution.py:109
  393.0 7.4 %gather_fusion.5 = bf16[384,2048]{1,0:T(8,128)(2,1)} fusion(bf16[768,2048]{1,0:T(8,128)(2,1)} %bitcast.11, s32[1024]{0:T(1024)S(1)} %pad_clamp_fusion), kind=kCustom, calls=%fused_computation.5 | custom fusion | bytes 3147264 | tf_op jit(solution)/shard_map/gather | solution.py:113
  400.3 5.6 %reshape.241 = f32[128,3,2048]{2,1,0:T(4,128)} reshape(bf16[384,2048]{1,0:T(8,128)(2,1)} %gather_fusion.5) | data formatting | bytes 4718592 | tf_op jit(solution)/shard_map/convert_element_type | solution.py:118
  405.9 6.5 %multiply_reduce_fusion = (f32[128,3]{1,0:T(8,128)S(1)}, bf16[128,2048]{1,0:T(8,128)(2,1)}) fusion(f32[128,3,2048]{2,1,0:T(4,128)} %reshape.241, f32[128,2048]{1,0:T(8,128)S(1)} %copy-done.15, f32[128,3]{1,0:T(8,128)S(1)} %copy-done.17), kind=kLoop, calls=%fused_computation.37 | loop fusion | flops 2883200 | bytes 4721664 | tf_op jit(solution)/shard_map/reduce_sum | solution.py:123
  413.1 3.9 reduce_sum.73
  (127 shorter events, 50.5 us)
Async XLA Ops:
  21.9 6.7 %copy-start.18 = (bf16[128,2048]{1,0:T(8,128)(2,1)S(1)}, bf16[128,2048]{1,0:T(8,128)(2,1)}, u32[]{:S(2)}) copy-start(bf16[128,2048]{1,0:T(8,128)(2,1)} %param.9) | copy-start | bytes 1572868
  21.9 76.6 %all-to-all-start.1 = ((bf16[16,48,2048]{2,1,0:T(8,128)(2,1)}), bf16[16,48,2048]{2,1,0:T(8,128)(2,1)}, u32[]{:S(2)}, u32[]{:S(2)}) async-start(bf16[16,48,2048]{2,1,0:T(8,128)(2,1)} %bitcast.93), calls=%async_computation.1 | async-start | bytes 6291456 | tf_op jit(solution)/shard_map/all_to_all | solution.py:57
  98.5 4.9 %copy-start.19 = (s32[2048,3]{0,1:T(4,128)S(1)}, s32[2048,3]{0,1:T(4,128)}, u32[]{:S(2)}) copy-start(s32[2048,3]{0,1:T(4,128)} %param.11) | copy-start | bytes 73732
  98.5 74.9 %all-to-all-start = ((bf16[16,48,2048]{2,1,0:T(8,128)(2,1)}), bf16[16,48,2048]{2,1,0:T(8,128)(2,1)}, u32[]{:S(2)}, u32[]{:S(2)}) async-start(bf16[16,48,2048]{2,1,0:T(8,128)(2,1)} %bitcast.91), calls=%async_computation | async-start | bytes 6291456 | tf_op jit(solution)/shard_map/all_to_all | solution.py:56
  188.1 3.0 copy-start.11
  188.1 3.3 copy-start.13
  191.1 2.0 copy-start.14
  191.1 2.4 copy-start.21
  194.7 2.0 copy-start
  197.6 2.3 copy-start.1
  198.5 2.1 copy-start.8
  199.9 2.1 copy-start.6
  200.6 2.3 copy-start.2
  202.0 2.0 copy-start.9
  206.7 3.1 copy-start.11
  206.7 3.3 copy-start.13
  209.7 2.0 copy-start.14
  209.7 2.4 copy-start.21
  213.3 2.0 copy-start
  216.3 2.3 copy-start.1
  217.1 2.1 copy-start.8
  218.6 2.1 copy-start.6
  219.2 2.3 copy-start.2
  220.7 2.0 copy-start.9
  234.7 74.8 %all-to-all-start.3 = ((bf16[16,48,2048]{2,1,0:T(8,128)(2,1)}), bf16[16,48,2048]{2,1,0:T(8,128)(2,1)}, u32[]{:S(2)}, u32[]{:S(2)}) async-start(bf16[16,48,2048]{2,1,0:T(8,128)(2,1)} %bitcast.94), calls=%async_computation.3 | async-start | bytes 6291456 | tf_op jit(solution)/shard_map/all_to_all | solution.py:110
  309.5 15.9 %copy-start.20 = (s32[384]{0:T(512)S(1)}, s32[384]{0:T(512)}, u32[]{:S(2)}) copy-start(s32[384]{0:T(512)} %get-tuple-element.96) | copy-start | bytes 4612
  309.5 15.9 %copy-start.4 = (f32[384,2048]{1,0:T(8,128)S(1)}, f32[384,2048]{1,0:T(8,128)}, u32[]{:S(2)}) copy-start(f32[384,2048]{1,0:T(8,128)} %get-tuple-element.77) | copy-start | bytes 9437188
  309.5 83.5 %all-to-all-start.2 = ((bf16[16,48,2048]{2,1,0:T(8,128)(2,1)}), bf16[16,48,2048]{2,1,0:T(8,128)(2,1)}, u32[]{:S(2)}, u32[]{:S(2)}) async-start(bf16[16,48,2048]{2,1,0:T(8,128)(2,1)} %bitcast.92), calls=%async_computation.2 | async-start | bytes 6291456 | tf_op jit(solution)/shard_map/all_to_all | solution.py:109
  323.1 3.7 copy-start.7
  323.1 3.7 copy-start.10
  400.3 5.6 %copy-start.15 = (f32[128,2048]{1,0:T(8,128)S(1)}, f32[128,2048]{1,0:T(8,128)}, u32[]{:S(2)}) copy-start(f32[128,2048]{1,0:T(8,128)} %convert_element_type.72) | copy-start | bytes 3145732
  400.3 5.6 %copy-start.17 = (f32[128,3]{1,0:T(8,128)S(1)}, f32[128,3]{1,0:T(8,128)}, u32[]{:S(2)}) copy-start(f32[128,3]{1,0:T(8,128)} %copy-done.16) | copy-start | bytes 4612
  (7 other events, 10.6 us)
where the time goes:
time: 425 us; the launch traced here: 417 us
  waiting for transfers between devices  237 us (56%)
  local copies, waits for them, and re-layouts  105 us (25%)
  starting transfers between devices  29.9 us (7%)
  matrix products  24 us (6%)
  other arithmetic  19.2 us (5%)
    all_to_all x1, waiting for transfers between devices, local(): lax.all_to_all(return_dx, 'owner', split_axis=0, concat_axis=0, tiled=True)  65.7 us
    all_to_all x1, waiting for transfers between devices, local(): lax.all_to_all(send_cotan, 'owner', split_axis=0, concat_axis=0, tiled=True)  60.6 us
    all_to_all x1, waiting for transfers between devices, local(): lax.all_to_all(send_tokens, 'owner', split_axis=0, concat_axis=0, tiled=T...  57.5 us
    all_to_all x1, waiting for transfers between devices, local(): lax.all_to_all(return_y, 'owner', split_axis=0, concat_axis=0, tiled=True)  52.8 us
    all_to_all x1, starting transfers between devices, local(): lax.all_to_all(return_y, 'owner', split_axis=0, concat_axis=0, tiled=True)  13.6 us
    while x52, local copies, waits for them, and re-layouts  12.9 us
    gather x1, local copies, waits for them, and re-layouts, local(): back_rows[return_pos].reshape(owner_count, slot_depth, model_width)  9.4 us
    mul x2, local copies, waits for them, and re-layouts, local(): gate_probs[:, :, None] * cotangent[:, None, :].astype(jnp.float32)  8.6 us
  transfers between devices with their start and end apart: 4, of which 4 were waited for; matrix products, arithmetic and copies ran while one was open for 10% of the time, Pallas kernels for 0%

commit v1 on v0

v1 whole, which is shorter than its diff:
```python
import jax
import jax.numpy as jnp
from jax import lax
from jax.sharding import PartitionSpec as P

F32 = jnp.float32
BF16 = jnp.bfloat16
LANES = 128


def rounded(value):
    return lax.reduce_precision(value, exponent_bits=8, mantissa_bits=7)


def split_three(value):
    high = rounded(value)
    rest = value - high
    middle = rounded(rest)
    low = rounded(rest - middle)
    return high, middle, low


def expert_pass(rows_x, rows_c, gate_w, up_w, down_w):
    def fwd(a, w):
        return jnp.einsum("erd,edf->erf", a, w, preferred_element_type=F32)

    def bwd(a, w):
        return jnp.einsum("erf,edf->erd", a, w, preferred_element_type=F32)

    gate_pre = fwd(rows_x, gate_w)
    up_pre = fwd(rows_x, up_w)
    gate_sig = jax.nn.sigmoid(gate_pre)
    gate_act = gate_pre * gate_sig
    hidden = (gate_act * up_pre).astype(BF16)
    expert_y = fwd(hidden, down_w).astype(BF16)
    d_hidden = bwd(rows_c, down_w)
    grad_gate_pre = (d_hidden * up_pre * gate_sig * (1.0 + gate_pre * (1.0 - gate_sig))).astype(BF16)
    grad_up_pre = (d_hidden * gate_act).astype(BF16)
    expert_dx = (bwd(grad_gate_pre, gate_w) + bwd(grad_up_pre, up_w)).astype(BF16)
    return expert_y, expert_dx, hidden, grad_gate_pre, grad_up_pre


def local(tokens, cotangent, route_ids, gate_probs, w_gate, w_up, w_down):
    owner_count = lax.axis_size("owner")
    me = lax.axis_index("owner")
    token_rows, width = tokens.shape
    route_count = route_ids.shape[1]
    depth = 2 * token_rows * route_count // owner_count
    side = 2 if owner_count % 4 == 0 else 1
    plane = 2 * side
    ring = owner_count // plane
    core = me % 2
    column = me % plane
    my_z = me // plane
    chip_slots = 2 * depth

    ring_up = [(i, (i + plane) % owner_count) for i in range(owner_count)]
    across = [(i, i ^ 2) for i in range(owner_count)]
    partner = [(i, i ^ 1) for i in range(owner_count)]

    def hop(value, pairs):
        return lax.ppermute(value, "owner", pairs)

    both_gate = jnp.stack([w_gate[0], hop(w_gate[0], partner)])
    both_up = jnp.stack([w_up[0], hop(w_up[0], partner)])
    both_down = jnp.stack([w_down[0], hop(w_down[0], partner)])

    offsets = jnp.arange(plane, dtype=jnp.int32)
    plane_experts = my_z * plane + jnp.bitwise_xor(column, (offsets // 2) * 2 + offsets % 2)

    id_table = route_ids.reshape(ring, plane, token_rows, route_count)
    line_ids = lax.dynamic_index_in_dim(id_table, column, 1, keepdims=False)
    slot_range = jnp.arange(depth, dtype=jnp.int32)

    p_parts = jnp.concatenate(split_three(gate_probs), axis=1).astype(BF16)
    pad = jnp.zeros((token_rows, LANES - p_parts.shape[1]), BF16)
    block = jnp.concatenate([tokens, cotangent, p_parts, pad], axis=1)

    blocks = [block]
    for _ in range(ring - 1):
        blocks.append(hop(blocks[-1], ring_up))

    def prepare(step):
        ids = lax.dynamic_index_in_dim(line_ids, (my_z - step) % ring, 0, keepdims=False)
        data = blocks[step]
        parts = data[:, 2 * width : 2 * width + 3 * route_count].astype(F32)
        probs = (
            parts[:, :route_count]
            + parts[:, route_count : 2 * route_count]
            + parts[:, 2 * route_count :]
        )
        match = ids[None, :, :] == plane_experts[:, None, None]
        named = jnp.any(match, axis=2)
        rank = jnp.cumsum(named.astype(jnp.int32), axis=1) - 1
        pick = named[:, None, :] & (rank[:, None, :] == slot_range[None, :, None])
        prob = jnp.sum(jnp.where(match, probs[None], 0.0), axis=2)
        slot_prob = jnp.sum(jnp.where(pick, prob[:, None, :], 0.0), axis=2)
        pick_flat = pick.reshape(plane * depth, token_rows)
        return ids, data, match, pick_flat, slot_prob.reshape(plane * depth)

    rows_x, rows_c, packs = [], [], []
    for step in range(ring):
        ids, data, match, pick, slot_prob = prepare(step)
        chooser = pick.astype(BF16)
        sel_x = jnp.dot(chooser, data[:, :width], preferred_element_type=F32).astype(BF16)
        sel_c = jnp.dot(chooser, data[:, width : 2 * width], preferred_element_type=F32)
        sel_c = (sel_c * slot_prob[:, None]).astype(BF16)
        own_x = sel_x[:chip_slots].reshape(2, depth, width)
        own_c = sel_c[:chip_slots].reshape(2, depth, width)
        if side == 2:
            sent = jnp.concatenate([sel_x[chip_slots:], sel_c[chip_slots:]], axis=1)
            got = hop(sent, across).reshape(2, depth, 2 * width)
            own_x = jnp.concatenate([own_x, got[:, :, :width]], axis=1)
            own_c = jnp.concatenate([own_c, got[:, :, width:]], axis=1)
        rows_x.append(own_x)
        rows_c.append(own_c)
        packs.append((data, match, pick, slot_prob))

    results = [
        expert_pass(rows_x[step], rows_c[step], both_gate, both_up, both_down)
        for step in range(ring)
    ]

    def combine(step):
        data, match, pick, slot_prob = packs[step]
        out_y, out_dx = results[step][:2]
        near_y = out_y[:, :depth].reshape(chip_slots, width)
        near_dx = out_dx[:, :depth].reshape(chip_slots, width)
        if side == 2:
            sent = jnp.concatenate([out_y[:, depth:], out_dx[:, depth:]], axis=2)
            got = hop(sent.reshape(chip_slots, 2 * width), across)
            near_y = jnp.concatenate([near_y, got[:, :width]], axis=0)
            near_dx = jnp.concatenate([near_dx, got[:, width:]], axis=0)
        spread = pick.T
        weight = jnp.where(spread, slot_prob[None, :], 0.0)
        weight_high = rounded(weight)
        weight_low = (weight - weight_high).astype(BF16)
        part_y = jnp.dot(
            weight_high.astype(BF16), near_y, preferred_element_type=F32
        ) + jnp.dot(weight_low, near_y, preferred_element_type=F32)
        part_dx = jnp.dot(spread.astype(BF16), near_dx, preferred_element_type=F32)
        dots = lax.dot_general(
            data[:, width : 2 * width],
            near_y,
            (((1,), (1,)), ((), ())),
            preferred_element_type=F32,
        )
        per_expert = jnp.sum(
            jnp.where(spread, dots, 0.0).reshape(token_rows, plane, depth), axis=2
        )
        part_gates = jnp.sum(jnp.where(match, per_expert.T[:, :, None], 0.0), axis=0)
        return part_y, part_dx, part_gates

    def pack_out(part_y, part_dx, part_gates):
        gates = jnp.concatenate(split_three(part_gates), axis=1)
        return jnp.concatenate(
            [part_y.astype(BF16), part_dx.astype(BF16), gates.astype(BF16), pad], axis=1
        )

    def unpack(value):
        value = value.astype(F32)
        gates = value[:, 2 * width : 2 * width + 3 * route_count]
        gates = gates.reshape(token_rows, 3, route_count).sum(axis=1)
        return value[:, :width], value[:, width : 2 * width], gates

    running = None
    for step in list(range(1, ring)) + [0]:
        part = combine(step)
        if running is not None:
            part = tuple(a + b for a, b in zip(part, unpack(running)))
        if step != 0:
            running = hop(pack_out(*part), ring_up)
    expert_out, grad_tokens, grad_gates = part

    all_x = jnp.concatenate(rows_x, axis=1)
    all_c = jnp.concatenate(rows_c, axis=1)
    hidden = jnp.concatenate([r[2] for r in results], axis=1)
    grad_gate_pre = jnp.concatenate([r[3] for r in results], axis=1)
    grad_up_pre = jnp.concatenate([r[4] for r in results], axis=1)

    def outer(a, b, which):
        return jnp.einsum("rm,rn->mn", a[which], b[which], preferred_element_type=F32)

    outs = []
    for left, right in ((all_x, grad_gate_pre), (all_x, grad_up_pre), (hidden, all_c)):
        theirs = outer(left, right, 1).astype(BF16)
        mine = outer(left, right, 0)
        outs.append((mine + hop(theirs, partner).astype(F32)).astype(BF16)[None])

    return (
        expert_out.astype(BF16),
        grad_tokens.astype(BF16),
        grad_gates,
        outs[0],
        outs[1],
        outs[2],
    )


def solution(mesh):
    rows = P(("group", "owner"), None)
    stacked = P(("group", "owner"), None, None)
    weights = P("owner", None, None)
    return jax.shard_map(
        local,
        mesh=mesh,
        in_specs=(rows, rows, P("group", None), rows, weights, weights, weights),
        out_specs=(rows, rows, rows, stacked, stacked, stacked),
        check_vma=False,
    )
```

time: 425 us -> 369 us (0.87)
  the two profiles are of different devices: /device:TPU:13 before, /device:TPU:0 now
where the time goes in v1:
time: 369 us; the launch traced here: 365 us
  waiting for transfers between devices  168 us (46%)
  matrix products  117 us (32%)
  local copies, waits for them, and re-layouts  43.4 us (12%)
  other arithmetic  20.3 us (6%)
  starting transfers between devices  13.1 us (4%)
    ppermute x20, waiting for transfers between devices, hop(): return lax.ppermute(value, 'owner', pairs)  168 us
    dot_general x12, matrix products, bwd(): return jnp.einsum('erf,edf->erd', a, w, preferred_element_type=F32)  38.2 us
    dot_general x12, matrix products, fwd(): return jnp.einsum('erd,edf->erf', a, w, preferred_element_type=F32)  31.8 us
    dot_general x6, matrix products, outer(): jnp.einsum('rm,rn->mn', a[which], b[which], preferred_element_type=F32)  21.8 us
    ppermute x20, starting transfers between devices, hop(): return lax.ppermute(value, 'owner', pairs)  13.1 us
    unnamed x167, local copies, waits for them, and re-layouts  11 us
    concatenate x3, local copies, waits for them, and re-layouts, pack_out(): jnp.concatenate([part_y.astype(BF16), part_dx.astype(BF16), gates.astype(...  7.54 us
  transfers between devices with their start and end apart: 20, of which 12 were waited for; matrix products, arithmetic and copies ran while one was open for 39% of the time, Pallas kernels for 0%

profile of v1, /device:TPU:0, one launch (start us, length us, event | category | flops | bytes accessed | tf_op | source)
XLA Modules:
  0.0 364.6 jit_solution(17252710724208509472)
XLA Ops:
  1.8 3.1 concatenate.121
  4.9 3.1 collective-permute-start.5
  12.1 22.0 %collective-permute-done.5 = bf16[128,4224]{1,0:T(8,128)(2,1)} collective-permute-done((bf16[128,4224]{1,0:T(8,128)(2,1)}, bf16[128,4224]{1,0:T(8,128)(2,1)}, u32[]{:S(2)}, u32[]{:S(2)}) %collective-permute-start.5) | collective-permute-done | bytes 1081376 | tf_op jit(solution)/shard_map/ppermute | solution.py:62
  36.6 24.7 %collective-permute-done.6 = bf16[128,4224]{1,0:T(8,128)(2,1)} collective-permute-done((bf16[128,4224]{1,0:T(8,128)(2,1)}, bf16[128,4224]{1,0:T(8,128)(2,1)}, u32[]{:S(2)}, u32[]{:S(2)}) %collective-permute-start.6) | collective-permute-done | bytes 1081376 | tf_op jit(solution)/shard_map/ppermute | solution.py:62
  64.3 23.8 %collective-permute-done.7 = bf16[128,4224]{1,0:T(8,128)(2,1)} collective-permute-done((bf16[128,4224]{1,0:T(8,128)(2,1)}, bf16[128,4224]{1,0:T(8,128)(2,1)}, u32[]{:S(2)}, u32[]{:S(2)}) %collective-permute-start.7) | collective-permute-done | bytes 1081376 | tf_op jit(solution)/shard_map/ppermute | solution.py:62
  102.8 8.6 %collective-permute-done = bf16[96,4096]{1,0:T(8,128)(2,1)} collective-permute-done((bf16[96,4096]{1,0:T(8,128)(2,1)}, bf16[96,4096]{1,0:T(8,128)(2,1)}, u32[]{:S(2)}, u32[]{:S(2)}) %collective-permute-start) | collective-permute-done | bytes 786464 | tf_op jit(solution)/shard_map/ppermute | solution.py:62
  113.9 14.4 %collective-permute-done.12 = bf16[96,4096]{1,0:T(8,128)(2,1)} collective-permute-done((bf16[96,4096]{1,0:T(8,128)(2,1)}, bf16[96,4096]{1,0:T(8,128)(2,1)}, u32[]{:S(2)}, u32[]{:S(2)}) %collective-permute-start.12) | collective-permute-done | bytes 786464 | tf_op jit(solution)/shard_map/ppermute | solution.py:62
  130.7 3.0 fusion.36
  133.7 11.3 %collective-permute-done.10 = bf16[96,4096]{1,0:T(8,128)(2,1)S(1)} collective-permute-done((bf16[96,4096]{1,0:T(8,128)(2,1)S(1)}, bf16[96,4096]{1,0:T(8,128)(2,1)S(1)}, u32[]{:S(2)}, u32[]{:S(2)}) %collective-permute-start.10) | collective-permute-done | bytes 786464 | tf_op jit(solution)/shard_map/ppermute | solution.py:62
  145.2 3.0 fusion.32
  153.5 5.0 %collective-permute-done.8 = bf16[96,4096]{1,0:T(8,128)(2,1)S(1)} collective-permute-done((bf16[96,4096]{1,0:T(8,128)(2,1)S(1)}, bf16[96,4096]{1,0:T(8,128)(2,1)S(1)}, u32[]{:S(2)}, u32[]{:S(2)}) %collective-permute-start.8) | collective-permute-done | bytes 786464 | tf_op jit(solution)/shard_map/ppermute | solution.py:62
  158.7 5.2 %fusion.28 = f32[2,96,384]{2,1,0:T(8,128)S(1)} fusion(bf16[2,48,2048]{2,1,0:T(8,128)(2,1)S(1)} %get-tuple-element.20, bf16[2,48,2048]{2,1,0:T(8,128)(2,1)S(1)} %bitcast.206, bf16[1,384,2048]{2,1,0:T(8,128)(2,1)} %bitcast.12, bf16[1,384,2048]{2,1,0:T(8,128)(2,1)} %param.13), kind=kOutput, calls=%fused_computation.75 | convolution fusion | flops 305135616 | bytes 4227072 | tf_op jit(solution)/shard_map/erf,edf->erd/dot_general | solution.py:28
  166.6 3.0 fusion.24
  174.9 2.8 convolution_convert_fusion.5
  177.7 3.0 fusion.168
  180.9 3.0 fusion.3
  191.7 3.0 fusion.167
  194.7 3.0 fusion.5
  206.7 3.1 fusion.166
  209.9 3.0 fusion.7
  221.6 3.0 fusion.169
  224.6 3.0 fusion.1
  243.1 8.6 %collective-permute-done.4 = bf16[96,4096]{1,0:T(8,128)(2,1)} collective-permute-done((bf16[96,4096]{1,0:T(8,128)(2,1)}, bf16[96,4096]{1,0:T(8,128)(2,1)}, u32[]{:S(2)}, u32[]{:S(2)}) %collective-permute-start.4) | collective-permute-done | bytes 786464 | tf_op jit(solution)/shard_map/ppermute | solution.py:62
  265.1 3.8 %convolution_convert_fusion = bf16[384,2048]{1,0:T(8,128)(2,1)} fusion(bf16[2,384,2048]{2,1,0:T(8,128)(2,1)} %copy-done.16, bf16[2,384,384]{2,1,0:T(8,128)(2,1)S(1)} %pad_maximum_fusion.21), kind=kOutput, calls=%fused_computation.6 | convolution fusion | flops 604766208 | bytes 3440640 | tf_op jit(solution)/shard_map/rm,rn->mn/dot_general | solution.py:182
  269.2 20.0 %collective-permute-done.14 = bf16[128,4224]{1,0:T(8,128)(2,1)S(1)} collective-permute-done((bf16[128,4224]{1,0:T(8,128)(2,1)}, bf16[128,4224]{1,0:T(8,128)(2,1)S(1)}, u32[]{:S(2)}, u32[]{:S(2)}) %collective-permute-start.14) | collective-permute-done | bytes 1081376 | tf_op jit(solution)/shard_map/ppermute | solution.py:62
  301.0 4.0 %convolution_convert_fusion.1 = bf16[2048,384]{1,0:T(8,128)(2,1)} fusion(bf16[2,384,2048]{2,1,0:T(8,128)(2,1)} %copy-done.60, bf16[2,384,384]{2,1,0:T(8,128)(2,1)S(1)} %pad_maximum_fusion.20), kind=kOutput, calls=%fused_computation.7 | convolution fusion | flops 604766208 | bytes 3440640 | tf_op jit(solution)/shard_map/rm,rn->mn/dot_general | solution.py:182
  308.4 17.0 %collective-permute-done.15 = bf16[128,4224]{1,0:T(8,128)(2,1)S(1)} collective-permute-done((bf16[128,4224]{1,0:T(8,128)(2,1)}, bf16[128,4224]{1,0:T(8,128)(2,1)S(1)}, u32[]{:S(2)}, u32[]{:S(2)}) %collective-permute-start.15) | collective-permute-done | bytes 1081376 | tf_op jit(solution)/shard_map/ppermute | solution.py:62
  331.9 3.0 concatenate.142
  335.6 4.2 %fusion.20 = bf16[1,384,2048]{2,1,0:T(8,128)(2,1)} fusion(bf16[384,2048]{1,0:T(8,128)(2,1)} %collective-permute-done.19, bf16[2,384,2048]{2,1,0:T(8,128)(2,1)} %copy-done.16, bf16[2,384,384]{2,1,0:T(8,128)(2,1)S(1)} %copy-done.15), kind=kOutput, calls=%fused_computation.53 | convolution fusion | flops 606339072 | bytes 5013504 | tf_op jit(solution)/shard_map/rm,rn->mn/dot_general | solution.py:182
  339.8 3.8 %fusion.19 = bf16[1,2048,384]{2,1,0:T(8,128)(2,1)} fusion(bf16[2048,384]{1,0:T(8,128)(2,1)} %collective-permute-done.18, bf16[2,384,2048]{2,1,0:T(8,128)(2,1)S(1)} %copy-done.62, bf16[2,384,384]{2,1,0:T(8,128)(2,1)S(1)} %copy-done.33), kind=kOutput, calls=%fused_computation.52 | convolution fusion | flops 606339072 | bytes 5013504 | tf_op jit(solution)/shard_map/rm,rn->mn/dot_general | solution.py:182
  343.6 3.7 %fusion.18 = bf16[1,2048,384]{2,1,0:T(8,128)(2,1)} fusion(bf16[2048,384]{1,0:T(8,128)(2,1)} %collective-permute-done.17, bf16[2,384,2048]{2,1,0:T(8,128)(2,1)S(1)} %copy-done.62, bf16[2,384,384]{2,1,0:T(8,128)(2,1)S(1)} %copy-done.35), kind=kOutput, calls=%fused_computation.51 | convolution fusion | flops 606339072 | bytes 5013504 | tf_op jit(solution)/shard_map/rm,rn->mn/dot_general | solution.py:182
  347.4 11.5 %collective-permute-done.16 = bf16[128,4224]{1,0:T(8,128)(2,1)S(1)} collective-permute-done((bf16[128,4224]{1,0:T(8,128)(2,1)}, bf16[128,4224]{1,0:T(8,128)(2,1)S(1)}, u32[]{:S(2)}, u32[]{:S(2)}) %collective-permute-start.16) | collective-permute-done | bytes 1081376 | tf_op jit(solution)/shard_map/ppermute | solution.py:62
  (338 shorter events, 125.8 us)
Async XLA Ops:
  4.9 29.3 %collective-permute-start.5 = (bf16[128,4224]{1,0:T(8,128)(2,1)}, bf16[128,4224]{1,0:T(8,128)(2,1)}, u32[]{:S(2)}, u32[]{:S(2)}) collective-permute-start(bf16[128,4224]{1,0:T(8,128)(2,1)} %concatenate.121), channel_id=1, source_target_pairs={{0,4},{1,5},{2,6},{3,7},{4,8},{5,9},{6,10},{7,11},{8,12},{9,13},{1... | collective-permute-start | bytes 3244040 | tf_op jit(solution)/shard_map/ppermute | solution.py:62
  7.9 122.7 %collective-permute-start.3 = (bf16[384,2048]{1,0:T(8,128)(2,1)}, bf16[384,2048]{1,0:T(8,128)(2,1)}, u32[]{:S(2)}, u32[]{:S(2)}) collective-permute-start(bf16[384,2048]{1,0:T(8,128)(2,1)} %bitcast.11), channel_id=1, source_target_pairs={{0,1},{1,0},{2,3},{3,2},{4,5},{5,4},{6,7},{7,6},{8,9},{9,8},{10,11... | collective-permute-start | bytes 4718600 | tf_op jit(solution)/shard_map/ppermute | solution.py:62
  7.9 140.3 %collective-permute-start.1 = (bf16[2048,384]{1,0:T(8,128)(2,1)}, bf16[2048,384]{1,0:T(8,128)(2,1)}, u32[]{:S(2)}, u32[]{:S(2)}) collective-permute-start(bf16[2048,384]{1,0:T(8,128)(2,1)} %bitcast.7), channel_id=1, source_target_pairs={{0,1},{1,0},{2,3},{3,2},{4,5},{5,4},{6,7},{7,6},{8,9},{9,8},{10,11... | collective-permute-start | bytes 4718600 | tf_op jit(solution)/shard_map/ppermute | solution.py:62
  8.4 163.7 %collective-permute-start.2 = (bf16[2048,384]{1,0:T(8,128)(2,1)}, bf16[2048,384]{1,0:T(8,128)(2,1)}, u32[]{:S(2)}, u32[]{:S(2)}) collective-permute-start(bf16[2048,384]{1,0:T(8,128)(2,1)} %bitcast.9), channel_id=1, source_target_pairs={{0,1},{1,0},{2,3},{3,2},{4,5},{5,4},{6,7},{7,6},{8,9},{9,8},{10,11... | collective-permute-start | bytes 4718600 | tf_op jit(solution)/shard_map/ppermute | solution.py:62
  8.5 80.5 %copy-start.76 = (s32[4]{0:T(128)}, s32[4]{0:T(128)S(1)}, u32[]{:S(2)}) copy-start(s32[4]{0:T(128)S(1)} %fusion.128) | copy-start | bytes 52
  10.8 78.5 %copy-start.20 = (pred[192,128]{1,0:T(32,128)(4,1)}, pred[192,128]{1,0:T(32,128)(4,1)S(1)}, u32[]{:S(2)}) copy-start(pred[192,128]{1,0:T(32,128)(4,1)S(1)} %get-tuple-element.105) | copy-start | bytes 73732
  10.8 81.2 %copy-start.30 = (pred[192,128]{1,0:T(32,128)(4,1)}, pred[192,128]{1,0:T(32,128)(4,1)S(1)}, u32[]{:S(2)}) copy-start(pred[192,128]{1,0:T(32,128)(4,1)S(1)} %get-tuple-element.102) | copy-start | bytes 73732
  10.8 84.6 %copy-start.26 = (pred[192,128]{1,0:T(32,128)(4,1)}, pred[192,128]{1,0:T(32,128)(4,1)S(1)}, u32[]{:S(2)}) copy-start(pred[192,128]{1,0:T(32,128)(4,1)S(1)} %get-tuple-element.104) | copy-start | bytes 73732
  10.8 89.1 %copy-start.23 = (pred[192,128]{1,0:T(32,128)(4,1)}, pred[192,128]{1,0:T(32,128)(4,1)S(1)}, u32[]{:S(2)}) copy-start(pred[192,128]{1,0:T(32,128)(4,1)S(1)} %get-tuple-element.103) | copy-start | bytes 73732
  34.1 27.1 %collective-permute-start.6 = (bf16[128,4224]{1,0:T(8,128)(2,1)}, bf16[128,4224]{1,0:T(8,128)(2,1)}, u32[]{:S(2)}, u32[]{:S(2)}) collective-permute-start(bf16[128,4224]{1,0:T(8,128)(2,1)} %collective-permute-done.5), channel_id=1, source_target_pairs={{0,4},{1,5},{2,6},{3,7},{4,8},{5,9},{6,10},{7,11},{8,12},{9,13},{1... | collective-permute-start | bytes 3244040 | tf_op jit(solution)/shard_map/ppermute | solution.py:62
  61.3 26.8 %collective-permute-start.7 = (bf16[128,4224]{1,0:T(8,128)(2,1)}, bf16[128,4224]{1,0:T(8,128)(2,1)}, u32[]{:S(2)}, u32[]{:S(2)}) collective-permute-start(bf16[128,4224]{1,0:T(8,128)(2,1)} %collective-permute-done.6), channel_id=1, source_target_pairs={{0,4},{1,5},{2,6},{3,7},{4,8},{5,9},{6,10},{7,11},{8,12},{9,13},{1... | collective-permute-start | bytes 3244040 | tf_op jit(solution)/shard_map/ppermute | solution.py:62
  62.7 26.6 %copy-start.3 = (bf16[128,2048]{1,0:T(8,128)(2,1)S(1)}, bf16[128,2048]{1,0:T(8,128)(2,1)}, u32[]{:S(2)}) copy-start(bf16[128,2048]{1,0:T(8,128)(2,1)} %param.8) | copy-start | bytes 1572868
  90.7 20.7 %collective-permute-start = (bf16[96,4096]{1,0:T(8,128)(2,1)}, bf16[96,4096]{1,0:T(8,128)(2,1)}, u32[]{:S(2)}, u32[]{:S(2)}) collective-permute-start(bf16[96,4096]{1,0:T(8,128)(2,1)} %pad_maximum_fusion.3), channel_id=1, source_target_pairs={{0,2},{1,3},{2,0},{3,1},{4,6},{5,7},{6,4},{7,5},{8,10},{9,11},{10,... | collective-permute-start | bytes 2359304 | tf_op jit(solution)/shard_map/ppermute | solution.py:62
  94.4 33.9 %collective-permute-start.12 = (bf16[96,4096]{1,0:T(8,128)(2,1)}, bf16[96,4096]{1,0:T(8,128)(2,1)}, u32[]{:S(2)}, u32[]{:S(2)}) collective-permute-start(bf16[96,4096]{1,0:T(8,128)(2,1)} %pad_maximum_fusion.15), channel_id=1, source_target_pairs={{0,2},{1,3},{2,0},{3,1},{4,6},{5,7},{6,4},{7,5},{8,10},{9,11},{10,... | collective-permute-start | bytes 2359304 | tf_op jit(solution)/shard_map/ppermute | solution.py:62
  111.4 33.6 %collective-permute-start.10 = (bf16[96,4096]{1,0:T(8,128)(2,1)S(1)}, bf16[96,4096]{1,0:T(8,128)(2,1)S(1)}, u32[]{:S(2)}, u32[]{:S(2)}) collective-permute-start(bf16[96,4096]{1,0:T(8,128)(2,1)S(1)} %pad_maximum_fusion.11), channel_id=1, source_target_pairs={{0,2},{1,3},{2,0},{3,1},{4,6},{5,7},{6,4},{7,5},{8,10},{9,11},{10,... | collective-permute-start | bytes 2359304 | tf_op jit(solution)/shard_map/ppermute | solution.py:62
  128.3 30.2 %collective-permute-start.8 = (bf16[96,4096]{1,0:T(8,128)(2,1)S(1)}, bf16[96,4096]{1,0:T(8,128)(2,1)S(1)}, u32[]{:S(2)}, u32[]{:S(2)}) collective-permute-start(bf16[96,4096]{1,0:T(8,128)(2,1)S(1)} %pad_maximum_fusion.7), channel_id=1, source_target_pairs={{0,2},{1,3},{2,0},{3,1},{4,6},{5,7},{6,4},{7,5},{8,10},{9,11},{10,... | collective-permute-start | bytes 2359304 | tf_op jit(solution)/shard_map/ppermute | solution.py:62
  184.8 45.7 %collective-permute-start.9 = (bf16[96,4096]{1,0:T(8,128)(2,1)S(1)}, bf16[96,4096]{1,0:T(8,128)(2,1)S(1)}, u32[]{:S(2)}, u32[]{:S(2)}) collective-permute-start(bf16[96,4096]{1,0:T(8,128)(2,1)S(1)} %bitcast.211), channel_id=1, source_target_pairs={{0,2},{1,3},{2,0},{3,1},{4,6},{5,7},{6,4},{7,5},{8,10},{9,11},{10,... | collective-permute-start | bytes 2359304 | tf_op jit(solution)/shard_map/ppermute | solution.py:62
  199.5 33.2 %collective-permute-start.11 = (bf16[96,4096]{1,0:T(8,128)(2,1)}, bf16[96,4096]{1,0:T(8,128)(2,1)}, u32[]{:S(2)}, u32[]{:S(2)}) collective-permute-start(bf16[96,4096]{1,0:T(8,128)(2,1)} %bitcast.35), channel_id=1, source_target_pairs={{0,2},{1,3},{2,0},{3,1},{4,6},{5,7},{6,4},{7,5},{8,10},{9,11},{10,... | collective-permute-start | bytes 2359304 | tf_op jit(solution)/shard_map/ppermute | solution.py:62
  206.7 34.7 %copy-start = (bf16[2,48,2048]{2,1,0:T(8,128)(2,1)}, bf16[2,48,2048]{2,1,0:T(8,128)(2,1)S(1)}, u32[]{:S(2)}) copy-start(bf16[2,48,2048]{2,1,0:T(8,128)(2,1)S(1)} %get-tuple-element.50) | copy-start | bytes 1179652
  214.6 22.6 %collective-permute-start.13 = (bf16[96,4096]{1,0:T(8,128)(2,1)}, bf16[96,4096]{1,0:T(8,128)(2,1)}, u32[]{:S(2)}, u32[]{:S(2)}) collective-permute-start(bf16[96,4096]{1,0:T(8,128)(2,1)} %bitcast.45), channel_id=1, source_target_pairs={{0,2},{1,3},{2,0},{3,1},{4,6},{5,7},{6,4},{7,5},{8,10},{9,11},{10,... | collective-permute-start | bytes 2359304 | tf_op jit(solution)/shard_map/ppermute | solution.py:62
  229.3 22.3 %collective-permute-start.4 = (bf16[96,4096]{1,0:T(8,128)(2,1)}, bf16[96,4096]{1,0:T(8,128)(2,1)}, u32[]{:S(2)}, u32[]{:S(2)}) collective-permute-start(bf16[96,4096]{1,0:T(8,128)(2,1)} %bitcast.15), channel_id=1, source_target_pairs={{0,2},{1,3},{2,0},{3,1},{4,6},{5,7},{6,4},{7,5},{8,10},{9,11},{10,... | collective-permute-start | bytes 2359304 | tf_op jit(solution)/shard_map/ppermute | solution.py:62
  241.4 12.2 %copy-start.4 = (bf16[128,2048]{1,0:T(8,128)(2,1)S(1)}, bf16[128,2048]{1,0:T(8,128)(2,1)}, u32[]{:S(2)}) copy-start(bf16[128,2048]{1,0:T(8,128)(2,1)} %param.8) | copy-start | bytes 1572868
  241.4 12.2 %copy-start.21 = (pred[192,128]{1,0:T(32,128)(4,1)S(1)}, pred[192,128]{1,0:T(32,128)(4,1)}, u32[]{:S(2)}) copy-start(pred[192,128]{1,0:T(32,128)(4,1)} %copy-done.20) | copy-start | bytes 73732
  243.1 12.5 %copy-start.77 = (s32[4]{0:T(128)S(1)}, s32[4]{0:T(128)}, u32[]{:S(2)}) copy-start(s32[4]{0:T(128)} %copy-done.76) | copy-start | bytes 52
  263.8 25.4 %collective-permute-start.14 = (bf16[128,4224]{1,0:T(8,128)(2,1)}, bf16[128,4224]{1,0:T(8,128)(2,1)S(1)}, u32[]{:S(2)}, u32[]{:S(2)}) collective-permute-start(bf16[128,4224]{1,0:T(8,128)(2,1)} %concatenate.138), channel_id=1, source_target_pairs={{0,4},{1,5},{2,6},{3,7},{4,8},{5,9},{6,10},{7,11},{8,12},{9,13},{1... | collective-permute-start | bytes 3244040 | tf_op jit(solution)/shard_map/ppermute | solution.py:62
  268.8 66.8 %collective-permute-start.19 = (bf16[384,2048]{1,0:T(8,128)(2,1)}, bf16[384,2048]{1,0:T(8,128)(2,1)}, u32[]{:S(2)}, u32[]{:S(2)}) collective-permute-start(bf16[384,2048]{1,0:T(8,128)(2,1)} %convolution_convert_fusion), channel_id=1, source_target_pairs={{0,1},{1,0},{2,3},{3,2},{4,5},{5,4},{6,7},{7,6},{8,9},{9,8},{10,11... | collective-permute-start | bytes 4718600 | tf_op jit(solution)/shard_map/ppermute | solution.py:62
  300.9 24.5 %collective-permute-start.15 = (bf16[128,4224]{1,0:T(8,128)(2,1)}, bf16[128,4224]{1,0:T(8,128)(2,1)S(1)}, u32[]{:S(2)}, u32[]{:S(2)}) collective-permute-start(bf16[128,4224]{1,0:T(8,128)(2,1)} %concatenate.140), channel_id=1, source_target_pairs={{0,4},{1,5},{2,6},{3,7},{4,8},{5,9},{6,10},{7,11},{8,12},{9,13},{1... | collective-permute-start | bytes 3244040 | tf_op jit(solution)/shard_map/ppermute | solution.py:62
  305.1 34.7 %collective-permute-start.18 = (bf16[2048,384]{1,0:T(8,128)(2,1)}, bf16[2048,384]{1,0:T(8,128)(2,1)}, u32[]{:S(2)}, u32[]{:S(2)}) collective-permute-start(bf16[2048,384]{1,0:T(8,128)(2,1)} %convolution_convert_fusion.1), channel_id=1, source_target_pairs={{0,1},{1,0},{2,3},{3,2},{4,5},{5,4},{6,7},{7,6},{8,9},{9,8},{10,11... | collective-permute-start | bytes 4718600 | tf_op jit(solution)/shard_map/ppermute | solution.py:62
  307.5 19.0 %copy-start.73 = (f32[128,3]{0,1:T(4,128)S(1)}, f32[128,3]{0,1:T(4,128)}, u32[]{:S(2)}) copy-start(f32[128,3]{0,1:T(4,128)} %get-tuple-element.9) | copy-start | bytes 4612
  307.5 36.1 %collective-permute-start.17 = (bf16[2048,384]{1,0:T(8,128)(2,1)}, bf16[2048,384]{1,0:T(8,128)(2,1)}, u32[]{:S(2)}, u32[]{:S(2)}) collective-permute-start(bf16[2048,384]{1,0:T(8,128)(2,1)} %convolution_convert_fusion.2), channel_id=1, source_target_pairs={{0,1},{1,0},{2,3},{3,2},{4,5},{5,4},{6,7},{7,6},{8,9},{9,8},{10,11... | collective-permute-start | bytes 4718600 | tf_op jit(solution)/shard_map/ppermute | solution.py:62
  334.9 23.9 %collective-permute-start.16 = (bf16[128,4224]{1,0:T(8,128)(2,1)}, bf16[128,4224]{1,0:T(8,128)(2,1)S(1)}, u32[]{:S(2)}, u32[]{:S(2)}) collective-permute-start(bf16[128,4224]{1,0:T(8,128)(2,1)} %concatenate.142), channel_id=1, source_target_pairs={{0,4},{1,5},{2,6},{3,7},{4,8},{5,9},{6,10},{7,11},{8,12},{9,13},{1... | collective-permute-start | bytes 3244040 | tf_op jit(solution)/shard_map/ppermute | solution.py:62
  343.6 16.4 %copy-start.72 = (f32[128,3]{0,1:T(4,128)S(1)}, f32[128,3]{0,1:T(4,128)}, u32[]{:S(2)}) copy-start(f32[128,3]{0,1:T(4,128)} %get-tuple-element.6) | copy-start | bytes 4612
  (66 other events, 209.9 us)

commit v2 on v1

v2 whole, which is shorter than its diff:
```python
import functools

import jax
import jax.numpy as jnp
from jax import lax
from jax.experimental import pallas as pl
from jax.experimental.pallas import tpu as pltpu
from jax.sharding import PartitionSpec as P

F32 = jnp.float32
BF16 = jnp.bfloat16
LANES = 128
TILE = 512
VMEM = pl.BlockSpec(memory_space=pltpu.VMEM)
SMEM = pl.BlockSpec(memory_space=pltpu.SMEM)


def rounded(value):
    return value.astype(BF16).astype(F32)


def nt(a, b):
    return lax.dot_general(a, b, (((1,), (1,)), ((), ())), preferred_element_type=F32)


def nn(a, b):
    return jnp.dot(a, b, preferred_element_type=F32)


def expert_ids(place, plane):
    return [place[0] * plane + jnp.bitwise_xor(place[1], e) for e in range(plane)]


def slots_of(place, ids, parts, plane, depth, route_count):
    tokens = ids.shape[1]
    rows = lax.broadcasted_iota(jnp.int32, (tokens, tokens), 0)
    cols = lax.broadcasted_iota(jnp.int32, (tokens, tokens), 1)
    before = jnp.where(rows < cols, 1.0, 0.0).astype(BF16)
    route = [ids[k : k + 1] for k in range(route_count)]
    probs = [
        parts[k : k + 1]
        + parts[route_count + k : route_count + k + 1]
        + parts[2 * route_count + k : 2 * route_count + k + 1]
        for k in range(route_count)
    ]
    slot = lax.broadcasted_iota(jnp.int32, (depth, tokens), 0)
    named, weight = [], []
    for eid in expert_ids(place, plane):
        hit = [jnp.where(r == eid, 1.0, 0.0) for r in route]
        named.append(sum(hit))
        weight.append(sum(h * p for h, p in zip(hit, probs)))
    pad = [jnp.zeros((8 - plane % 8, tokens), F32)] if plane % 8 else []
    rank = nn(jnp.concatenate(named + pad, axis=0).astype(BF16), before)
    picks, gates = [], []
    for e in range(plane):
        wanted = jnp.broadcast_to(rank[e : e + 1], (depth, tokens)).astype(jnp.int32)
        present = jnp.broadcast_to(named[e], (depth, tokens))
        pick = jnp.where(wanted == slot, present, 0.0)
        picks.append(pick)
        gates.append(jnp.sum(pick * weight[e], axis=1, keepdims=True))
    return jnp.concatenate(picks, axis=0), jnp.concatenate(gates, axis=0)


def select_kernel(plane, depth, route_count, place, ids, block, *outs):
    width = outs[0].shape[1] // 2
    parts = block[0:16, 2 * width :].astype(F32)
    pick, gate = slots_of(place, ids[...], parts, plane, depth, route_count)
    chooser = pick.astype(BF16)
    for start in range(0, 2 * width, TILE):
        cols = pl.ds(start, TILE)
        found = nn(chooser, block[:, cols])
        if start >= width:
            found = found * gate
        found = found.astype(BF16)
        for e in range(plane):
            outs[e][:, cols] = found[e * depth : (e + 1) * depth]


def expert_kernel(plane, *refs):
    rows = refs[:plane]
    gate_w, up_w, down_w = refs[plane : plane + 3]
    outs = refs[plane + 3 : 2 * plane + 3]
    hidden_out, ggp_out, gup_out = refs[2 * plane + 3 :]
    width = gate_w.shape[0]
    depth = rows[0].shape[0]
    row_x = jnp.concatenate([r[:, :width] for r in rows], axis=0)
    row_c = jnp.concatenate([r[:, width:] for r in rows], axis=0)
    gate_pre = nn(row_x, gate_w[...])
    up_pre = nn(row_x, up_w[...])
    gate_sig = 1.0 / (1.0 + jnp.exp(-gate_pre))
    gate_act = gate_pre * gate_sig
    hidden = (gate_act * up_pre).astype(BF16)
    hidden_out[...] = hidden
    d_hidden = nt(row_c, down_w[...])
    ggp = (d_hidden * up_pre * gate_sig * (1.0 + gate_pre * (1.0 - gate_sig))).astype(BF16)
    gup = (d_hidden * gate_act).astype(BF16)
    ggp_out[...] = ggp
    gup_out[...] = gup
    for start in range(0, width, TILE):
        cols = pl.ds(start, TILE)
        y = nn(hidden, down_w[:, cols]).astype(BF16)
        dx = (nt(ggp, gate_w[cols, :]) + nt(gup, up_w[cols, :])).astype(BF16)
        for e in range(plane):
            part = slice(e * depth, (e + 1) * depth)
            outs[e][:, cols] = y[part]
            outs[e][:, pl.ds(width + start, TILE)] = dx[part]


def combine_kernel(plane, depth, route_count, has_running, is_last, place, ids, block, *refs):
    near = refs[:plane]
    refs = refs[plane:]
    running = None
    if has_running:
        running, refs = refs[0], refs[1:]
    width = near[0].shape[1] // 2
    tokens = ids.shape[1]
    ids_now = ids[...]
    parts = block[0:16, 2 * width :].astype(F32)
    pick, gate = slots_of(place, ids_now, parts, plane, depth, route_count)
    weighted = pick * gate
    weight_high = rounded(weighted)
    high = jnp.transpose(weight_high).astype(BF16)
    low = jnp.transpose(weighted - weight_high).astype(BF16)
    spread = jnp.transpose(pick).astype(BF16)
    dots = jnp.zeros((plane * depth, tokens), F32)
    for start in range(0, width, TILE):
        cols = pl.ds(start, TILE)
        cols_dx = pl.ds(width + start, TILE)
        y = jnp.concatenate([n[:, cols] for n in near], axis=0)
        dx = jnp.concatenate([n[:, cols_dx] for n in near], axis=0)
        part_y = nn(high, y) + nn(low, y)
        part_dx = nn(spread, dx)
        dots = dots + nt(y, block[:, cols_dx])
        if has_running:
            part_y = part_y + running[:, cols].astype(F32)
            part_dx = part_dx + running[:, cols_dx].astype(F32)
        if is_last:
            refs[0][:, cols] = part_y.astype(BF16)
            refs[1][:, cols] = part_dx.astype(BF16)
        else:
            refs[0][:, cols] = part_y.astype(BF16)
            refs[0][:, cols_dx] = part_dx.astype(BF16)
    dots = pick * dots
    found = [jnp.sum(dots[e * depth : (e + 1) * depth], axis=0, keepdims=True) for e in range(plane)]
    gates = []
    for k in range(route_count):
        mine = ids_now[k : k + 1]
        total = jnp.zeros((1, tokens), F32)
        for eid, value in zip(expert_ids(place, plane), found):
            total = total + jnp.where(mine == eid, value, 0.0)
        gates.append(total)
    if has_running:
        old = running[0:16, 2 * width :].astype(F32)
        for k in range(route_count):
            for piece in range(3):
                at = piece * route_count + k
                gates[k] = gates[k] + old[at : at + 1]
    if is_last:
        pad = jnp.zeros((8 - route_count, tokens), F32)
        refs[2][...] = jnp.concatenate(gates + [pad], axis=0)
    else:
        high = [rounded(g) for g in gates]
        middle = [rounded(g - h) for g, h in zip(gates, high)]
        low = [g - h - m for g, h, m in zip(gates, high, middle)]
        pad = jnp.zeros((tokens - 3 * route_count, tokens), F32)
        refs[0][:, 2 * width :] = jnp.concatenate(high + middle + low + [pad], axis=0).astype(BF16)


def grads_kernel(ring, plane, *refs):
    rows = refs[: ring * plane]
    small = refs[ring * plane : ring * plane + 3 * ring]
    gate_out, up_out, down_out = refs[ring * plane + 3 * ring :]
    width = gate_out.shape[0]
    hidden = jnp.transpose(jnp.concatenate([small[3 * s][...] for s in range(ring)], axis=0))
    ggp = jnp.concatenate([small[3 * s + 1][...] for s in range(ring)], axis=0)
    gup = jnp.concatenate([small[3 * s + 2][...] for s in range(ring)], axis=0)
    step = TILE // 2
    for start in range(0, width, step):
        cols = pl.ds(start, step)
        x = jnp.transpose(jnp.concatenate([r[:, cols] for r in rows], axis=0))
        gate_out[cols, :] = nn(x, ggp).astype(BF16)
        up_out[cols, :] = nn(x, gup).astype(BF16)
        c = jnp.concatenate([r[:, pl.ds(width + start, step)] for r in rows], axis=0)
        down_out[:, cols] = nn(hidden, c).astype(BF16)


def call(body, outs, flops, inputs, name):
    total = sum(x.size * x.dtype.itemsize for x in inputs)
    total += sum(o.size * o.dtype.itemsize for o in outs)
    specs = [SMEM if x.dtype == jnp.int32 and x.ndim == 1 else VMEM for x in inputs]
    return pl.pallas_call(
        body,
        out_shape=tuple(outs),
        in_specs=specs,
        out_specs=tuple(VMEM for _ in outs),
        cost_estimate=pl.CostEstimate(flops=flops, bytes_accessed=total, transcendentals=0),
        compiler_params=pltpu.CompilerParams(vmem_limit_bytes=40 * 1024 * 1024),
        name=name,
    )(*inputs)


def local(tokens, cotangent, route_ids, gate_probs, w_gate, w_up, w_down):
    owner_count = lax.axis_size("owner")
    me = lax.axis_index("owner")
    token_rows, width = tokens.shape
    route_count = route_ids.shape[1]
    hidden_width = w_gate.shape[2]
    depth = 2 * token_rows * route_count // owner_count
    depth = (depth + 15) // 16 * 16
    plane = 4 if owner_count % 4 == 0 else 2
    ring = owner_count // plane
    column = me % plane
    my_z = me // plane
    place = jnp.stack([my_z, column]).astype(jnp.int32)

    ring_up = [(i, (i + plane) % owner_count) for i in range(owner_count)]
    swaps = [[(i, i ^ e) for i in range(owner_count)] for e in range(plane)]

    def hop(value, pairs, scope):
        with jax.named_scope(scope):
            return lax.ppermute(value, "owner", pairs)

    id_table = route_ids.reshape(ring, plane, token_rows, route_count)
    line_ids = lax.dynamic_index_in_dim(id_table, column, 1, keepdims=False)
    line_ids = jnp.swapaxes(line_ids, 1, 2)
    line_ids = jnp.pad(line_ids, ((0, 0), (0, 8 - route_count), (0, 0)), constant_values=-1)
    step_ids = [
        lax.dynamic_index_in_dim(line_ids, (my_z - s) % ring, 0, keepdims=False) for s in range(ring)
    ]

    probs = gate_probs.T
    high = lax.reduce_precision(probs, 8, 7)
    middle = lax.reduce_precision(probs - high, 8, 7)
    low = probs - high - middle
    tail = jnp.concatenate([high, middle, low], axis=0).astype(BF16)
    tail = jnp.pad(tail, ((0, token_rows - 3 * route_count), (0, 0)))
    block = jnp.concatenate([tokens, cotangent, tail], axis=1)
    packed = 2 * width + token_rows

    blocks = [block]
    for s in range(ring - 1):
        blocks.append(hop(blocks[-1], ring_up, f"zin{s + 1}"))

    slot_shape = jax.ShapeDtypeStruct((depth, 2 * width), BF16)
    small_shape = jax.ShapeDtypeStruct((plane * depth, hidden_width), BF16)
    weights = [w_gate[0], w_up[0], w_down[0]]
    rows = plane * depth

    def exchange(values, scope):
        return [values[0]] + [hop(values[e], swaps[e], f"{scope}_{e}") for e in range(1, plane)]

    got, result = [], []
    for s in range(ring):
        picked = call(
            functools.partial(select_kernel, plane, depth, route_count),
            [slot_shape] * plane,
            2 * rows * token_rows * 2 * width,
            [place, step_ids[s], blocks[s]],
            f"select{s}",
        )
        got.append(exchange(picked, f"yin{s}"))
    for s in range(ring):
        result.append(
            call(
                functools.partial(expert_kernel, plane),
                [slot_shape] * plane + [small_shape] * 3,
                12 * rows * width * hidden_width,
                got[s] + weights,
                f"expert{s}",
            )
        )

    running = None
    for s in list(range(1, ring)) + [0]:
        near = exchange(result[s][:plane], f"yout{s}")
        last = s == 0
        if last:
            row_shape = jax.ShapeDtypeStruct((token_rows, width), BF16)
            outs = [row_shape, row_shape, jax.ShapeDtypeStruct((8, token_rows), F32)]
        else:
            outs = [jax.ShapeDtypeStruct((token_rows, packed), BF16)]
        inputs = [place, step_ids[s], blocks[s]] + near
        if running is not None:
            inputs.append(running)
        done = call(
            functools.partial(
                combine_kernel, plane, depth, route_count, running is not None, last
            ),
            outs,
            8 * rows * token_rows * width,
            inputs,
            f"combine{s}",
        )
        if not last:
            running = hop(done[0], ring_up, f"zout{s}")
    expert_out, grad_tokens, gates = done

    small = [r for s in range(ring) for r in result[s][plane:]]
    grads = call(
        functools.partial(grads_kernel, ring, plane),
        [
            jax.ShapeDtypeStruct((width, hidden_width), BF16),
            jax.ShapeDtypeStruct((width, hidden_width), BF16),
            jax.ShapeDtypeStruct((hidden_width, width), BF16),
        ],
        6 * ring * rows * width * hidden_width,
        [g for s in range(ring) for g in got[s]] + small,
        "grads",
    )
    return (
        expert_out,
        grad_tokens,
        gates[:route_count].T,
        grads[0][None],
        grads[1][None],
        grads[2][None],
    )


def solution(mesh):
    rows = P(("group", "owner"), None)
    stacked = P(("group", "owner"), None, None)
    weights = P("owner", None, None)
    return jax.shard_map(
        local,
        mesh=mesh,
        in_specs=(rows, rows, P("group", None), rows, weights, weights, weights),
        out_specs=(rows, rows, rows, stacked, stacked, stacked),
        check_vma=False,
    )
```

time: 369 us -> 224 us (0.61)
  the two profiles are of different devices: /device:TPU:0 before, /device:TPU:13 now
where the time goes in v2:
time: 224 us; the launch traced here: 220 us
  waiting for transfers between devices  155 us (69%)
  Pallas kernels  31.1 us (14%)
  starting transfers between devices  26.3 us (12%)
  local copies, waits for them, and re-layouts  4.87 us (2%)
    ppermute x30, waiting for transfers between devices, hop(): return lax.ppermute(value, 'owner', pairs)  155 us
    pallas_call x13, Pallas kernels, call(): pl.pallas_call(body, out_shape=tuple(outs), in_specs=specs, out_specs=tup...  31.1 us
    ppermute x30, starting transfers between devices, hop(): return lax.ppermute(value, 'owner', pairs)  26.3 us
  transfers between devices with their start and end apart: 30, of which 18 were waited for; matrix products, arithmetic and copies ran while one was open for 0% of the time, Pallas kernels for 12%

profile of v2, /device:TPU:13, one launch (start us, length us, event | category | flops | bytes accessed | tf_op | source)
XLA Modules:
  0.0 220.4 jit_solution(3810454780922577380)
XLA Ops:
  4.2 23.3 %collective-permute-done.6.block = bf16[128,4224]{1,0:T(8,128)(2,1)S(1)} collective-permute-done((bf16[128,4224]{1,0:T(8,128)(2,1)S(1)}, bf16[128,4224]{1,0:T(8,128)(2,1)S(1)}, u32[]{:S(2)}, u32[]{:S(2)}) %collective-permute-start.6) | collective-permute-done | bytes 1081376 | tf_op jit(solution)/shard_map/zin1/ppermute | solution.py:221
  28.7 1.6 collective-permute-start.21
  33.3 7.6 %collective-permute-done.22.refs_2_.refs_6_ = bf16[48,4096]{1,0:T(8,128)(2,1)S(1)} collective-permute-done((bf16[48,4096]{1,0:T(8,128)(2,1)S(1)}, bf16[48,4096]{1,0:T(8,128)(2,1)S(1)}, u32[]{:S(2)}, u32[]{:S(2)}) %collective-permute-start.22) | collective-permute-done | bytes 393248 | tf_op jit(solution)/shard_map/yin1_2/ppermute | solution.py:221
  40.9 9.0 %collective-permute-done.23.refs_3_.refs_7_ = bf16[48,4096]{1,0:T(8,128)(2,1)S(1)} collective-permute-done((bf16[48,4096]{1,0:T(8,128)(2,1)S(1)}, bf16[48,4096]{1,0:T(8,128)(2,1)S(1)}, u32[]{:S(2)}, u32[]{:S(2)}) %collective-permute-start.23) | collective-permute-done | bytes 393248 | tf_op jit(solution)/shard_map/yin1_3/ppermute | solution.py:221
  54.1 3.0 %expert1.1 = (bf16[48,4096]{1,0:T(8,128)(2,1)S(1)}, bf16[48,4096]{1,0:T(8,128)(2,1)S(1)}, bf16[48,4096]{1,0:T(8,128)(2,1)S(1)}, bf16[48,4096]{1,0:T(8,128)(2,1)S...) custom-call(bf16[48,4096]{1,0:T(8,128)(2,1)S(1)} %get-tuple-element.80.refs_0_.refs_4_, ...), custom_call_target="tpu_custom_call" | custom-call | flops 1811939328 | bytes 8306688 | tf_op jit(solution)/shard_map/expert1/pallas_call | solution.py:191
  57.4 1.8 collective-permute-start.26
  59.2 8.2 %collective-permute-done.25.refs_2_ = bf16[48,4096]{1,0:T(8,128)(2,1)S(1)} collective-permute-done((bf16[48,4096]{1,0:T(8,128)(2,1)S(1)}, bf16[48,4096]{1,0:T(8,128)(2,1)S(1)}, u32[]{:S(2)}, u32[]{:S(2)}) %collective-permute-start.25) | collective-permute-done | bytes 393248 | tf_op jit(solution)/shard_map/yout1_2/ppermute | solution.py:221
  67.4 9.0 %collective-permute-done.26.refs_3_ = bf16[48,4096]{1,0:T(8,128)(2,1)S(1)} collective-permute-done((bf16[48,4096]{1,0:T(8,128)(2,1)S(1)}, bf16[48,4096]{1,0:T(8,128)(2,1)S(1)}, u32[]{:S(2)}, u32[]{:S(2)}) %collective-permute-start.26) | collective-permute-done | bytes 393248 | tf_op jit(solution)/shard_map/yout1_3/ppermute | solution.py:221
  76.4 1.7 combine1.1
  81.1 1.8 collective-permute-start.17
  84.2 6.9 %collective-permute-done.16.refs_2_.refs_10_ = bf16[48,4096]{1,0:T(8,128)(2,1)S(1)} collective-permute-done((bf16[48,4096]{1,0:T(8,128)(2,1)S(1)}, bf16[48,4096]{1,0:T(8,128)(2,1)S(1)}, u32[]{:S(2)}, u32[]{:S(2)}) %collective-permute-start.16) | collective-permute-done | bytes 393248 | tf_op jit(solution)/shard_map/yin2_2/ppermute | solution.py:221
  91.1 9.3 %collective-permute-done.17.refs_3_.refs_11_ = bf16[48,4096]{1,0:T(8,128)(2,1)S(1)} collective-permute-done((bf16[48,4096]{1,0:T(8,128)(2,1)S(1)}, bf16[48,4096]{1,0:T(8,128)(2,1)S(1)}, u32[]{:S(2)}, u32[]{:S(2)}) %collective-permute-start.17) | collective-permute-done | bytes 393248 | tf_op jit(solution)/shard_map/yin2_3/ppermute | solution.py:221
  100.4 3.0 %expert2.1 = (bf16[48,4096]{1,0:T(8,128)(2,1)S(1)}, bf16[48,4096]{1,0:T(8,128)(2,1)S(1)}, bf16[48,4096]{1,0:T(8,128)(2,1)S(1)}, bf16[48,4096]{1,0:T(8,128)(2,1)S...) custom-call(bf16[48,4096]{1,0:T(8,128)(2,1)S(1)} %get-tuple-element.72.refs_0_.refs_8_, ...), custom_call_target="tpu_custom_call" | custom-call | flops 1811939328 | bytes 8306688 | tf_op jit(solution)/shard_map/expert2/pallas_call | solution.py:191
  103.8 1.8 collective-permute-start.20
  105.6 8.2 %collective-permute-done.19.refs_2_ = bf16[48,4096]{1,0:T(8,128)(2,1)S(1)} collective-permute-done((bf16[48,4096]{1,0:T(8,128)(2,1)S(1)}, bf16[48,4096]{1,0:T(8,128)(2,1)S(1)}, u32[]{:S(2)}, u32[]{:S(2)}) %collective-permute-start.19) | collective-permute-done | bytes 393248 | tf_op jit(solution)/shard_map/yout2_2/ppermute | solution.py:221
  113.8 9.3 %collective-permute-done.20.refs_3_ = bf16[48,4096]{1,0:T(8,128)(2,1)S(1)} collective-permute-done((bf16[48,4096]{1,0:T(8,128)(2,1)S(1)}, bf16[48,4096]{1,0:T(8,128)(2,1)S(1)}, u32[]{:S(2)}, u32[]{:S(2)}) %collective-permute-start.20) | collective-permute-done | bytes 393248 | tf_op jit(solution)/shard_map/yout2_3/ppermute | solution.py:221
  123.1 1.7 combine2.1
  131.3 8.7 %collective-permute-done.10.refs_2_.refs_14_ = bf16[48,4096]{1,0:T(8,128)(2,1)S(1)} collective-permute-done((bf16[48,4096]{1,0:T(8,128)(2,1)S(1)}, bf16[48,4096]{1,0:T(8,128)(2,1)S(1)}, u32[]{:S(2)}, u32[]{:S(2)}) %collective-permute-start.10) | collective-permute-done | bytes 393248 | tf_op jit(solution)/shard_map/yin3_2/ppermute | solution.py:221
  140.0 9.1 %collective-permute-done.11.refs_3_.refs_15_ = bf16[48,4096]{1,0:T(8,128)(2,1)S(1)} collective-permute-done((bf16[48,4096]{1,0:T(8,128)(2,1)S(1)}, bf16[48,4096]{1,0:T(8,128)(2,1)S(1)}, u32[]{:S(2)}, u32[]{:S(2)}) %collective-permute-start.11) | collective-permute-done | bytes 393248 | tf_op jit(solution)/shard_map/yin3_3/ppermute | solution.py:221
  149.0 3.0 %expert3.1 = (bf16[48,4096]{1,0:T(8,128)(2,1)S(1)}, bf16[48,4096]{1,0:T(8,128)(2,1)S(1)}, bf16[48,4096]{1,0:T(8,128)(2,1)S(1)}, bf16[48,4096]{1,0:T(8,128)(2,1)S...) custom-call(bf16[48,4096]{1,0:T(8,128)(2,1)S(1)} %get-tuple-element.64.refs_0_.refs_12, ...), custom_call_target="tpu_custom_call" | custom-call | flops 1811939328 | bytes 8306688 | tf_op jit(solution)/shard_map/expert3/pallas_call | solution.py:191
  152.4 1.8 collective-permute-start.14
  154.2 8.2 %collective-permute-done.13.refs_2_ = bf16[48,4096]{1,0:T(8,128)(2,1)S(1)} collective-permute-done((bf16[48,4096]{1,0:T(8,128)(2,1)S(1)}, bf16[48,4096]{1,0:T(8,128)(2,1)S(1)}, u32[]{:S(2)}, u32[]{:S(2)}) %collective-permute-start.13) | collective-permute-done | bytes 393248 | tf_op jit(solution)/shard_map/yout3_2/ppermute | solution.py:221
  162.4 9.0 %collective-permute-done.14.refs_3_ = bf16[48,4096]{1,0:T(8,128)(2,1)S(1)} collective-permute-done((bf16[48,4096]{1,0:T(8,128)(2,1)S(1)}, bf16[48,4096]{1,0:T(8,128)(2,1)S(1)}, u32[]{:S(2)}, u32[]{:S(2)}) %collective-permute-start.14) | collective-permute-done | bytes 393248 | tf_op jit(solution)/shard_map/yout3_3/ppermute | solution.py:221
  171.4 1.7 combine3.1
  175.5 1.8 collective-permute-start.2
  177.4 8.2 %collective-permute-done.1.refs_2_ = bf16[48,4096]{1,0:T(8,128)(2,1)S(1)} collective-permute-done((bf16[48,4096]{1,0:T(8,128)(2,1)S(1)}, bf16[48,4096]{1,0:T(8,128)(2,1)S(1)}, u32[]{:S(2)}, u32[]{:S(2)}) %collective-permute-start.1) | collective-permute-done | bytes 393248 | tf_op jit(solution)/shard_map/yin0_2/ppermute | solution.py:221
  185.6 9.3 %collective-permute-done.2.refs_3_ = bf16[48,4096]{1,0:T(8,128)(2,1)S(1)} collective-permute-done((bf16[48,4096]{1,0:T(8,128)(2,1)S(1)}, bf16[48,4096]{1,0:T(8,128)(2,1)S(1)}, u32[]{:S(2)}, u32[]{:S(2)}) %collective-permute-start.2) | collective-permute-done | bytes 393248 | tf_op jit(solution)/shard_map/yin0_3/ppermute | solution.py:221
  194.9 3.0 %expert0.1 = (bf16[48,4096]{1,0:T(8,128)(2,1)S(1)}, bf16[48,4096]{1,0:T(8,128)(2,1)S(1)}, bf16[48,4096]{1,0:T(8,128)(2,1)S(1)}, bf16[48,4096]{1,0:T(8,128)(2,1)S...) custom-call(bf16[48,4096]{1,0:T(8,128)(2,1)S(1)} %get-tuple-element.56.refs_0_, ...), custom_call_target="tpu_custom_call" | custom-call | flops 1811939328 | bytes 8306688 | tf_op jit(solution)/shard_map/expert0/pallas_call | solution.py:191
  198.2 1.8 collective-permute-start.5
  200.0 6.7 %grads.1 = (bf16[2048,384]{1,0:T(8,128)(2,1)}, bf16[2048,384]{1,0:T(8,128)(2,1)}, bf16[384,2048]{1,0:T(8,128)(2,1)}) custom-call(bf16[48,4096]{1,0:T(8,128)(2,1)S(1)} %get-tuple-element.56.refs_0_, bf16[48,4096]{1,0:T(8,128)(2,1)S(1)} %collective-permute-done.refs_1_, bf16[48,4096]{1,0:T(8,128)(2,1)S(1)} %collective-permute-done.1.refs_2_, ...), custom_call_target="tpu_custom_call" | custom-call | flops 3623878656 | bytes 12779520 | tf_op jit(solution)/shard_map/grads/pallas_call | solution.py:191
  208.2 9.0 %collective-permute-done.5.refs_3_ = bf16[48,4096]{1,0:T(8,128)(2,1)S(1)} collective-permute-done((bf16[48,4096]{1,0:T(8,128)(2,1)S(1)}, bf16[48,4096]{1,0:T(8,128)(2,1)S(1)}, u32[]{:S(2)}, u32[]{:S(2)}) %collective-permute-start.5) | collective-permute-done | bytes 393248 | tf_op jit(solution)/shard_map/yout0_3/ppermute | solution.py:221
  217.3 2.6 %combine0.1 = (bf16[128,2048]{1,0:T(8,128)(2,1)}, bf16[128,2048]{1,0:T(8,128)(2,1)}, f32[8,128]{1,0:T(8,128)S(1)}) custom-call(s32[2]{0:T(128)S(1)} %pad_add_fusion.place, s32[8,128]{1,0:T(8,128)S(1)} %get-tuple-element.109.ids, bf16[128,4224]{1,0:T(8,128)(2,1)S(1)} %pad_maximum_fusion.block, bf16[48,4096]{1,0:T(8,128)(2,1)S(1)} %get-tuple-element.60.refs_0_, ...), custom_call_target="tpu_custom_call" | custom-call | flops 402653184 | bytes 4792328 | tf_op jit(solution)/shard_map/combine0/pallas_call | solution.py:191
  (62 shorter events, 28.5 us)
Async XLA Ops:
  2.6 24.8 %collective-permute-start.6 = (bf16[128,4224]{1,0:T(8,128)(2,1)S(1)}, bf16[128,4224]{1,0:T(8,128)(2,1)S(1)}, u32[]{:S(2)}, u32[]{:S(2)}) collective-permute-start(bf16[128,4224]{1,0:T(8,128)(2,1)S(1)} %pad_maximum_fusion.block), channel_id=1, source_target_pairs={{0,4},{1,5},{2,6},{3,7},{4,8},{5,9},{6,10},{7,11},{8,12},{9,13},{1... | collective-permute-start | bytes 3244040 | tf_op jit(solution)/shard_map/zin1/ppermute | solution.py:221
  28.7 4.6 %collective-permute-start.21 = (bf16[48,4096]{1,0:T(8,128)(2,1)S(1)}, bf16[48,4096]{1,0:T(8,128)(2,1)S(1)}, u32[]{:S(2)}, u32[]{:S(2)}) collective-permute-start(bf16[48,4096]{1,0:T(8,128)(2,1)S(1)} %get-tuple-element.81), channel_id=1, source_target_pairs={{0,1},{1,0},{2,3},{3,2},{4,5},{5,4},{6,7},{7,6},{8,9},{9,8},{10,11... | collective-permute-start | bytes 1179656 | tf_op jit(solution)/shard_map/yin1_1/ppermute | solution.py:221
  30.3 10.6 %collective-permute-start.22 = (bf16[48,4096]{1,0:T(8,128)(2,1)S(1)}, bf16[48,4096]{1,0:T(8,128)(2,1)S(1)}, u32[]{:S(2)}, u32[]{:S(2)}) collective-permute-start(bf16[48,4096]{1,0:T(8,128)(2,1)S(1)} %get-tuple-element.82), channel_id=1, source_target_pairs={{0,2},{1,3},{2,0},{3,1},{4,6},{5,7},{6,4},{7,5},{8,10},{9,11},{10,... | collective-permute-start | bytes 1179656 | tf_op jit(solution)/shard_map/yin1_2/ppermute | solution.py:221
  30.5 19.3 %collective-permute-start.23 = (bf16[48,4096]{1,0:T(8,128)(2,1)S(1)}, bf16[48,4096]{1,0:T(8,128)(2,1)S(1)}, u32[]{:S(2)}, u32[]{:S(2)}) collective-permute-start(bf16[48,4096]{1,0:T(8,128)(2,1)S(1)} %get-tuple-element.83), channel_id=1, source_target_pairs={{0,3},{1,2},{2,1},{3,0},{4,7},{5,6},{6,5},{7,4},{8,11},{9,10},{10,... | collective-permute-start | bytes 1179656 | tf_op jit(solution)/shard_map/yin1_3/ppermute | solution.py:221
  32.0 47.5 %collective-permute-start.7 = (bf16[128,4224]{1,0:T(8,128)(2,1)S(1)}, bf16[128,4224]{1,0:T(8,128)(2,1)S(1)}, u32[]{:S(2)}, u32[]{:S(2)}) collective-permute-start(bf16[128,4224]{1,0:T(8,128)(2,1)S(1)} %collective-permute-done.6.block), channel_id=1, source_target_pairs={{0,4},{1,5},{2,6},{3,7},{4,8},{5,9},{6,10},{7,11},{8,12},{9,13},{1... | collective-permute-start | bytes 3244040 | tf_op jit(solution)/shard_map/zin2/ppermute | solution.py:221
  57.0 2.2 %collective-permute-start.24 = (bf16[48,4096]{1,0:T(8,128)(2,1)S(1)}, bf16[48,4096]{1,0:T(8,128)(2,1)S(1)}, u32[]{:S(2)}, u32[]{:S(2)}) collective-permute-start(bf16[48,4096]{1,0:T(8,128)(2,1)S(1)} %get-tuple-element.85), channel_id=1, source_target_pairs={{0,1},{1,0},{2,3},{3,2},{4,5},{5,4},{6,7},{7,6},{8,9},{9,8},{10,11... | collective-permute-start | bytes 1179656 | tf_op jit(solution)/shard_map/yout1_1/ppermute | solution.py:221
  57.1 10.3 %collective-permute-start.25 = (bf16[48,4096]{1,0:T(8,128)(2,1)S(1)}, bf16[48,4096]{1,0:T(8,128)(2,1)S(1)}, u32[]{:S(2)}, u32[]{:S(2)}) collective-permute-start(bf16[48,4096]{1,0:T(8,128)(2,1)S(1)} %get-tuple-element.86), channel_id=1, source_target_pairs={{0,2},{1,3},{2,0},{3,1},{4,6},{5,7},{6,4},{7,5},{8,10},{9,11},{10,... | collective-permute-start | bytes 1179656 | tf_op jit(solution)/shard_map/yout1_2/ppermute | solution.py:221
  57.4 19.0 %collective-permute-start.26 = (bf16[48,4096]{1,0:T(8,128)(2,1)S(1)}, bf16[48,4096]{1,0:T(8,128)(2,1)S(1)}, u32[]{:S(2)}, u32[]{:S(2)}) collective-permute-start(bf16[48,4096]{1,0:T(8,128)(2,1)S(1)} %get-tuple-element.87), channel_id=1, source_target_pairs={{0,3},{1,2},{2,1},{3,0},{4,7},{5,6},{6,5},{7,4},{8,11},{9,10},{10,... | collective-permute-start | bytes 1179656 | tf_op jit(solution)/shard_map/yout1_3/ppermute | solution.py:221
  76.4 24.0 %copy-start.1 = (bf16[1,2048,384]{2,1,0:T(8,128)(2,1)S(1)}, bf16[1,2048,384]{2,1,0:T(8,128)(2,1)}, u32[]{:S(2)}) copy-start(bf16[1,2048,384]{2,1,0:T(8,128)(2,1)} %param.11) | copy-start | bytes 4718596
  76.4 24.0 %copy-start.3 = (bf16[1,2048,384]{2,1,0:T(8,128)(2,1)S(1)}, bf16[1,2048,384]{2,1,0:T(8,128)(2,1)}, u32[]{:S(2)}) copy-start(bf16[1,2048,384]{2,1,0:T(8,128)(2,1)} %param.12) | copy-start | bytes 4718596
  78.1 45.0 %collective-permute-start.27 = (bf16[128,4224]{1,0:T(8,128)(2,1)S(1)}, bf16[128,4224]{1,0:T(8,128)(2,1)S(1)}, u32[]{:S(2)}, u32[]{:S(2)}) collective-permute-start(bf16[128,4224]{1,0:T(8,128)(2,1)S(1)} %combine1.1), channel_id=1, source_target_pairs={{0,4},{1,5},{2,6},{3,7},{4,8},{5,9},{6,10},{7,11},{8,12},{9,13},{1... | collective-permute-start | bytes 3244040 | tf_op jit(solution)/shard_map/zout1/ppermute | solution.py:221
  80.7 3.5 %collective-permute-start.15 = (bf16[48,4096]{1,0:T(8,128)(2,1)S(1)}, bf16[48,4096]{1,0:T(8,128)(2,1)S(1)}, u32[]{:S(2)}, u32[]{:S(2)}) collective-permute-start(bf16[48,4096]{1,0:T(8,128)(2,1)S(1)} %get-tuple-element.73), channel_id=1, source_target_pairs={{0,1},{1,0},{2,3},{3,2},{4,5},{5,4},{6,7},{7,6},{8,9},{9,8},{10,11... | collective-permute-start | bytes 1179656 | tf_op jit(solution)/shard_map/yin2_1/ppermute | solution.py:221
  80.9 10.2 %collective-permute-start.16 = (bf16[48,4096]{1,0:T(8,128)(2,1)S(1)}, bf16[48,4096]{1,0:T(8,128)(2,1)S(1)}, u32[]{:S(2)}, u32[]{:S(2)}) collective-permute-start(bf16[48,4096]{1,0:T(8,128)(2,1)S(1)} %get-tuple-element.74), channel_id=1, source_target_pairs={{0,2},{1,3},{2,0},{3,1},{4,6},{5,7},{6,4},{7,5},{8,10},{9,11},{10,... | collective-permute-start | bytes 1179656 | tf_op jit(solution)/shard_map/yin2_2/ppermute | solution.py:221
  81.1 19.3 %collective-permute-start.17 = (bf16[48,4096]{1,0:T(8,128)(2,1)S(1)}, bf16[48,4096]{1,0:T(8,128)(2,1)S(1)}, u32[]{:S(2)}, u32[]{:S(2)}) collective-permute-start(bf16[48,4096]{1,0:T(8,128)(2,1)S(1)} %get-tuple-element.75), channel_id=1, source_target_pairs={{0,3},{1,2},{2,1},{3,0},{4,7},{5,6},{6,5},{7,4},{8,11},{9,10},{10,... | collective-permute-start | bytes 1179656 | tf_op jit(solution)/shard_map/yin2_3/ppermute | solution.py:221
  82.9 44.9 %collective-permute-start.8 = (bf16[128,4224]{1,0:T(8,128)(2,1)S(1)}, bf16[128,4224]{1,0:T(8,128)(2,1)S(1)}, u32[]{:S(2)}, u32[]{:S(2)}) collective-permute-start(bf16[128,4224]{1,0:T(8,128)(2,1)S(1)} %collective-permute-done.7.block), channel_id=1, source_target_pairs={{0,4},{1,5},{2,6},{3,7},{4,8},{5,9},{6,10},{7,11},{8,12},{9,13},{1... | collective-permute-start | bytes 3244040 | tf_op jit(solution)/shard_map/zin3/ppermute | solution.py:221
  103.4 2.2 %collective-permute-start.18 = (bf16[48,4096]{1,0:T(8,128)(2,1)S(1)}, bf16[48,4096]{1,0:T(8,128)(2,1)S(1)}, u32[]{:S(2)}, u32[]{:S(2)}) collective-permute-start(bf16[48,4096]{1,0:T(8,128)(2,1)S(1)} %get-tuple-element.77), channel_id=1, source_target_pairs={{0,1},{1,0},{2,3},{3,2},{4,5},{5,4},{6,7},{7,6},{8,9},{9,8},{10,11... | collective-permute-start | bytes 1179656 | tf_op jit(solution)/shard_map/yout2_1/ppermute | solution.py:221
  103.5 10.3 %collective-permute-start.19 = (bf16[48,4096]{1,0:T(8,128)(2,1)S(1)}, bf16[48,4096]{1,0:T(8,128)(2,1)S(1)}, u32[]{:S(2)}, u32[]{:S(2)}) collective-permute-start(bf16[48,4096]{1,0:T(8,128)(2,1)S(1)} %get-tuple-element.78), channel_id=1, source_target_pairs={{0,2},{1,3},{2,0},{3,1},{4,6},{5,7},{6,4},{7,5},{8,10},{9,11},{10,... | collective-permute-start | bytes 1179656 | tf_op jit(solution)/shard_map/yout2_2/ppermute | solution.py:221
  103.8 19.3 %collective-permute-start.20 = (bf16[48,4096]{1,0:T(8,128)(2,1)S(1)}, bf16[48,4096]{1,0:T(8,128)(2,1)S(1)}, u32[]{:S(2)}, u32[]{:S(2)}) collective-permute-start(bf16[48,4096]{1,0:T(8,128)(2,1)S(1)} %get-tuple-element.79), channel_id=1, source_target_pairs={{0,3},{1,2},{2,1},{3,0},{4,7},{5,6},{6,5},{7,4},{8,11},{9,10},{10,... | collective-permute-start | bytes 1179656 | tf_op jit(solution)/shard_map/yout2_3/ppermute | solution.py:221
  124.8 29.4 %collective-permute-start.28 = (bf16[128,4224]{1,0:T(8,128)(2,1)S(1)}, bf16[128,4224]{1,0:T(8,128)(2,1)S(1)}, u32[]{:S(2)}, u32[]{:S(2)}) collective-permute-start(bf16[128,4224]{1,0:T(8,128)(2,1)S(1)} %combine2.1), channel_id=1, source_target_pairs={{0,4},{1,5},{2,6},{3,7},{4,8},{5,9},{6,10},{7,11},{8,12},{9,13},{1... | collective-permute-start | bytes 3244040 | tf_op jit(solution)/shard_map/zout2/ppermute | solution.py:221
  129.1 2.2 %collective-permute-start.9 = (bf16[48,4096]{1,0:T(8,128)(2,1)S(1)}, bf16[48,4096]{1,0:T(8,128)(2,1)S(1)}, u32[]{:S(2)}, u32[]{:S(2)}) collective-permute-start(bf16[48,4096]{1,0:T(8,128)(2,1)S(1)} %get-tuple-element.65), channel_id=1, source_target_pairs={{0,1},{1,0},{2,3},{3,2},{4,5},{5,4},{6,7},{7,6},{8,9},{9,8},{10,11... | collective-permute-start | bytes 1179656 | tf_op jit(solution)/shard_map/yin3_1/ppermute | solution.py:221
  129.5 10.5 %collective-permute-start.10 = (bf16[48,4096]{1,0:T(8,128)(2,1)S(1)}, bf16[48,4096]{1,0:T(8,128)(2,1)S(1)}, u32[]{:S(2)}, u32[]{:S(2)}) collective-permute-start(bf16[48,4096]{1,0:T(8,128)(2,1)S(1)} %get-tuple-element.66), channel_id=1, source_target_pairs={{0,2},{1,3},{2,0},{3,1},{4,6},{5,7},{6,4},{7,5},{8,10},{9,11},{10,... | collective-permute-start | bytes 1179656 | tf_op jit(solution)/shard_map/yin3_2/ppermute | solution.py:221
  129.7 19.3 %collective-permute-start.11 = (bf16[48,4096]{1,0:T(8,128)(2,1)S(1)}, bf16[48,4096]{1,0:T(8,128)(2,1)S(1)}, u32[]{:S(2)}, u32[]{:S(2)}) collective-permute-start(bf16[48,4096]{1,0:T(8,128)(2,1)S(1)} %get-tuple-element.67), channel_id=1, source_target_pairs={{0,3},{1,2},{2,1},{3,0},{4,7},{5,6},{6,5},{7,4},{8,11},{9,10},{10,... | collective-permute-start | bytes 1179656 | tf_op jit(solution)/shard_map/yin3_3/ppermute | solution.py:221
  152.0 2.2 %collective-permute-start.12 = (bf16[48,4096]{1,0:T(8,128)(2,1)S(1)}, bf16[48,4096]{1,0:T(8,128)(2,1)S(1)}, u32[]{:S(2)}, u32[]{:S(2)}) collective-permute-start(bf16[48,4096]{1,0:T(8,128)(2,1)S(1)} %get-tuple-element.69), channel_id=1, source_target_pairs={{0,1},{1,0},{2,3},{3,2},{4,5},{5,4},{6,7},{7,6},{8,9},{9,8},{10,11... | collective-permute-start | bytes 1179656 | tf_op jit(solution)/shard_map/yout3_1/ppermute | solution.py:221
  152.1 10.3 %collective-permute-start.13 = (bf16[48,4096]{1,0:T(8,128)(2,1)S(1)}, bf16[48,4096]{1,0:T(8,128)(2,1)S(1)}, u32[]{:S(2)}, u32[]{:S(2)}) collective-permute-start(bf16[48,4096]{1,0:T(8,128)(2,1)S(1)} %get-tuple-element.70), channel_id=1, source_target_pairs={{0,2},{1,3},{2,0},{3,1},{4,6},{5,7},{6,4},{7,5},{8,10},{9,11},{10,... | collective-permute-start | bytes 1179656 | tf_op jit(solution)/shard_map/yout3_2/ppermute | solution.py:221
  152.4 19.0 %collective-permute-start.14 = (bf16[48,4096]{1,0:T(8,128)(2,1)S(1)}, bf16[48,4096]{1,0:T(8,128)(2,1)S(1)}, u32[]{:S(2)}, u32[]{:S(2)}) collective-permute-start(bf16[48,4096]{1,0:T(8,128)(2,1)S(1)} %get-tuple-element.71), channel_id=1, source_target_pairs={{0,3},{1,2},{2,1},{3,0},{4,7},{5,6},{6,5},{7,4},{8,11},{9,10},{10,... | collective-permute-start | bytes 1179656 | tf_op jit(solution)/shard_map/yout3_3/ppermute | solution.py:221
  173.1 44.1 %collective-permute-start.29 = (bf16[128,4224]{1,0:T(8,128)(2,1)S(1)}, bf16[128,4224]{1,0:T(8,128)(2,1)S(1)}, u32[]{:S(2)}, u32[]{:S(2)}) collective-permute-start(bf16[128,4224]{1,0:T(8,128)(2,1)S(1)} %combine3.1), channel_id=1, source_target_pairs={{0,4},{1,5},{2,6},{3,7},{4,8},{5,9},{6,10},{7,11},{8,12},{9,13},{1... | collective-permute-start | bytes 3244040 | tf_op jit(solution)/shard_map/zout3/ppermute | solution.py:221
  175.2 2.2 %collective-permute-start = (bf16[48,4096]{1,0:T(8,128)(2,1)S(1)}, bf16[48,4096]{1,0:T(8,128)(2,1)S(1)}, u32[]{:S(2)}, u32[]{:S(2)}) collective-permute-start(bf16[48,4096]{1,0:T(8,128)(2,1)S(1)} %get-tuple-element.57), channel_id=1, source_target_pairs={{0,1},{1,0},{2,3},{3,2},{4,5},{5,4},{6,7},{7,6},{8,9},{9,8},{10,11... | collective-permute-start | bytes 1179656 | tf_op jit(solution)/shard_map/yin0_1/ppermute | solution.py:221
  175.3 10.2 %collective-permute-start.1 = (bf16[48,4096]{1,0:T(8,128)(2,1)S(1)}, bf16[48,4096]{1,0:T(8,128)(2,1)S(1)}, u32[]{:S(2)}, u32[]{:S(2)}) collective-permute-start(bf16[48,4096]{1,0:T(8,128)(2,1)S(1)} %get-tuple-element.58), channel_id=1, source_target_pairs={{0,2},{1,3},{2,0},{3,1},{4,6},{5,7},{6,4},{7,5},{8,10},{9,11},{10,... | collective-permute-start | bytes 1179656 | tf_op jit(solution)/shard_map/yin0_2/ppermute | solution.py:221
  175.5 19.3 %collective-permute-start.2 = (bf16[48,4096]{1,0:T(8,128)(2,1)S(1)}, bf16[48,4096]{1,0:T(8,128)(2,1)S(1)}, u32[]{:S(2)}, u32[]{:S(2)}) collective-permute-start(bf16[48,4096]{1,0:T(8,128)(2,1)S(1)} %get-tuple-element.59), channel_id=1, source_target_pairs={{0,3},{1,2},{2,1},{3,0},{4,7},{5,6},{6,5},{7,4},{8,11},{9,10},{10,... | collective-permute-start | bytes 1179656 | tf_op jit(solution)/shard_map/yin0_3/ppermute | solution.py:221
  197.8 8.9 %collective-permute-start.3 = (bf16[48,4096]{1,0:T(8,128)(2,1)S(1)}, bf16[48,4096]{1,0:T(8,128)(2,1)S(1)}, u32[]{:S(2)}, u32[]{:S(2)}) collective-permute-start(bf16[48,4096]{1,0:T(8,128)(2,1)S(1)} %get-tuple-element.61), channel_id=1, source_target_pairs={{0,1},{1,0},{2,3},{3,2},{4,5},{5,4},{6,7},{7,6},{8,9},{9,8},{10,11... | collective-permute-start | bytes 1179656 | tf_op jit(solution)/shard_map/yout0_1/ppermute | solution.py:221
  197.9 10.3 %collective-permute-start.4 = (bf16[48,4096]{1,0:T(8,128)(2,1)S(1)}, bf16[48,4096]{1,0:T(8,128)(2,1)S(1)}, u32[]{:S(2)}, u32[]{:S(2)}) collective-permute-start(bf16[48,4096]{1,0:T(8,128)(2,1)S(1)} %get-tuple-element.62), channel_id=1, source_target_pairs={{0,2},{1,3},{2,0},{3,1},{4,6},{5,7},{6,4},{7,5},{8,10},{9,11},{10,... | collective-permute-start | bytes 1179656 | tf_op jit(solution)/shard_map/yout0_2/ppermute | solution.py:221
  198.2 19.0 %collective-permute-start.5 = (bf16[48,4096]{1,0:T(8,128)(2,1)S(1)}, bf16[48,4096]{1,0:T(8,128)(2,1)S(1)}, u32[]{:S(2)}, u32[]{:S(2)}) collective-permute-start(bf16[48,4096]{1,0:T(8,128)(2,1)S(1)} %get-tuple-element.63), channel_id=1, source_target_pairs={{0,3},{1,2},{2,1},{3,0},{4,7},{5,6},{6,5},{7,4},{8,11},{9,10},{10,... | collective-permute-start | bytes 1179656 | tf_op jit(solution)/shard_map/yout0_3/ppermute | solution.py:221
  (4 other events, 6.9 us)

commit v3 on v2

v3 whole, which is shorter than its diff:
```python
import functools

import jax
import jax.numpy as jnp
from jax import lax
from jax.experimental import pallas as pl
from jax.experimental.pallas import tpu as pltpu
from jax.sharding import PartitionSpec as P


F32 = jnp.float32
BF16 = jnp.bfloat16
TILE = 512
VMEM = pl.BlockSpec(memory_space=pltpu.VMEM)
SMEM = pl.BlockSpec(memory_space=pltpu.SMEM)


def rounded(value):
    return value.astype(BF16).astype(F32)


def nt(a, b):
    return lax.dot_general(a, b, (((1,), (1,)), ((), ())), preferred_element_type=F32)


def nn(a, b):
    return jnp.dot(a, b, preferred_element_type=F32)


def expert_ids(place, plane):
    return [place[0] * plane + jnp.bitwise_xor(place[1], e) for e in range(plane)]


def slots_of(place, ids, parts, plane, depth, route_count):
    tokens = ids.shape[1]
    rows = lax.broadcasted_iota(jnp.int32, (tokens, tokens), 0)
    cols = lax.broadcasted_iota(jnp.int32, (tokens, tokens), 1)
    before = jnp.where(rows < cols, 1.0, 0.0).astype(BF16)
    route = [ids[k : k + 1] for k in range(route_count)]
    probs = [
        parts[k : k + 1]
        + parts[route_count + k : route_count + k + 1]
        + parts[2 * route_count + k : 2 * route_count + k + 1]
        for k in range(route_count)
    ]
    slot = lax.broadcasted_iota(jnp.int32, (depth, tokens), 0)
    named, weight = [], []
    for eid in expert_ids(place, plane):
        hit = [jnp.where(r == eid, 1.0, 0.0) for r in route]
        named.append(sum(hit))
        weight.append(sum(h * p for h, p in zip(hit, probs)))
    pad = [jnp.zeros((8 - plane % 8, tokens), F32)] if plane % 8 else []
    rank = nn(jnp.concatenate(named + pad, axis=0).astype(BF16), before)
    picks, gates = [], []
    for e in range(plane):
        wanted = jnp.broadcast_to(rank[e : e + 1], (depth, tokens)).astype(jnp.int32)
        present = jnp.broadcast_to(named[e], (depth, tokens))
        pick = jnp.where(wanted == slot, present, 0.0)
        picks.append(pick)
        gates.append(jnp.sum(pick * weight[e], axis=1, keepdims=True))
    return jnp.concatenate(picks, axis=0), jnp.concatenate(gates, axis=0)


def select_kernel(plane, depth, route_count, scaled, place, ids, block, *outs):
    width = outs[0].shape[1]
    tokens = ids.shape[1]
    if scaled:
        parts = block[0:16, width:].astype(F32)
    else:
        parts = jnp.zeros((16, tokens), F32)
    pick, gate = slots_of(place, ids[...], parts, plane, depth, route_count)
    chooser = pick.astype(BF16)
    for start in range(0, width, TILE):
        cols = pl.ds(start, TILE)
        found = nn(chooser, block[:, cols])
        if scaled:
            found = found * gate
        found = found.astype(BF16)
        for e in range(plane):
            outs[e][:, cols] = found[e * depth : (e + 1) * depth]


def forward_kernel(plane, *refs):
    rows = refs[:plane]
    gate_w, up_w, down_w = refs[plane : plane + 3]
    outs = refs[plane + 3 : 2 * plane + 3]
    hidden_out, gate_out, up_out = refs[2 * plane + 3 :]
    width = gate_w.shape[0]
    depth = rows[0].shape[0]
    row_x = jnp.concatenate([r[...] for r in rows], axis=0)
    gate_pre = nn(row_x, gate_w[...])
    up_pre = nn(row_x, up_w[...])
    gate_out[...] = gate_pre
    up_out[...] = up_pre
    gate_sig = 1.0 / (1.0 + jnp.exp(-gate_pre))
    hidden = (gate_pre * gate_sig * up_pre).astype(BF16)
    hidden_out[...] = hidden
    for start in range(0, width, TILE):
        cols = pl.ds(start, TILE)
        y = nn(hidden, down_w[:, cols]).astype(BF16)
        for e in range(plane):
            outs[e][:, cols] = y[e * depth : (e + 1) * depth]


def backward_kernel(plane, *refs):
    rows = refs[:plane]
    gate_pre, up_pre, gate_w, up_w, down_w = refs[plane : plane + 5]
    outs = refs[plane + 5 : 2 * plane + 5]
    ggp_out, gup_out = refs[2 * plane + 5 :]
    width = gate_w.shape[0]
    depth = rows[0].shape[0]
    row_c = jnp.concatenate([r[...] for r in rows], axis=0)
    d_hidden = nt(row_c, down_w[...])
    gate_pre = gate_pre[...]
    gate_sig = 1.0 / (1.0 + jnp.exp(-gate_pre))
    slope = gate_sig * (1.0 + gate_pre * (1.0 - gate_sig))
    ggp = (d_hidden * up_pre[...] * slope).astype(BF16)
    gup = (d_hidden * (gate_pre * gate_sig)).astype(BF16)
    ggp_out[...] = ggp
    gup_out[...] = gup
    for start in range(0, width, TILE):
        cols = pl.ds(start, TILE)
        dx = (nt(ggp, gate_w[cols, :]) + nt(gup, up_w[cols, :])).astype(BF16)
        for e in range(plane):
            outs[e][:, cols] = dx[e * depth : (e + 1) * depth]


def combine_out_kernel(plane, depth, route_count, has_running, is_last, place, ids, block, *refs):
    near = refs[:plane]
    refs = refs[plane:]
    running = None
    if has_running:
        running, refs = refs[0], refs[1:]
    width = near[0].shape[1]
    tokens = ids.shape[1]
    ids_now = ids[...]
    parts = block[0:16, width:].astype(F32)
    pick, gate = slots_of(place, ids_now, parts, plane, depth, route_count)
    weighted = pick * gate
    weight_high = rounded(weighted)
    high = jnp.transpose(weight_high).astype(BF16)
    low = jnp.transpose(weighted - weight_high).astype(BF16)
    dots = jnp.zeros((plane * depth, tokens), F32)
    for start in range(0, width, TILE):
        cols = pl.ds(start, TILE)
        y = jnp.concatenate([n[:, cols] for n in near], axis=0)
        part_y = nn(high, y) + nn(low, y)
        dots = dots + nt(y, block[:, cols])
        if has_running:
            part_y = part_y + running[:, cols].astype(F32)
        refs[0][:, cols] = part_y.astype(BF16)
    dots = pick * dots
    found = [jnp.sum(dots[e * depth : (e + 1) * depth], axis=0, keepdims=True) for e in range(plane)]
    gates = []
    for k in range(route_count):
        mine = ids_now[k : k + 1]
        total = jnp.zeros((1, tokens), F32)
        for eid, value in zip(expert_ids(place, plane), found):
            total = total + jnp.where(mine == eid, value, 0.0)
        gates.append(total)
    if has_running:
        old = running[0:16, width:].astype(F32)
        for k in range(route_count):
            for piece in range(3):
                at = piece * route_count + k
                gates[k] = gates[k] + old[at : at + 1]
    if is_last:
        pad = jnp.zeros((8 - route_count, tokens), F32)
        refs[1][...] = jnp.concatenate(gates + [pad], axis=0)
    else:
        high = [rounded(g) for g in gates]
        middle = [rounded(g - h) for g, h in zip(gates, high)]
        low = [g - h - m for g, h, m in zip(gates, high, middle)]
        pad = jnp.zeros((tokens - 3 * route_count, tokens), F32)
        refs[0][:, width:] = jnp.concatenate(high + middle + low + [pad], axis=0).astype(BF16)


def combine_back_kernel(plane, depth, route_count, has_running, place, ids, *refs):
    near = refs[:plane]
    out = refs[-1]
    width = near[0].shape[1]
    parts = jnp.zeros((16, ids.shape[1]), F32)
    pick, _ = slots_of(place, ids[...], parts, plane, depth, route_count)
    spread = jnp.transpose(pick).astype(BF16)
    for start in range(0, width, TILE):
        cols = pl.ds(start, TILE)
        dx = jnp.concatenate([n[:, cols] for n in near], axis=0)
        part_dx = nn(spread, dx)
        if has_running:
            part_dx = part_dx + refs[plane][:, cols].astype(F32)
        out[:, cols] = part_dx.astype(BF16)


def grads_kernel(ring, plane, *refs):
    count = ring * plane
    rows_x, rows_c = refs[:count], refs[count : 2 * count]
    small = refs[2 * count : 2 * count + 3 * ring]
    gate_out, up_out, down_out = refs[2 * count + 3 * ring :]
    width = gate_out.shape[0]
    hidden = jnp.transpose(jnp.concatenate([small[3 * s][...] for s in range(ring)], axis=0))
    ggp = jnp.concatenate([small[3 * s + 1][...] for s in range(ring)], axis=0)
    gup = jnp.concatenate([small[3 * s + 2][...] for s in range(ring)], axis=0)
    step = TILE // 2
    for start in range(0, width, step):
        cols = pl.ds(start, step)
        x = jnp.transpose(jnp.concatenate([r[:, cols] for r in rows_x], axis=0))
        gate_out[cols, :] = nn(x, ggp).astype(BF16)
        up_out[cols, :] = nn(x, gup).astype(BF16)
        c = jnp.concatenate([r[:, cols] for r in rows_c], axis=0)
        down_out[:, cols] = nn(hidden, c).astype(BF16)


def call(body, outs, flops, inputs):
    total = sum(x.size * x.dtype.itemsize for x in inputs)
    total += sum(o.size * o.dtype.itemsize for o in outs)
    specs = [SMEM if x.dtype == jnp.int32 and x.ndim == 1 else VMEM for x in inputs]
    return pl.pallas_call(
        body,
        out_shape=tuple(outs),
        in_specs=specs,
        out_specs=tuple(VMEM for _ in outs),
        cost_estimate=pl.CostEstimate(flops=flops, bytes_accessed=total, transcendentals=0),
        compiler_params=pltpu.CompilerParams(vmem_limit_bytes=40 * 1024 * 1024),
    )(*inputs)


def local(tokens, cotangent, route_ids, gate_probs, w_gate, w_up, w_down):
    owner_count = lax.axis_size("owner")
    me = lax.axis_index("owner")
    token_rows, width = tokens.shape
    route_count = route_ids.shape[1]
    hidden_width = w_gate.shape[2]
    depth = 2 * token_rows * route_count // owner_count
    depth = (depth + 15) // 16 * 16
    plane = 4 if owner_count % 4 == 0 else 2
    ring = owner_count // plane
    column = me % plane
    my_z = me // plane
    place = jnp.stack([my_z, column]).astype(jnp.int32)

    ring_up = [(i, (i + plane) % owner_count) for i in range(owner_count)]
    swaps = [[(i, i ^ e) for i in range(owner_count)] for e in range(plane)]

    def hop(value, pairs):
        return lax.ppermute(value, "owner", pairs)

    id_table = route_ids.reshape(ring, plane, token_rows, route_count)
    line_ids = lax.dynamic_index_in_dim(id_table, column, 1, keepdims=False)
    line_ids = jnp.swapaxes(line_ids, 1, 2)
    line_ids = jnp.pad(line_ids, ((0, 0), (0, 8 - route_count), (0, 0)), constant_values=-1)
    step_ids = [
        lax.dynamic_index_in_dim(line_ids, (my_z - s) % ring, 0, keepdims=False) for s in range(ring)
    ]

    probs = gate_probs.T
    high = lax.reduce_precision(probs, 8, 7)
    middle = lax.reduce_precision(probs - high, 8, 7)
    low = probs - high - middle
    tail = jnp.concatenate([high, middle, low], axis=0).astype(BF16)
    tail = jnp.pad(tail, ((0, token_rows - 3 * route_count), (0, 0)))
    block_x = [tokens]
    block_c = [jnp.concatenate([cotangent, tail], axis=1)]
    for _ in range(1, ring):
        block_x.append(hop(block_x[-1], ring_up))
        block_c.append(hop(block_c[-1], ring_up))

    def shape(*dims, kind=BF16):
        return jax.ShapeDtypeStruct(dims, kind)

    rows = plane * depth
    slots = [shape(depth, width)] * plane
    weights = [w_gate[0], w_up[0], w_down[0]]
    move_flops = 2 * rows * token_rows * width
    dense_flops = 2 * rows * width * hidden_width

    def exchange(values):
        return [values[0]] + [hop(values[e], swaps[e]) for e in range(1, plane)]

    got_x, got_c, small = [], [], []
    back_y, back_d = [], []
    for s in range(ring):
        for blocks, got, scaled in ((block_x, got_x, False), (block_c, got_c, True)):
            picked = call(
                functools.partial(select_kernel, plane, depth, route_count, scaled),
                slots,
                move_flops,
                [place, step_ids[s], blocks[s]],
            )
            got.append(exchange(picked))
        ahead = call(
            functools.partial(forward_kernel, plane),
            slots + [shape(rows, hidden_width)] + [shape(rows, hidden_width, kind=F32)] * 2,
            3 * dense_flops,
            got_x[s] + weights,
        )
        back = call(
            functools.partial(backward_kernel, plane),
            slots + [shape(rows, hidden_width)] * 2,
            3 * dense_flops,
            got_c[s] + list(ahead[plane + 1 :]) + weights,
        )
        small += [ahead[plane], back[plane], back[plane + 1]]
        back_y.append(exchange(ahead[:plane]))
        back_d.append(exchange(back[:plane]))

    run_y, run_d = [], []
    for s in list(range(1, ring)) + [0]:
        last = s == 0
        row = shape(token_rows, width)
        outs_y = [row, shape(8, token_rows, kind=F32)]
        if not last:
            outs_y = [shape(token_rows, width + token_rows)]
        done_y = call(
            functools.partial(
                combine_out_kernel, plane, depth, route_count, bool(run_y), last
            ),
            outs_y,
            3 * move_flops,
            [place, step_ids[s], block_c[s]] + back_y[s] + run_y,
        )
        done_d = call(
            functools.partial(combine_back_kernel, plane, depth, route_count, bool(run_d)),
            [row],
            move_flops,
            [place, step_ids[s]] + back_d[s] + run_d,
        )
        if not last:
            run_y = [hop(done_y[0], ring_up)]
            run_d = [hop(done_d[0], ring_up)]
    expert_out, gates = done_y
    grad_tokens = done_d[0]

    grads = call(
        functools.partial(grads_kernel, ring, plane),
        [shape(width, hidden_width), shape(width, hidden_width), shape(hidden_width, width)],
        3 * ring * dense_flops,
        [g for got in (got_x, got_c) for s in range(ring) for g in got[s]] + small,
    )
    return (
        expert_out,
        grad_tokens,
        gates[:route_count].T,
        grads[0][None],
        grads[1][None],
        grads[2][None],
    )


def solution(mesh):
    rows = P(("group", "owner"), None)
    stacked = P(("group", "owner"), None, None)
    weights = P("owner", None, None)

    return jax.shard_map(
        local,
        mesh=mesh,
        in_specs=(rows, rows, P("group", None), rows, weights, weights, weights),
        out_specs=(rows, rows, rows, stacked, stacked, stacked),
        check_vma=False,
    )
```

time: 224 us -> 184 us (0.82)
  waiting for transfers between devices: 155 us -> 75.7 us
  starting transfers between devices: 26.3 us -> 57.5 us
  Pallas kernels: 31.1 us -> 40.6 us
    ppermute x30 -> x60, waiting for transfers between devices: 155 us -> 75.7 us  [hop(): return lax.ppermute(value, 'owner', pairs)]
    ppermute x30 -> x60, starting transfers between devices: 26.3 us -> 57.5 us  [hop(): return lax.ppermute(value, 'owner', pairs)]
    pallas_call x13 -> x25, Pallas kernels: 31.1 us -> 40.6 us  [call(): pl.pallas_call(body, out_shape=tuple(outs), in_specs=specs, out_specs=tup...]
  transfers between devices with their start and end apart: 30 -> 60, of which waited for: 18 -> 23; matrix products, arithmetic and copies ran while one was open for 0% -> 2% of each run, Pallas kernels for 12% -> 21%
where the time goes in v3:
time: 184 us; the launch traced here: 181 us
  waiting for transfers between devices  75.7 us (41%)
  starting transfers between devices  57.5 us (31%)
  Pallas kernels  40.6 us (22%)
  local copies, waits for them, and re-layouts  4.22 us (2%)
  other arithmetic  1.86 us (1%)
    ppermute x60, waiting for transfers between devices, hop(): return lax.ppermute(value, 'owner', pairs)  75.7 us
    ppermute x60, starting transfers between devices, hop(): return lax.ppermute(value, 'owner', pairs)  57.5 us
    pallas_call x25, Pallas kernels, call(): pl.pallas_call(body, out_shape=tuple(outs), in_specs=specs, out_specs=tup...  40.6 us
  transfers between devices with their start and end apart: 60, of which 23 were waited for; matrix products, arithmetic and copies ran while one was open for 2% of the time, Pallas kernels for 21%

profile of v3, /device:TPU:13, one launch (start us, length us, event | category | flops | bytes accessed | tf_op | source)
XLA Modules:
  0.0 180.9 jit_solution(8573254288767825577)
XLA Ops:
  8.4 5.4 %collective-permute-done.9.block = bf16[128,2048]{1,0:T(8,128)(2,1)} collective-permute-done((bf16[128,2048]{1,0:T(8,128)(2,1)}, bf16[128,2048]{1,0:T(8,128)(2,1)}, u32[]{:S(2)}, u32[]{:S(2)}) %collective-permute-start.9) | collective-permute-done | bytes 524320 | tf_op jit(solution)/shard_map/ppermute | solution.py:245
  15.4 2.7 %collective-permute-start.24 = (bf16[48,2048]{1,0:T(8,128)(2,1)S(1)}, bf16[48,2048]{1,0:T(8,128)(2,1)S(1)}, u32[]{:S(2)}, u32[]{:S(2)}) collective-permute-start(bf16[48,2048]{1,0:T(8,128)(2,1)S(1)} %get-tuple-element.120), channel_id=1, source_target_pairs={{0,1},{1,0},{2,3},{3,2},{4,5},{5,4},{6,7},{7,6},{8,9},{9,8},{10,11... | collective-permute-start | bytes 589832 | tf_op jit(solution)/shard_map/ppermute | solution.py:245
  19.8 5.9 %collective-permute-done.6.block = bf16[128,2176]{1,0:T(8,128)(2,1)S(1)} collective-permute-done((bf16[128,2176]{1,0:T(8,128)(2,1)S(1)}, bf16[128,2176]{1,0:T(8,128)(2,1)S(1)}, u32[]{:S(2)}, u32[]{:S(2)}) %collective-permute-start.6) | collective-permute-done | bytes 557088 | tf_op jit(solution)/shard_map/ppermute | solution.py:245
  37.2 2.1 %collective-permute-start.2 = (bf16[48,2048]{1,0:T(8,128)(2,1)S(1)}, bf16[48,2048]{1,0:T(8,128)(2,1)S(1)}, u32[]{:S(2)}, u32[]{:S(2)}) collective-permute-start(bf16[48,2048]{1,0:T(8,128)(2,1)S(1)} %get-tuple-element.98), channel_id=1, source_target_pairs={{0,3},{1,2},{2,1},{3,0},{4,7},{5,6},{6,5},{7,4},{8,11},{9,10},{10,... | collective-permute-start | bytes 589832 | tf_op jit(solution)/shard_map/ppermute | solution.py:245
  39.4 1.8 %shard_map.137 = (bf16[48,2048]{1,0:T(8,128)(2,1)S(1)}, bf16[48,2048]{1,0:T(8,128)(2,1)S(1)}, bf16[48,2048]{1,0:T(8,128)(2,1)S(1)}, bf16[48,2048]{1,0:T(8,128)(2...) custom-call(bf16[48,2048]{1,0:T(8,128)(2,1)S(1)} %get-tuple-element.158.refs_0_.refs_20_, ...), custom_call_target="tpu_custom_call" | custom-call | flops 905969664 | bytes 7176192 | tf_op jit(solution)/shard_map/pallas_call | solution.py:217
  43.0 6.3 %collective-permute-done.2.refs_3_ = bf16[48,2048]{1,0:T(8,128)(2,1)S(1)} collective-permute-done((bf16[48,2048]{1,0:T(8,128)(2,1)S(1)}, bf16[48,2048]{1,0:T(8,128)(2,1)S(1)}, u32[]{:S(2)}, u32[]{:S(2)}) %collective-permute-start.2) | collective-permute-done | bytes 196640 | tf_op jit(solution)/shard_map/ppermute | solution.py:245
  53.9 3.5 %collective-permute-done.29.refs_3_ = bf16[48,2048]{1,0:T(8,128)(2,1)S(1)} collective-permute-done((bf16[48,2048]{1,0:T(8,128)(2,1)S(1)}, bf16[48,2048]{1,0:T(8,128)(2,1)S(1)}, u32[]{:S(2)}, u32[]{:S(2)}) %collective-permute-start.29) | collective-permute-done | bytes 196640 | tf_op jit(solution)/shard_map/ppermute | solution.py:245
  64.6 5.2 %collective-permute-done.20.refs_3_.refs_11_ = bf16[48,2048]{1,0:T(8,128)(2,1)S(1)} collective-permute-done((bf16[48,2048]{1,0:T(8,128)(2,1)S(1)}, bf16[48,2048]{1,0:T(8,128)(2,1)S(1)}, u32[]{:S(2)}, u32[]{:S(2)}) %collective-permute-start.20) | collective-permute-done | bytes 196640 | tf_op jit(solution)/shard_map/ppermute | solution.py:245
  71.3 2.7 %collective-permute-done.56.refs_3_ = bf16[48,2048]{1,0:T(8,128)(2,1)S(1)} collective-permute-done((bf16[48,2048]{1,0:T(8,128)(2,1)S(1)}, bf16[48,2048]{1,0:T(8,128)(2,1)S(1)}, u32[]{:S(2)}, u32[]{:S(2)}) %collective-permute-start.56) | collective-permute-done | bytes 196640 | tf_op jit(solution)/shard_map/ppermute | solution.py:245
  75.6 1.9 %collective-permute-start.30 = (bf16[128,2176]{1,0:T(8,128)(2,1)S(1)}, bf16[128,2176]{1,0:T(8,128)(2,1)S(1)}, u32[]{:S(2)}, u32[]{:S(2)}) collective-permute-start(bf16[128,2176]{1,0:T(8,128)(2,1)S(1)} %shard_map.126), channel_id=1, source_target_pairs={{0,4},{1,5},{2,6},{3,7},{4,8},{5,9},{6,10},{7,11},{8,12},{9,13},{1... | collective-permute-start | bytes 1671176 | tf_op jit(solution)/shard_map/ppermute | solution.py:245
  78.9 2.9 %collective-permute-done.47.refs_3_.refs_27_ = bf16[48,2048]{1,0:T(8,128)(2,1)S(1)} collective-permute-done((bf16[48,2048]{1,0:T(8,128)(2,1)S(1)}, bf16[48,2048]{1,0:T(8,128)(2,1)S(1)}, u32[]{:S(2)}, u32[]{:S(2)}) %collective-permute-start.47) | collective-permute-done | bytes 196640 | tf_op jit(solution)/shard_map/ppermute | solution.py:245
  83.9 6.2 %collective-permute-done.22.refs_2_ = bf16[48,2048]{1,0:T(8,128)(2,1)S(1)} collective-permute-done((bf16[48,2048]{1,0:T(8,128)(2,1)S(1)}, bf16[48,2048]{1,0:T(8,128)(2,1)S(1)}, u32[]{:S(2)}, u32[]{:S(2)}) %collective-permute-start.22) | collective-permute-done | bytes 196640 | tf_op jit(solution)/shard_map/ppermute | solution.py:245
  91.1 1.8 %shard_map.135 = (bf16[48,2048]{1,0:T(8,128)(2,1)S(1)}, bf16[48,2048]{1,0:T(8,128)(2,1)S(1)}, bf16[48,2048]{1,0:T(8,128)(2,1)S(1)}, bf16[48,2048]{1,0:T(8,128)(2...) custom-call(bf16[48,2048]{1,0:T(8,128)(2,1)S(1)} %get-tuple-element.148.refs_0_.refs_24_, ...), custom_call_target="tpu_custom_call" | custom-call | flops 905969664 | bytes 7176192 | tf_op jit(solution)/shard_map/pallas_call | solution.py:217
  94.0 3.3 %collective-permute-done.23.refs_3_ = bf16[48,2048]{1,0:T(8,128)(2,1)S(1)} collective-permute-done((bf16[48,2048]{1,0:T(8,128)(2,1)S(1)}, bf16[48,2048]{1,0:T(8,128)(2,1)S(1)}, u32[]{:S(2)}, u32[]{:S(2)}) %collective-permute-start.23) | collective-permute-done | bytes 196640 | tf_op jit(solution)/shard_map/ppermute | solution.py:245
  98.3 2.7 %collective-permute-done.57.refs_4_ = bf16[128,2048]{1,0:T(8,128)(2,1)S(1)} collective-permute-done((bf16[128,2048]{1,0:T(8,128)(2,1)S(1)}, bf16[128,2048]{1,0:T(8,128)(2,1)S(1)}, u32[]{:S(2)}, u32[]{:S(2)}) %collective-permute-start.57) | collective-permute-done | bytes 524320 | tf_op jit(solution)/shard_map/ppermute | solution.py:245
  101.0 2.0 %collective-permute-start.14 = (bf16[48,2048]{1,0:T(8,128)(2,1)S(1)}, bf16[48,2048]{1,0:T(8,128)(2,1)S(1)}, u32[]{:S(2)}, u32[]{:S(2)}) collective-permute-start(bf16[48,2048]{1,0:T(8,128)(2,1)S(1)} %get-tuple-element.106), channel_id=1, source_target_pairs={{0,3},{1,2},{2,1},{3,0},{4,7},{5,6},{6,5},{7,4},{8,11},{9,10},{10,... | collective-permute-start | bytes 589832 | tf_op jit(solution)/shard_map/ppermute | solution.py:245
  104.5 2.0 %collective-permute-start.31 = (bf16[128,2176]{1,0:T(8,128)(2,1)S(1)}, bf16[128,2176]{1,0:T(8,128)(2,1)S(1)}, u32[]{:S(2)}, u32[]{:S(2)}) collective-permute-start(bf16[128,2176]{1,0:T(8,128)(2,1)S(1)} %shard_map.127), channel_id=1, source_target_pairs={{0,4},{1,5},{2,6},{3,7},{4,8},{5,9},{6,10},{7,11},{8,12},{9,13},{1... | collective-permute-start | bytes 1671176 | tf_op jit(solution)/shard_map/ppermute | solution.py:245
  106.6 6.3 %collective-permute-done.8.block = bf16[128,2176]{1,0:T(8,128)(2,1)S(1)} collective-permute-done((bf16[128,2176]{1,0:T(8,128)(2,1)S(1)}, bf16[128,2176]{1,0:T(8,128)(2,1)S(1)}, u32[]{:S(2)}, u32[]{:S(2)}) %collective-permute-start.8) | collective-permute-done | bytes 557088 | tf_op jit(solution)/shard_map/ppermute | solution.py:245
  114.3 3.3 %collective-permute-start.50 = (bf16[48,2048]{1,0:T(8,128)(2,1)S(1)}, bf16[48,2048]{1,0:T(8,128)(2,1)S(1)}, u32[]{:S(2)}, u32[]{:S(2)}) collective-permute-start(bf16[48,2048]{1,0:T(8,128)(2,1)S(1)} %get-tuple-element.157), channel_id=1, source_target_pairs={{0,3},{1,2},{2,1},{3,0},{4,7},{5,6},{6,5},{7,4},{8,11},{9,10},{10,... | collective-permute-start | bytes 589832 | tf_op jit(solution)/shard_map/ppermute | solution.py:245
  119.3 2.4 %collective-permute-start.15 = (bf16[48,2048]{1,0:T(8,128)(2,1)S(1)}, bf16[48,2048]{1,0:T(8,128)(2,1)S(1)}, u32[]{:S(2)}, u32[]{:S(2)}) collective-permute-start(bf16[48,2048]{1,0:T(8,128)(2,1)S(1)} %get-tuple-element.108), channel_id=1, source_target_pairs={{0,1},{1,0},{2,3},{3,2},{4,5},{5,4},{6,7},{7,6},{8,9},{9,8},{10,11... | collective-permute-start | bytes 589832 | tf_op jit(solution)/shard_map/ppermute | solution.py:245
  121.7 3.8 %collective-permute-done.50.refs_3_ = bf16[48,2048]{1,0:T(8,128)(2,1)S(1)} collective-permute-done((bf16[48,2048]{1,0:T(8,128)(2,1)S(1)}, bf16[48,2048]{1,0:T(8,128)(2,1)S(1)}, u32[]{:S(2)}, u32[]{:S(2)}) %collective-permute-start.50) | collective-permute-done | bytes 196640 | tf_op jit(solution)/shard_map/ppermute | solution.py:245
  129.2 1.9 %collective-permute-start.41 = (bf16[48,2048]{1,0:T(8,128)(2,1)S(1)}, bf16[48,2048]{1,0:T(8,128)(2,1)S(1)}, u32[]{:S(2)}, u32[]{:S(2)}) collective-permute-start(bf16[48,2048]{1,0:T(8,128)(2,1)S(1)} %get-tuple-element.141), channel_id=1, source_target_pairs={{0,3},{1,2},{2,1},{3,0},{4,7},{5,6},{6,5},{7,4},{8,11},{9,10},{10,... | collective-permute-start | bytes 589832 | tf_op jit(solution)/shard_map/ppermute | solution.py:245
  133.5 3.8 %collective-permute-done.17.refs_3_ = bf16[48,2048]{1,0:T(8,128)(2,1)S(1)} collective-permute-done((bf16[48,2048]{1,0:T(8,128)(2,1)S(1)}, bf16[48,2048]{1,0:T(8,128)(2,1)S(1)}, u32[]{:S(2)}, u32[]{:S(2)}) %collective-permute-start.17) | collective-permute-done | bytes 196640 | tf_op jit(solution)/shard_map/ppermute | solution.py:245
  143.1 1.8 %shard_map.133 = (bf16[48,2048]{1,0:T(8,128)(2,1)S(1)}, bf16[48,2048]{1,0:T(8,128)(2,1)S(1)}, bf16[48,2048]{1,0:T(8,128)(2,1)S(1)}, bf16[48,2048]{1,0:T(8,128)(2...) custom-call(bf16[48,2048]{1,0:T(8,128)(2,1)S(1)} %get-tuple-element.138.refs_0_.refs_28_, ...), custom_call_target="tpu_custom_call" | custom-call | flops 905969664 | bytes 7176192 | tf_op jit(solution)/shard_map/pallas_call | solution.py:217
  145.7 4.2 %collective-permute-done.35.refs_3_.refs_19_ = bf16[48,2048]{1,0:T(8,128)(2,1)S(1)} collective-permute-done((bf16[48,2048]{1,0:T(8,128)(2,1)S(1)}, bf16[48,2048]{1,0:T(8,128)(2,1)S(1)}, u32[]{:S(2)}, u32[]{:S(2)}) %collective-permute-start.35) | collective-permute-done | bytes 196640 | tf_op jit(solution)/shard_map/ppermute | solution.py:245
  151.6 1.9 %shard_map.131 = (bf16[48,2048]{1,0:T(8,128)(2,1)S(1)}, bf16[48,2048]{1,0:T(8,128)(2,1)S(1)}, bf16[48,2048]{1,0:T(8,128)(2,1)S(1)}, bf16[48,2048]{1,0:T(8,128)(2...) custom-call(bf16[48,2048]{1,0:T(8,128)(2,1)S(1)} %get-tuple-element.128.refs_0_.refs_16_, ...), custom_call_target="tpu_custom_call" | custom-call | flops 905969664 | bytes 7176192 | tf_op jit(solution)/shard_map/pallas_call | solution.py:217
  155.6 2.5 %collective-permute-done.44.refs_3_ = bf16[48,2048]{1,0:T(8,128)(2,1)S(1)} collective-permute-done((bf16[48,2048]{1,0:T(8,128)(2,1)S(1)}, bf16[48,2048]{1,0:T(8,128)(2,1)S(1)}, u32[]{:S(2)}, u32[]{:S(2)}) %collective-permute-start.44) | collective-permute-done | bytes 196640 | tf_op jit(solution)/shard_map/ppermute | solution.py:245
  159.2 2.1 %collective-permute-start.59 = (bf16[128,2048]{1,0:T(8,128)(2,1)S(1)}, bf16[128,2048]{1,0:T(8,128)(2,1)S(1)}, u32[]{:S(2)}, u32[]{:S(2)}) collective-permute-start(bf16[128,2048]{1,0:T(8,128)(2,1)S(1)} %shard_map.140), channel_id=1, source_target_pairs={{0,4},{1,5},{2,6},{3,7},{4,8},{5,9},{6,10},{7,11},{8,12},{9,13},{1... | collective-permute-start | bytes 1572872 | tf_op jit(solution)/shard_map/ppermute | solution.py:245
  161.3 6.8 %shard_map.142 = (bf16[2048,384]{1,0:T(8,128)(2,1)}, bf16[2048,384]{1,0:T(8,128)(2,1)}, bf16[384,2048]{1,0:T(8,128)(2,1)}) custom-call(bf16[48,2048]{1,0:T(8,128)(2,1)S(1)} %get-tuple-element.95.refs_0_, bf16[48,2048]{1,0:T(8,128)(2,1)S(1)} %collective-permute-done.refs_1_, bf16[48,2048]{1,0:T(8,128)(2,1)S(1)} %collective-permute-done.1.refs_2_, ...), custom_call_target="tpu_custom_call" | custom-call | flops 3623878656 | bytes 12779520 | tf_op jit(solution)/shard_map/pallas_call | solution.py:217
  170.2 2.3 %shard_map.129 = (bf16[128,2048]{1,0:T(8,128)(2,1)}, f32[8,128]{1,0:T(8,128)S(1)}) custom-call(s32[2]{0:T(128)S(1)} %pad_add_fusion.place, s32[8,128]{1,0:T(8,128)S(1)} %get-tuple-element.187.ids, bf16[128,2176]{1,0:T(8,128)(2,1)S(1)} %pad_maximum_fusion.block, bf16[48,2048]{1,0:T(8,128)(2,1)S(1)} %get-tuple-element.99.refs_0_, ...), custom_call_target="tpu_custom_call" | custom-call | flops 301989888 | bytes 2433032 | tf_op jit(solution)/shard_map/pallas_call | solution.py:217
  174.3 4.7 %collective-permute-done.38.refs_3_ = bf16[48,2048]{1,0:T(8,128)(2,1)S(1)} collective-permute-done((bf16[48,2048]{1,0:T(8,128)(2,1)S(1)}, bf16[48,2048]{1,0:T(8,128)(2,1)S(1)}, u32[]{:S(2)}, u32[]{:S(2)}) %collective-permute-start.38) | collective-permute-done | bytes 196640 | tf_op jit(solution)/shard_map/ppermute | solution.py:245
  179.1 1.8 %shard_map.141 = bf16[128,2048]{1,0:T(8,128)(2,1)} custom-call(s32[2]{0:T(128)S(1)} %pad_add_fusion.place, s32[8,128]{1,0:T(8,128)S(1)} %get-tuple-element.187.ids, bf16[48,2048]{1,0:T(8,128)(2,1)S(1)} %get-tuple-element.134.refs_0_, bf16[48,2048]{1,0:T(8,128)(2,1)S(1)} %collective-permute-done.36.refs_1_, ...), custom_call_target="tpu_custom_call" | custom-call | flops 100663296 | bytes 1839112 | tf_op jit(solution)/shard_map/pallas_call | solution.py:217
  (134 shorter events, 71.7 us)
Async XLA Ops:
  0.7 13.2 %collective-permute-start.9 = (bf16[128,2048]{1,0:T(8,128)(2,1)}, bf16[128,2048]{1,0:T(8,128)(2,1)}, u32[]{:S(2)}, u32[]{:S(2)}) collective-permute-start(bf16[128,2048]{1,0:T(8,128)(2,1)} %block.1), channel_id=1, source_target_pairs={{0,4},{1,5},{2,6},{3,7},{4,8},{5,9},{6,10},{7,11},{8,12},{9,13},{1... | collective-permute-start | bytes 1572872 | tf_op jit(solution)/shard_map/ppermute | solution.py:245
  3.8 21.9 %collective-permute-start.6 = (bf16[128,2176]{1,0:T(8,128)(2,1)S(1)}, bf16[128,2176]{1,0:T(8,128)(2,1)S(1)}, u32[]{:S(2)}, u32[]{:S(2)}) collective-permute-start(bf16[128,2176]{1,0:T(8,128)(2,1)S(1)} %pad_maximum_fusion.block), channel_id=1, source_target_pairs={{0,4},{1,5},{2,6},{3,7},{4,8},{5,9},{6,10},{7,11},{8,12},{9,13},{1... | collective-permute-start | bytes 1671176 | tf_op jit(solution)/shard_map/ppermute | solution.py:245
  7.1 21.2 %collective-permute-start = (bf16[48,2048]{1,0:T(8,128)(2,1)S(1)}, bf16[48,2048]{1,0:T(8,128)(2,1)S(1)}, u32[]{:S(2)}, u32[]{:S(2)}) collective-permute-start(bf16[48,2048]{1,0:T(8,128)(2,1)S(1)} %get-tuple-element.96), channel_id=1, source_target_pairs={{0,1},{1,0},{2,3},{3,2},{4,5},{5,4},{6,7},{7,6},{8,9},{9,8},{10,11... | collective-permute-start | bytes 589832 | tf_op jit(solution)/shard_map/ppermute | solution.py:245
  15.4 13.2 %collective-permute-start.24 = (bf16[48,2048]{1,0:T(8,128)(2,1)S(1)}, bf16[48,2048]{1,0:T(8,128)(2,1)S(1)}, u32[]{:S(2)}, u32[]{:S(2)}) collective-permute-start(bf16[48,2048]{1,0:T(8,128)(2,1)S(1)} %get-tuple-element.120), channel_id=1, source_target_pairs={{0,1},{1,0},{2,3},{3,2},{4,5},{5,4},{6,7},{7,6},{8,9},{9,8},{10,11... | collective-permute-start | bytes 589832 | tf_op jit(solution)/shard_map/ppermute | solution.py:245
  18.1 11.9 %collective-permute-start.25 = (bf16[48,2048]{1,0:T(8,128)(2,1)S(1)}, bf16[48,2048]{1,0:T(8,128)(2,1)S(1)}, u32[]{:S(2)}, u32[]{:S(2)}) collective-permute-start(bf16[48,2048]{1,0:T(8,128)(2,1)S(1)} %get-tuple-element.121), channel_id=1, source_target_pairs={{0,2},{1,3},{2,0},{3,1},{4,6},{5,7},{6,4},{7,5},{8,10},{9,11},{10,... | collective-permute-start | bytes 589832 | tf_op jit(solution)/shard_map/ppermute | solution.py:245
  18.3 13.0 %collective-permute-start.26 = (bf16[48,2048]{1,0:T(8,128)(2,1)S(1)}, bf16[48,2048]{1,0:T(8,128)(2,1)S(1)}, u32[]{:S(2)}, u32[]{:S(2)}) collective-permute-start(bf16[48,2048]{1,0:T(8,128)(2,1)S(1)} %get-tuple-element.122), channel_id=1, source_target_pairs={{0,3},{1,2},{2,1},{3,0},{4,7},{5,6},{6,5},{7,4},{8,11},{9,10},{10,... | collective-permute-start | bytes 589832 | tf_op jit(solution)/shard_map/ppermute | solution.py:245
  30.0 19.9 %collective-permute-start.10 = (bf16[128,2048]{1,0:T(8,128)(2,1)}, bf16[128,2048]{1,0:T(8,128)(2,1)S(1)}, u32[]{:S(2)}, u32[]{:S(2)}) collective-permute-start(bf16[128,2048]{1,0:T(8,128)(2,1)} %collective-permute-done.9.block), channel_id=1, source_target_pairs={{0,4},{1,5},{2,6},{3,7},{4,8},{5,9},{6,10},{7,11},{8,12},{9,13},{1... | collective-permute-start | bytes 1572872 | tf_op jit(solution)/shard_map/ppermute | solution.py:245
  31.3 26.1 %collective-permute-start.7 = (bf16[128,2176]{1,0:T(8,128)(2,1)S(1)}, bf16[128,2176]{1,0:T(8,128)(2,1)S(1)}, u32[]{:S(2)}, u32[]{:S(2)}) collective-permute-start(bf16[128,2176]{1,0:T(8,128)(2,1)S(1)} %collective-permute-done.6.block), channel_id=1, source_target_pairs={{0,4},{1,5},{2,6},{3,7},{4,8},{5,9},{6,10},{7,11},{8,12},{9,13},{1... | collective-permute-start | bytes 1671176 | tf_op jit(solution)/shard_map/ppermute | solution.py:245
  37.2 12.1 %collective-permute-start.2 = (bf16[48,2048]{1,0:T(8,128)(2,1)S(1)}, bf16[48,2048]{1,0:T(8,128)(2,1)S(1)}, u32[]{:S(2)}, u32[]{:S(2)}) collective-permute-start(bf16[48,2048]{1,0:T(8,128)(2,1)S(1)} %get-tuple-element.98), channel_id=1, source_target_pairs={{0,3},{1,2},{2,1},{3,0},{4,7},{5,6},{6,5},{7,4},{8,11},{9,10},{10,... | collective-permute-start | bytes 589832 | tf_op jit(solution)/shard_map/ppermute | solution.py:245
  57.4 12.4 %collective-permute-start.20 = (bf16[48,2048]{1,0:T(8,128)(2,1)S(1)}, bf16[48,2048]{1,0:T(8,128)(2,1)S(1)}, u32[]{:S(2)}, u32[]{:S(2)}) collective-permute-start(bf16[48,2048]{1,0:T(8,128)(2,1)S(1)} %get-tuple-element.114), channel_id=1, source_target_pairs={{0,3},{1,2},{2,1},{3,0},{4,7},{5,6},{6,5},{7,4},{8,11},{9,10},{10,... | collective-permute-start | bytes 589832 | tf_op jit(solution)/shard_map/ppermute | solution.py:245
  57.5 16.6 %collective-permute-start.56 = (bf16[48,2048]{1,0:T(8,128)(2,1)S(1)}, bf16[48,2048]{1,0:T(8,128)(2,1)S(1)}, u32[]{:S(2)}, u32[]{:S(2)}) collective-permute-start(bf16[48,2048]{1,0:T(8,128)(2,1)S(1)} %get-tuple-element.167), channel_id=1, source_target_pairs={{0,3},{1,2},{2,1},{3,0},{4,7},{5,6},{6,5},{7,4},{8,11},{9,10},{10,... | collective-permute-start | bytes 589832 | tf_op jit(solution)/shard_map/ppermute | solution.py:245
  60.2 15.4 %collective-permute-start.45 = (bf16[48,2048]{1,0:T(8,128)(2,1)S(1)}, bf16[48,2048]{1,0:T(8,128)(2,1)S(1)}, u32[]{:S(2)}, u32[]{:S(2)}) collective-permute-start(bf16[48,2048]{1,0:T(8,128)(2,1)S(1)} %get-tuple-element.149), channel_id=1, source_target_pairs={{0,1},{1,0},{2,3},{3,2},{4,5},{5,4},{6,7},{7,6},{8,9},{9,8},{10,11... | collective-permute-start | bytes 589832 | tf_op jit(solution)/shard_map/ppermute | solution.py:245
  61.8 31.1 %collective-permute-start.11 = (bf16[128,2048]{1,0:T(8,128)(2,1)S(1)}, bf16[128,2048]{1,0:T(8,128)(2,1)S(1)}, u32[]{:S(2)}, u32[]{:S(2)}) collective-permute-start(bf16[128,2048]{1,0:T(8,128)(2,1)S(1)} %collective-permute-done.10.block), channel_id=1, source_target_pairs={{0,4},{1,5},{2,6},{3,7},{4,8},{5,9},{6,10},{7,11},{8,12},{9,13},{1... | collective-permute-start | bytes 1572872 | tf_op jit(solution)/shard_map/ppermute | solution.py:245
  64.3 14.2 %collective-permute-start.46 = (bf16[48,2048]{1,0:T(8,128)(2,1)S(1)}, bf16[48,2048]{1,0:T(8,128)(2,1)S(1)}, u32[]{:S(2)}, u32[]{:S(2)}) collective-permute-start(bf16[48,2048]{1,0:T(8,128)(2,1)S(1)} %get-tuple-element.150), channel_id=1, source_target_pairs={{0,2},{1,3},{2,0},{3,1},{4,6},{5,7},{6,4},{7,5},{8,10},{9,11},{10,... | collective-permute-start | bytes 589832 | tf_op jit(solution)/shard_map/ppermute | solution.py:245
  69.8 12.0 %collective-permute-start.47 = (bf16[48,2048]{1,0:T(8,128)(2,1)S(1)}, bf16[48,2048]{1,0:T(8,128)(2,1)S(1)}, u32[]{:S(2)}, u32[]{:S(2)}) collective-permute-start(bf16[48,2048]{1,0:T(8,128)(2,1)S(1)} %get-tuple-element.151), channel_id=1, source_target_pairs={{0,3},{1,2},{2,1},{3,0},{4,7},{5,6},{6,5},{7,4},{8,11},{9,10},{10,... | collective-permute-start | bytes 589832 | tf_op jit(solution)/shard_map/ppermute | solution.py:245
  75.6 22.3 %collective-permute-start.30 = (bf16[128,2176]{1,0:T(8,128)(2,1)S(1)}, bf16[128,2176]{1,0:T(8,128)(2,1)S(1)}, u32[]{:S(2)}, u32[]{:S(2)}) collective-permute-start(bf16[128,2176]{1,0:T(8,128)(2,1)S(1)} %shard_map.126), channel_id=1, source_target_pairs={{0,4},{1,5},{2,6},{3,7},{4,8},{5,9},{6,10},{7,11},{8,12},{9,13},{1... | collective-permute-start | bytes 1671176 | tf_op jit(solution)/shard_map/ppermute | solution.py:245
  78.5 22.5 %collective-permute-start.57 = (bf16[128,2048]{1,0:T(8,128)(2,1)S(1)}, bf16[128,2048]{1,0:T(8,128)(2,1)S(1)}, u32[]{:S(2)}, u32[]{:S(2)}) collective-permute-start(bf16[128,2048]{1,0:T(8,128)(2,1)S(1)} %shard_map.138), channel_id=1, source_target_pairs={{0,4},{1,5},{2,6},{3,7},{4,8},{5,9},{6,10},{7,11},{8,12},{9,13},{1... | collective-permute-start | bytes 1572872 | tf_op jit(solution)/shard_map/ppermute | solution.py:245
  81.8 31.1 %collective-permute-start.8 = (bf16[128,2176]{1,0:T(8,128)(2,1)S(1)}, bf16[128,2176]{1,0:T(8,128)(2,1)S(1)}, u32[]{:S(2)}, u32[]{:S(2)}) collective-permute-start(bf16[128,2176]{1,0:T(8,128)(2,1)S(1)} %collective-permute-done.7.block), channel_id=1, source_target_pairs={{0,4},{1,5},{2,6},{3,7},{4,8},{5,9},{6,10},{7,11},{8,12},{9,13},{1... | collective-permute-start | bytes 1671176 | tf_op jit(solution)/shard_map/ppermute | solution.py:245
  97.4 16.9 %collective-permute-start.12 = (bf16[48,2048]{1,0:T(8,128)(2,1)S(1)}, bf16[48,2048]{1,0:T(8,128)(2,1)S(1)}, u32[]{:S(2)}, u32[]{:S(2)}) collective-permute-start(bf16[48,2048]{1,0:T(8,128)(2,1)S(1)} %get-tuple-element.104), channel_id=1, source_target_pairs={{0,1},{1,0},{2,3},{3,2},{4,5},{5,4},{6,7},{7,6},{8,9},{9,8},{10,11... | collective-permute-start | bytes 589832 | tf_op jit(solution)/shard_map/ppermute | solution.py:245
  98.0 19.6 %collective-permute-start.13 = (bf16[48,2048]{1,0:T(8,128)(2,1)S(1)}, bf16[48,2048]{1,0:T(8,128)(2,1)S(1)}, u32[]{:S(2)}, u32[]{:S(2)}) collective-permute-start(bf16[48,2048]{1,0:T(8,128)(2,1)S(1)} %get-tuple-element.105), channel_id=1, source_target_pairs={{0,2},{1,3},{2,0},{3,1},{4,6},{5,7},{6,4},{7,5},{8,10},{9,11},{10,... | collective-permute-start | bytes 589832 | tf_op jit(solution)/shard_map/ppermute | solution.py:245
  101.0 16.6 %collective-permute-start.14 = (bf16[48,2048]{1,0:T(8,128)(2,1)S(1)}, bf16[48,2048]{1,0:T(8,128)(2,1)S(1)}, u32[]{:S(2)}, u32[]{:S(2)}) collective-permute-start(bf16[48,2048]{1,0:T(8,128)(2,1)S(1)} %get-tuple-element.106), channel_id=1, source_target_pairs={{0,3},{1,2},{2,1},{3,0},{4,7},{5,6},{6,5},{7,4},{8,11},{9,10},{10,... | collective-permute-start | bytes 589832 | tf_op jit(solution)/shard_map/ppermute | solution.py:245
  104.5 32.8 %collective-permute-start.31 = (bf16[128,2176]{1,0:T(8,128)(2,1)S(1)}, bf16[128,2176]{1,0:T(8,128)(2,1)S(1)}, u32[]{:S(2)}, u32[]{:S(2)}) collective-permute-start(bf16[128,2176]{1,0:T(8,128)(2,1)S(1)} %shard_map.127), channel_id=1, source_target_pairs={{0,4},{1,5},{2,6},{3,7},{4,8},{5,9},{6,10},{7,11},{8,12},{9,13},{1... | collective-permute-start | bytes 1671176 | tf_op jit(solution)/shard_map/ppermute | solution.py:245
  125.5 11.8 %collective-permute-start.17 = (bf16[48,2048]{1,0:T(8,128)(2,1)S(1)}, bf16[48,2048]{1,0:T(8,128)(2,1)S(1)}, u32[]{:S(2)}, u32[]{:S(2)}) collective-permute-start(bf16[48,2048]{1,0:T(8,128)(2,1)S(1)} %get-tuple-element.110), channel_id=1, source_target_pairs={{0,3},{1,2},{2,1},{3,0},{4,7},{5,6},{6,5},{7,4},{8,11},{9,10},{10,... | collective-permute-start | bytes 589832 | tf_op jit(solution)/shard_map/ppermute | solution.py:245
  127.4 26.0 %collective-permute-start.58 = (bf16[128,2048]{1,0:T(8,128)(2,1)S(1)}, bf16[128,2048]{1,0:T(8,128)(2,1)S(1)}, u32[]{:S(2)}, u32[]{:S(2)}) collective-permute-start(bf16[128,2048]{1,0:T(8,128)(2,1)S(1)} %shard_map.139), channel_id=1, source_target_pairs={{0,4},{1,5},{2,6},{3,7},{4,8},{5,9},{6,10},{7,11},{8,12},{9,13},{1... | collective-permute-start | bytes 1572872 | tf_op jit(solution)/shard_map/ppermute | solution.py:245
  129.2 12.3 %collective-permute-start.41 = (bf16[48,2048]{1,0:T(8,128)(2,1)S(1)}, bf16[48,2048]{1,0:T(8,128)(2,1)S(1)}, u32[]{:S(2)}, u32[]{:S(2)}) collective-permute-start(bf16[48,2048]{1,0:T(8,128)(2,1)S(1)} %get-tuple-element.141), channel_id=1, source_target_pairs={{0,3},{1,2},{2,1},{3,0},{4,7},{5,6},{6,5},{7,4},{8,11},{9,10},{10,... | collective-permute-start | bytes 589832 | tf_op jit(solution)/shard_map/ppermute | solution.py:245
  132.4 12.6 %collective-permute-start.33 = (bf16[48,2048]{1,0:T(8,128)(2,1)S(1)}, bf16[48,2048]{1,0:T(8,128)(2,1)S(1)}, u32[]{:S(2)}, u32[]{:S(2)}) collective-permute-start(bf16[48,2048]{1,0:T(8,128)(2,1)S(1)} %get-tuple-element.129), channel_id=1, source_target_pairs={{0,1},{1,0},{2,3},{3,2},{4,5},{5,4},{6,7},{7,6},{8,9},{9,8},{10,11... | collective-permute-start | bytes 589832 | tf_op jit(solution)/shard_map/ppermute | solution.py:245
  137.3 12.6 %collective-permute-start.35 = (bf16[48,2048]{1,0:T(8,128)(2,1)S(1)}, bf16[48,2048]{1,0:T(8,128)(2,1)S(1)}, u32[]{:S(2)}, u32[]{:S(2)}) collective-permute-start(bf16[48,2048]{1,0:T(8,128)(2,1)S(1)} %get-tuple-element.131), channel_id=1, source_target_pairs={{0,3},{1,2},{2,1},{3,0},{4,7},{5,6},{6,5},{7,4},{8,11},{9,10},{10,... | collective-permute-start | bytes 589832 | tf_op jit(solution)/shard_map/ppermute | solution.py:245
  141.5 28.7 %collective-permute-start.32 = (bf16[128,2176]{1,0:T(8,128)(2,1)S(1)}, bf16[128,2176]{1,0:T(8,128)(2,1)S(1)}, u32[]{:S(2)}, u32[]{:S(2)}) collective-permute-start(bf16[128,2176]{1,0:T(8,128)(2,1)S(1)} %shard_map.128), channel_id=1, source_target_pairs={{0,4},{1,5},{2,6},{3,7},{4,8},{5,9},{6,10},{7,11},{8,12},{9,13},{1... | collective-permute-start | bytes 1671176 | tf_op jit(solution)/shard_map/ppermute | solution.py:245
  153.4 14.6 %collective-permute-start.3 = (bf16[48,2048]{1,0:T(8,128)(2,1)S(1)}, bf16[48,2048]{1,0:T(8,128)(2,1)S(1)}, u32[]{:S(2)}, u32[]{:S(2)}) collective-permute-start(bf16[48,2048]{1,0:T(8,128)(2,1)S(1)} %get-tuple-element.100), channel_id=1, source_target_pairs={{0,1},{1,0},{2,3},{3,2},{4,5},{5,4},{6,7},{7,6},{8,9},{9,8},{10,11... | collective-permute-start | bytes 589832 | tf_op jit(solution)/shard_map/ppermute | solution.py:245
  153.5 14.7 %collective-permute-start.4 = (bf16[48,2048]{1,0:T(8,128)(2,1)S(1)}, bf16[48,2048]{1,0:T(8,128)(2,1)S(1)}, u32[]{:S(2)}, u32[]{:S(2)}) collective-permute-start(bf16[48,2048]{1,0:T(8,128)(2,1)S(1)} %get-tuple-element.101), channel_id=1, source_target_pairs={{0,2},{1,3},{2,0},{3,1},{4,6},{5,7},{6,4},{7,5},{8,10},{9,11},{10,... | collective-permute-start | bytes 589832 | tf_op jit(solution)/shard_map/ppermute | solution.py:245
  155.2 13.5 %collective-permute-start.5 = (bf16[48,2048]{1,0:T(8,128)(2,1)S(1)}, bf16[48,2048]{1,0:T(8,128)(2,1)S(1)}, u32[]{:S(2)}, u32[]{:S(2)}) collective-permute-start(bf16[48,2048]{1,0:T(8,128)(2,1)S(1)} %get-tuple-element.102), channel_id=1, source_target_pairs={{0,3},{1,2},{2,1},{3,0},{4,7},{5,6},{6,5},{7,4},{8,11},{9,10},{10,... | collective-permute-start | bytes 589832 | tf_op jit(solution)/shard_map/ppermute | solution.py:245
  159.2 19.9 %collective-permute-start.59 = (bf16[128,2048]{1,0:T(8,128)(2,1)S(1)}, bf16[128,2048]{1,0:T(8,128)(2,1)S(1)}, u32[]{:S(2)}, u32[]{:S(2)}) collective-permute-start(bf16[128,2048]{1,0:T(8,128)(2,1)S(1)} %shard_map.140), channel_id=1, source_target_pairs={{0,4},{1,5},{2,6},{3,7},{4,8},{5,9},{6,10},{7,11},{8,12},{9,13},{1... | collective-permute-start | bytes 1572872 | tf_op jit(solution)/shard_map/ppermute | solution.py:245
  (34 other events, 329.0 us)

commit v4 on v3

--- a/solution.py
+++ b/solution.py
@@ -31,24 +31,25 @@
     return [place[0] * plane + jnp.bitwise_xor(place[1], e) for e in range(plane)]
 
 
-def slots_of(place, ids, parts, plane, depth, route_count):
+def block_ids(place, ids, tokens, step, plane, ring):
+    origin = lax.rem(place[0] + (ring - step), ring)
+    start = pl.multiple_of((origin * plane + place[1]) * tokens, tokens)
+    return ids[:, pl.ds(start, tokens)]
+
+
+def slots_of(place, ids, probs, plane, depth, route_count):
     tokens = ids.shape[1]
     rows = lax.broadcasted_iota(jnp.int32, (tokens, tokens), 0)
     cols = lax.broadcasted_iota(jnp.int32, (tokens, tokens), 1)
     before = jnp.where(rows < cols, 1.0, 0.0).astype(BF16)
     route = [ids[k : k + 1] for k in range(route_count)]
-    probs = [
-        parts[k : k + 1]
-        + parts[route_count + k : route_count + k + 1]
-        + parts[2 * route_count + k : 2 * route_count + k + 1]
-        for k in range(route_count)
-    ]
     slot = lax.broadcasted_iota(jnp.int32, (depth, tokens), 0)
     named, weight = [], []
     for eid in expert_ids(place, plane):
         hit = [jnp.where(r == eid, 1.0, 0.0) for r in route]
         named.append(sum(hit))
-        weight.append(sum(h * p for h, p in zip(hit, probs)))
+        if probs is not None:
+            weight.append(sum(h * probs[k : k + 1] for k, h in enumerate(hit)))
     pad = [jnp.zeros((8 - plane % 8, tokens), F32)] if plane % 8 else []
     rank = nn(jnp.concatenate(named + pad, axis=0).astype(BF16), before)
     picks, gates = [], []
@@ -57,18 +58,20 @@
         present = jnp.broadcast_to(named[e], (depth, tokens))
         pick = jnp.where(wanted == slot, present, 0.0)
         picks.append(pick)
-        gates.append(jnp.sum(pick * weight[e], axis=1, keepdims=True))
-    return jnp.concatenate(picks, axis=0), jnp.concatenate(gates, axis=0)
-
-
-def select_kernel(plane, depth, route_count, scaled, place, ids, block, *outs):
+        if probs is not None:
+            gates.append(jnp.sum(pick * weight[e], axis=1, keepdims=True))
+    pick = jnp.concatenate(picks, axis=0)
+    return pick, jnp.concatenate(gates, axis=0) if gates else None
+
+
+def select_kernel(plane, ring, depth, step, scaled, place, ids, block, *outs):
+    route_count = ids.shape[0]
+    ids = block_ids(place, ids, block.shape[0], step, plane, ring)
+    probs = None
+    if scaled:
+        probs, outs = outs[0][...], outs[1:]
     width = outs[0].shape[1]
-    tokens = ids.shape[1]
-    if scaled:
-        parts = block[0:16, width:].astype(F32)
-    else:
-        parts = jnp.zeros((16, tokens), F32)
-    pick, gate = slots_of(place, ids[...], parts, plane, depth, route_count)
+    pick, gate = slots_of(place, ids, probs, plane, depth, route_count)
     chooser = pick.astype(BF16)
     for start in range(0, width, TILE):
         cols = pl.ds(start, TILE)
@@ -125,17 +128,18 @@
             outs[e][:, cols] = dx[e * depth : (e + 1) * depth]
 
 
-def combine_out_kernel(plane, depth, route_count, has_running, is_last, place, ids, block, *refs):
+def combine_out_kernel(plane, ring, depth, step, has_running, place, ids, block, *refs):
+    tokens = block.shape[0]
+    route_count = ids.shape[0]
+    probs, refs = refs[0][...], refs[1:]
     near = refs[:plane]
     refs = refs[plane:]
     running = None
     if has_running:
-        running, refs = refs[0], refs[1:]
+        running, run_gates, refs = refs[0], refs[1], refs[2:]
     width = near[0].shape[1]
-    tokens = ids.shape[1]
-    ids_now = ids[...]
-    parts = block[0:16, width:].astype(F32)
-    pick, gate = slots_of(place, ids_now, parts, plane, depth, route_count)
+    ids_now = block_ids(place, ids, tokens, step, plane, ring)
+    pick, gate = slots_of(place, ids_now, probs, plane, depth, route_count)
     weighted = pick * gate
     weight_high = rounded(weighted)
     high = jnp.transpose(weight_high).astype(BF16)
@@ -158,29 +162,20 @@
         for eid, value in zip(expert_ids(place, plane), found):
             total = total + jnp.where(mine == eid, value, 0.0)
         gates.append(total)
+    pad = jnp.zeros((8 - route_count, tokens), F32)
+    total = jnp.concatenate(gates + [pad], axis=0)
     if has_running:
-        old = running[0:16, width:].astype(F32)
-        for k in range(route_count):
-            for piece in range(3):
-                at = piece * route_count + k
-                gates[k] = gates[k] + old[at : at + 1]
-    if is_last:
-        pad = jnp.zeros((8 - route_count, tokens), F32)
-        refs[1][...] = jnp.concatenate(gates + [pad], axis=0)
-    else:
-        high = [rounded(g) for g in gates]
-        middle = [rounded(g - h) for g, h in zip(gates, high)]
-        low = [g - h - m for g, h, m in zip(gates, high, middle)]
-        pad = jnp.zeros((tokens - 3 * route_count, tokens), F32)
-        refs[0][:, width:] = jnp.concatenate(high + middle + low + [pad], axis=0).astype(BF16)
-
-
-def combine_back_kernel(plane, depth, route_count, has_running, place, ids, *refs):
+        total = total + run_gates[...]
+    refs[1][...] = total
+
+
+def combine_back_kernel(plane, ring, depth, step, has_running, place, ids, *refs):
     near = refs[:plane]
     out = refs[-1]
+    route_count = ids.shape[0]
+    ids = block_ids(place, ids, out.shape[0], step, plane, ring)
     width = near[0].shape[1]
-    parts = jnp.zeros((16, ids.shape[1]), F32)
-    pick, _ = slots_of(place, ids[...], parts, plane, depth, route_count)
+    pick, _ = slots_of(place, ids, None, plane, depth, route_count)
     spread = jnp.transpose(pick).astype(BF16)
     for start in range(0, width, TILE):
         cols = pl.ds(start, TILE)
@@ -188,7 +183,7 @@
         part_dx = nn(spread, dx)
         if has_running:
             part_dx = part_dx + refs[plane][:, cols].astype(F32)
-        out[:, cols] = part_dx.astype(BF16)
+        out[:, cols] = part_dx.astype(out.dtype)
 
 
 def grads_kernel(ring, plane, *refs):
@@ -244,25 +239,14 @@
     def hop(value, pairs):
         return lax.ppermute(value, "owner", pairs)
 
-    id_table = route_ids.reshape(ring, plane, token_rows, route_count)
-    line_ids = lax.dynamic_index_in_dim(id_table, column, 1, keepdims=False)
-    line_ids = jnp.swapaxes(line_ids, 1, 2)
-    line_ids = jnp.pad(line_ids, ((0, 0), (0, 8 - route_count), (0, 0)), constant_values=-1)
-    step_ids = [
-        lax.dynamic_index_in_dim(line_ids, (my_z - s) % ring, 0, keepdims=False) for s in range(ring)
-    ]
-
-    probs = gate_probs.T
-    high = lax.reduce_precision(probs, 8, 7)
-    middle = lax.reduce_precision(probs - high, 8, 7)
-    low = probs - high - middle
-    tail = jnp.concatenate([high, middle, low], axis=0).astype(BF16)
-    tail = jnp.pad(tail, ((0, token_rows - 3 * route_count), (0, 0)))
-    block_x = [tokens]
-    block_c = [jnp.concatenate([cotangent, tail], axis=1)]
+    ids = route_ids.T
+    block_x, block_c = [tokens], [cotangent]
     for _ in range(1, ring):
         block_x.append(hop(block_x[-1], ring_up))
         block_c.append(hop(block_c[-1], ring_up))
+    probs = [jnp.pad(gate_probs.T, ((0, 8 - route_count), (0, 0)))]
+    for _ in range(1, ring):
+        probs.append(hop(probs[-1], ring_up))
 
     def shape(*dims, kind=BF16):
         return jax.ShapeDtypeStruct(dims, kind)
@@ -279,12 +263,12 @@
     got_x, got_c, small = [], [], []
     back_y, back_d = [], []
     for s in range(ring):
-        for blocks, got, scaled in ((block_x, got_x, False), (block_c, got_c, True)):
+        for blocks, got, extra in ((block_x, got_x, []), (block_c, got_c, [probs[s]])):
             picked = call(
-                functools.partial(select_kernel, plane, depth, route_count, scaled),
+                functools.partial(select_kernel, plane, ring, depth, s, bool(extra)),
                 slots,
                 move_flops,
-                [place, step_ids[s], blocks[s]],
+                [place, ids, blocks[s]] + extra,
             )
             got.append(exchange(picked))
         ahead = call(
@@ -303,32 +287,34 @@
         back_y.append(exchange(ahead[:plane]))
         back_d.append(exchange(back[:plane]))
 
-    run_y, run_d = [], []
+    run_y, run_d, run_gates = [], [], []
     for s in list(range(1, ring)) + [0]:
         last = s == 0
         row = shape(token_rows, width)
-        outs_y = [row, shape(8, token_rows, kind=F32)]
-        if not last:
-            outs_y = [shape(token_rows, width + token_rows)]
         done_y = call(
             functools.partial(
-                combine_out_kernel, plane, depth, route_count, bool(run_y), last
+                combine_out_kernel, plane, ring, depth, s, bool(run_y)
             ),
-            outs_y,
+            [row, shape(8, token_rows, kind=F32)],
             3 * move_flops,
-            [place, step_ids[s], block_c[s]] + back_y[s] + run_y,
+            [place, ids, block_c[s], probs[s]] + back_y[s] + run_y + run_gates,
         )
+        before = [] if last else run_d
         done_d = call(
-            functools.partial(combine_back_kernel, plane, depth, route_count, bool(run_d)),
-            [row],
+            functools.partial(combine_back_kernel, plane, ring, depth, s, bool(before)),
+            [shape(token_rows, width, kind=F32) if last else row],
             move_flops,
-            [place, step_ids[s]] + back_d[s] + run_d,
+            [place, ids] + back_d[s] + before,
         )
         if not last:
             run_y = [hop(done_y[0], ring_up)]
             run_d = [hop(done_d[0], ring_up)]
+            run_gates = [hop(done_y[1], ring_up)]
     expert_out, gates = done_y
     grad_tokens = done_d[0]
+    if run_d:
+        grad_tokens = grad_tokens + run_d[0].astype(F32)
+    grad_tokens = grad_tokens.astype(BF16)
 
     grads = call(
         functools.partial(grads_kernel, ring, plane),

time: 184 us -> 204 us (1.11)
  the two profiles are of different devices: /device:TPU:13 before, /device:TPU:0 now
where the time goes in v4:
time: 204 us
  waiting for transfers between devices  111 us (54%)
  starting transfers between devices  42.3 us (21%)
  Pallas kernels  39.2 us (19%)
  local copies, waits for them, and re-layouts  8.81 us (4%)
    ppermute x66, waiting for transfers between devices, hop(): return lax.ppermute(value, 'owner', pairs)  111 us
    ppermute x66, starting transfers between devices, hop(): return lax.ppermute(value, 'owner', pairs)  42.3 us
    pallas_call x25, Pallas kernels, call(): pl.pallas_call(body, out_shape=tuple(outs), in_specs=specs, out_specs=tup...  39.2 us
    unnamed x22, local copies, waits for them, and re-layouts  7.55 us
  transfers between devices with their start and end apart: 66, of which 30 were waited for; matrix products, arithmetic and copies ran while one was open for 1% of the time, Pallas kernels for 19%

profile of v4, /device:TPU:0, one launch (start us, length us, event | category | flops | bytes accessed | tf_op | source)
XLA Modules:
  0.0 203.6 jit_solution(3879669452046737475)
XLA Ops:
  0.6 3.1 %collective-permute-start.12 = (bf16[128,2048]{1,0:T(8,128)(2,1)}, bf16[128,2048]{1,0:T(8,128)(2,1)S(1)}, u32[]{:S(2)}, u32[]{:S(2)}) collective-permute-start(bf16[128,2048]{1,0:T(8,128)(2,1)} %block.3), channel_id=1, source_target_pairs={{0,4},{1,5},{2,6},{3,7},{4,8},{5,9},{6,10},{7,11},{8,12},{9,13},{1... | collective-permute-start | bytes 1572872 | tf_op jit(solution)/shard_map/ppermute | solution.py:240
  16.1 1.7 collective-permute-done.2.refs_3_
  17.8 2.2 %collective-permute-start.41 = (bf16[48,2048]{1,0:T(8,128)(2,1)S(1)}, bf16[48,2048]{1,0:T(8,128)(2,1)S(1)}, u32[]{:S(2)}, u32[]{:S(2)}) collective-permute-start(bf16[48,2048]{1,0:T(8,128)(2,1)S(1)} %get-tuple-element.143), channel_id=1, source_target_pairs={{0,3},{1,2},{2,1},{3,0},{4,7},{5,6},{6,5},{7,4},{8,11},{9,10},{10,... | collective-permute-start | bytes 589832 | tf_op jit(solution)/shard_map/ppermute | solution.py:240
  26.6 1.8 shard_map.131
  32.9 3.8 %collective-permute-done.9.refs_0_.outs_0_ = f32[8,128]{1,0:T(8,128)S(1)} collective-permute-done((f32[8,128]{1,0:T(8,128)S(1)}, f32[8,128]{1,0:T(8,128)S(1)}, u32[]{:S(2)}, u32[]{:S(2)}) %collective-permute-start.9) | collective-permute-done | bytes 4128 | tf_op jit(solution)/shard_map/ppermute | solution.py:240
  36.8 5.4 %collective-permute-done.10.refs_0_.outs_0_ = f32[8,128]{1,0:T(8,128)S(1)} collective-permute-done((f32[8,128]{1,0:T(8,128)S(1)}, f32[8,128]{1,0:T(8,128)S(1)}, u32[]{:S(2)}, u32[]{:S(2)}) %collective-permute-start.10) | collective-permute-done | bytes 4128 | tf_op jit(solution)/shard_map/ppermute | solution.py:240
  42.2 5.4 %collective-permute-done.11.refs_0_.outs_0_ = f32[8,128]{1,0:T(8,128)S(1)} collective-permute-done((f32[8,128]{1,0:T(8,128)S(1)}, f32[8,128]{1,0:T(8,128)S(1)}, u32[]{:S(2)}, u32[]{:S(2)}) %collective-permute-start.11) | collective-permute-done | bytes 4128 | tf_op jit(solution)/shard_map/ppermute | solution.py:240
  51.4 4.0 %collective-permute-done.28.refs_2_.refs_6_ = bf16[48,2048]{1,0:T(8,128)(2,1)S(1)} collective-permute-done((bf16[48,2048]{1,0:T(8,128)(2,1)S(1)}, bf16[48,2048]{1,0:T(8,128)(2,1)S(1)}, u32[]{:S(2)}, u32[]{:S(2)}) %collective-permute-start.28) | collective-permute-done | bytes 196640 | tf_op jit(solution)/shard_map/ppermute | solution.py:240
  56.7 2.2 %collective-permute-start.59 = (bf16[48,2048]{1,0:T(8,128)(2,1)S(1)}, bf16[48,2048]{1,0:T(8,128)(2,1)S(1)}, u32[]{:S(2)}, u32[]{:S(2)}) collective-permute-start(bf16[48,2048]{1,0:T(8,128)(2,1)S(1)} %get-tuple-element.173), channel_id=1, source_target_pairs={{0,3},{1,2},{2,1},{3,0},{4,7},{5,6},{6,5},{7,4},{8,11},{9,10},{10,... | collective-permute-start | bytes 589832 | tf_op jit(solution)/shard_map/ppermute | solution.py:240
  60.4 2.7 %collective-permute-done.58.refs_2_.refs_22_ = bf16[48,2048]{1,0:T(8,128)(2,1)S(1)} collective-permute-done((bf16[48,2048]{1,0:T(8,128)(2,1)S(1)}, bf16[48,2048]{1,0:T(8,128)(2,1)S(1)}, u32[]{:S(2)}, u32[]{:S(2)}) %collective-permute-start.58) | collective-permute-done | bytes 196640 | tf_op jit(solution)/shard_map/ppermute | solution.py:240
  64.3 2.6 %collective-permute-start.31 = (bf16[48,2048]{1,0:T(8,128)(2,1)S(1)}, bf16[48,2048]{1,0:T(8,128)(2,1)S(1)}, u32[]{:S(2)}, u32[]{:S(2)}) collective-permute-start(bf16[48,2048]{1,0:T(8,128)(2,1)S(1)} %get-tuple-element.131), channel_id=1, source_target_pairs={{0,2},{1,3},{2,0},{3,1},{4,6},{5,7},{6,4},{7,5},{8,10},{9,11},{10,... | collective-permute-start | bytes 589832 | tf_op jit(solution)/shard_map/ppermute | solution.py:240
  66.9 1.8 shard_map.138
  68.7 2.0 collective-permute-start.32
  71.0 3.2 %collective-permute-done.31.refs_3_ = bf16[48,2048]{1,0:T(8,128)(2,1)S(1)} collective-permute-done((bf16[48,2048]{1,0:T(8,128)(2,1)S(1)}, bf16[48,2048]{1,0:T(8,128)(2,1)S(1)}, u32[]{:S(2)}, u32[]{:S(2)}) %collective-permute-start.31) | collective-permute-done | bytes 196640 | tf_op jit(solution)/shard_map/ppermute | solution.py:240
  82.8 4.1 %collective-permute-done.62.refs_3_ = bf16[48,2048]{1,0:T(8,128)(2,1)S(1)} collective-permute-done((bf16[48,2048]{1,0:T(8,128)(2,1)S(1)}, bf16[48,2048]{1,0:T(8,128)(2,1)S(1)}, u32[]{:S(2)}, u32[]{:S(2)}) %collective-permute-start.62) | collective-permute-done | bytes 196640 | tf_op jit(solution)/shard_map/ppermute | solution.py:240
  91.5 3.8 %collective-permute-done.23.refs_3_.refs_11_ = bf16[48,2048]{1,0:T(8,128)(2,1)S(1)} collective-permute-done((bf16[48,2048]{1,0:T(8,128)(2,1)S(1)}, bf16[48,2048]{1,0:T(8,128)(2,1)S(1)}, u32[]{:S(2)}, u32[]{:S(2)}) %collective-permute-start.23) | collective-permute-done | bytes 196640 | tf_op jit(solution)/shard_map/ppermute | solution.py:240
  100.0 3.8 %collective-permute-done.53.refs_3_.refs_27_ = bf16[48,2048]{1,0:T(8,128)(2,1)S(1)} collective-permute-done((bf16[48,2048]{1,0:T(8,128)(2,1)S(1)}, bf16[48,2048]{1,0:T(8,128)(2,1)S(1)}, u32[]{:S(2)}, u32[]{:S(2)}) %collective-permute-start.53) | collective-permute-done | bytes 196640 | tf_op jit(solution)/shard_map/ppermute | solution.py:240
  104.9 3.1 %collective-permute-done.25.refs_3_ = bf16[48,2048]{1,0:T(8,128)(2,1)S(1)} collective-permute-done((bf16[48,2048]{1,0:T(8,128)(2,1)S(1)}, bf16[48,2048]{1,0:T(8,128)(2,1)S(1)}, u32[]{:S(2)}, u32[]{:S(2)}) %collective-permute-start.25) | collective-permute-done | bytes 196640 | tf_op jit(solution)/shard_map/ppermute | solution.py:240
  108.0 1.8 shard_map.136
  109.8 2.4 %collective-permute-done.26.refs_4_ = bf16[48,2048]{1,0:T(8,128)(2,1)S(1)} collective-permute-done((bf16[48,2048]{1,0:T(8,128)(2,1)S(1)}, bf16[48,2048]{1,0:T(8,128)(2,1)S(1)}, u32[]{:S(2)}, u32[]{:S(2)}) %collective-permute-start.26) | collective-permute-done | bytes 196640 | tf_op jit(solution)/shard_map/ppermute | solution.py:240
  116.1 5.3 %collective-permute-done.55.refs_2_ = bf16[48,2048]{1,0:T(8,128)(2,1)S(1)} collective-permute-done((bf16[48,2048]{1,0:T(8,128)(2,1)S(1)}, bf16[48,2048]{1,0:T(8,128)(2,1)S(1)}, u32[]{:S(2)}, u32[]{:S(2)}) %collective-permute-start.55) | collective-permute-done | bytes 196640 | tf_op jit(solution)/shard_map/ppermute | solution.py:240
  121.4 2.5 %collective-permute-done.56.refs_3_ = bf16[48,2048]{1,0:T(8,128)(2,1)S(1)} collective-permute-done((bf16[48,2048]{1,0:T(8,128)(2,1)S(1)}, bf16[48,2048]{1,0:T(8,128)(2,1)S(1)}, u32[]{:S(2)}, u32[]{:S(2)}) %collective-permute-start.56) | collective-permute-done | bytes 196640 | tf_op jit(solution)/shard_map/ppermute | solution.py:240
  127.8 17.0 %collective-permute-done.8.block = bf16[128,2048]{1,0:T(8,128)(2,1)S(1)} collective-permute-done((bf16[128,2048]{1,0:T(8,128)(2,1)S(1)}, bf16[128,2048]{1,0:T(8,128)(2,1)S(1)}, u32[]{:S(2)}, u32[]{:S(2)}) %collective-permute-start.8) | collective-permute-done | bytes 524320 | tf_op jit(solution)/shard_map/ppermute | solution.py:240
  149.2 10.5 %collective-permute-done.36.refs_6_ = f32[8,128]{1,0:T(8,128)S(1)} collective-permute-done((f32[8,128]{1,0:T(8,128)S(1)}, f32[8,128]{1,0:T(8,128)S(1)}, u32[]{:S(2)}, u32[]{:S(2)}) %collective-permute-start.36) | collective-permute-done | bytes 4128 | tf_op jit(solution)/shard_map/ppermute | solution.py:240
  162.8 1.8 shard_map.134
  165.0 3.7 %collective-permute-done.19.refs_3_ = bf16[48,2048]{1,0:T(8,128)(2,1)S(1)} collective-permute-done((bf16[48,2048]{1,0:T(8,128)(2,1)S(1)}, bf16[48,2048]{1,0:T(8,128)(2,1)S(1)}, u32[]{:S(2)}, u32[]{:S(2)}) %collective-permute-start.19) | collective-permute-done | bytes 196640 | tf_op jit(solution)/shard_map/ppermute | solution.py:240
  168.7 3.3 %collective-permute-done.20.refs_4_ = bf16[48,2048]{1,0:T(8,128)(2,1)S(1)} collective-permute-done((bf16[48,2048]{1,0:T(8,128)(2,1)S(1)}, bf16[48,2048]{1,0:T(8,128)(2,1)S(1)}, u32[]{:S(2)}, u32[]{:S(2)}) %collective-permute-start.20) | collective-permute-done | bytes 196640 | tf_op jit(solution)/shard_map/ppermute | solution.py:240
  176.6 3.2 %collective-permute-done.49.refs_2_ = bf16[48,2048]{1,0:T(8,128)(2,1)S(1)} collective-permute-done((bf16[48,2048]{1,0:T(8,128)(2,1)S(1)}, bf16[48,2048]{1,0:T(8,128)(2,1)S(1)}, u32[]{:S(2)}, u32[]{:S(2)}) %collective-permute-start.49) | collective-permute-done | bytes 196640 | tf_op jit(solution)/shard_map/ppermute | solution.py:240
  180.3 2.9 %collective-permute-done.50.refs_3_ = bf16[48,2048]{1,0:T(8,128)(2,1)S(1)} collective-permute-done((bf16[48,2048]{1,0:T(8,128)(2,1)S(1)}, bf16[48,2048]{1,0:T(8,128)(2,1)S(1)}, u32[]{:S(2)}, u32[]{:S(2)}) %collective-permute-start.50) | collective-permute-done | bytes 196640 | tf_op jit(solution)/shard_map/ppermute | solution.py:240
  185.6 6.8 %shard_map.142 = (bf16[2048,384]{1,0:T(8,128)(2,1)}, bf16[2048,384]{1,0:T(8,128)(2,1)}, bf16[384,2048]{1,0:T(8,128)(2,1)}) custom-call(bf16[48,2048]{1,0:T(8,128)(2,1)S(1)} %get-tuple-element.101.refs_0_, bf16[48,2048]{1,0:T(8,128)(2,1)S(1)} %collective-permute-done.refs_1_, bf16[48,2048]{1,0:T(8,128)(2,1)S(1)} %collective-permute-done.1.refs_2_, ...), custom_call_target="tpu_custom_call" | custom-call | flops 3623878656 | bytes 12779520 | tf_op jit(solution)/shard_map/pallas_call | solution.py:212
  192.4 2.3 %shard_map.129 = (bf16[128,2048]{1,0:T(8,128)(2,1)}, f32[8,128]{1,0:T(8,128)S(1)}) custom-call(s32[2]{0:T(128)S(1)} %pad_add_fusion.place, s32[3,2048]{1,0:T(4,128)S(1)} %bitcast.51, bf16[128,2048]{1,0:T(8,128)(2,1)S(1)} %copy-done.9, f32[8,128]{1,0:T(8,128)S(1)} %pad.4.refs_0_.outs_0_, bf16[48,2048]{1,0:T(8,128)(2,1)S(1)} %get-tuple-element.105.refs_1_, ...), custom_call_target="tpu_custom_call" | custom-call | flops 301989888 | bytes 2396168 | tf_op jit(solution)/shard_map/pallas_call | solution.py:212
  195.3 7.4 %collective-permute-done.65 = bf16[128,2048]{1,0:T(8,128)(2,1)S(1)} collective-permute-done((bf16[128,2048]{1,0:T(8,128)(2,1)S(1)}, bf16[128,2048]{1,0:T(8,128)(2,1)S(1)}, u32[]{:S(2)}, u32[]{:S(2)}) %collective-permute-start.65) | collective-permute-done | bytes 524320 | tf_op jit(solution)/shard_map/ppermute | solution.py:240
  (151 shorter events, 75.0 us)
Async XLA Ops:
  0.6 29.6 %collective-permute-start.12 = (bf16[128,2048]{1,0:T(8,128)(2,1)}, bf16[128,2048]{1,0:T(8,128)(2,1)S(1)}, u32[]{:S(2)}, u32[]{:S(2)}) collective-permute-start(bf16[128,2048]{1,0:T(8,128)(2,1)} %block.3), channel_id=1, source_target_pairs={{0,4},{1,5},{2,6},{3,7},{4,8},{5,9},{6,10},{7,11},{8,12},{9,13},{1... | collective-permute-start | bytes 1572872 | tf_op jit(solution)/shard_map/ppermute | solution.py:240
  8.6 39.5 %collective-permute-start.6 = (bf16[128,2048]{1,0:T(8,128)(2,1)}, bf16[128,2048]{1,0:T(8,128)(2,1)S(1)}, u32[]{:S(2)}, u32[]{:S(2)}) collective-permute-start(bf16[128,2048]{1,0:T(8,128)(2,1)} %block.5), channel_id=1, source_target_pairs={{0,4},{1,5},{2,6},{3,7},{4,8},{5,9},{6,10},{7,11},{8,12},{9,13},{1... | collective-permute-start | bytes 1572872 | tf_op jit(solution)/shard_map/ppermute | solution.py:240
  12.9 12.8 %collective-permute-start.39 = (bf16[48,2048]{1,0:T(8,128)(2,1)S(1)}, bf16[48,2048]{1,0:T(8,128)(2,1)S(1)}, u32[]{:S(2)}, u32[]{:S(2)}) collective-permute-start(bf16[48,2048]{1,0:T(8,128)(2,1)S(1)} %get-tuple-element.141), channel_id=1, source_target_pairs={{0,1},{1,0},{2,3},{3,2},{4,5},{5,4},{6,7},{7,6},{8,9},{9,8},{10,11... | collective-permute-start | bytes 589832 | tf_op jit(solution)/shard_map/ppermute | solution.py:240
  28.4 20.7 %collective-permute-start.42 = (bf16[48,2048]{1,0:T(8,128)(2,1)S(1)}, bf16[48,2048]{1,0:T(8,128)(2,1)S(1)}, u32[]{:S(2)}, u32[]{:S(2)}) collective-permute-start(bf16[48,2048]{1,0:T(8,128)(2,1)S(1)} %get-tuple-element.147), channel_id=1, source_target_pairs={{0,1},{1,0},{2,3},{3,2},{4,5},{5,4},{6,7},{7,6},{8,9},{9,8},{10,11... | collective-permute-start | bytes 589832 | tf_op jit(solution)/shard_map/ppermute | solution.py:240
  28.7 22.1 %collective-permute-start.43 = (bf16[48,2048]{1,0:T(8,128)(2,1)S(1)}, bf16[48,2048]{1,0:T(8,128)(2,1)S(1)}, u32[]{:S(2)}, u32[]{:S(2)}) collective-permute-start(bf16[48,2048]{1,0:T(8,128)(2,1)S(1)} %get-tuple-element.148), channel_id=1, source_target_pairs={{0,2},{1,3},{2,0},{3,1},{4,6},{5,7},{6,4},{7,5},{8,10},{9,11},{10,... | collective-permute-start | bytes 589832 | tf_op jit(solution)/shard_map/ppermute | solution.py:240
  31.2 20.1 %collective-permute-start.27 = (bf16[48,2048]{1,0:T(8,128)(2,1)S(1)}, bf16[48,2048]{1,0:T(8,128)(2,1)S(1)}, u32[]{:S(2)}, u32[]{:S(2)}) collective-permute-start(bf16[48,2048]{1,0:T(8,128)(2,1)S(1)} %get-tuple-element.126), channel_id=1, source_target_pairs={{0,1},{1,0},{2,3},{3,2},{4,5},{5,4},{6,7},{7,6},{8,9},{9,8},{10,11... | collective-permute-start | bytes 589832 | tf_op jit(solution)/shard_map/ppermute | solution.py:240
  50.8 12.3 %collective-permute-start.58 = (bf16[48,2048]{1,0:T(8,128)(2,1)S(1)}, bf16[48,2048]{1,0:T(8,128)(2,1)S(1)}, u32[]{:S(2)}, u32[]{:S(2)}) collective-permute-start(bf16[48,2048]{1,0:T(8,128)(2,1)S(1)} %get-tuple-element.172), channel_id=1, source_target_pairs={{0,2},{1,3},{2,0},{3,1},{4,6},{5,7},{6,4},{7,5},{8,10},{9,11},{10,... | collective-permute-start | bytes 589832 | tf_op jit(solution)/shard_map/ppermute | solution.py:240
  51.4 23.6 %collective-permute-start.13 = (bf16[128,2048]{1,0:T(8,128)(2,1)S(1)}, bf16[128,2048]{1,0:T(8,128)(2,1)S(1)}, u32[]{:S(2)}, u32[]{:S(2)}) collective-permute-start(bf16[128,2048]{1,0:T(8,128)(2,1)S(1)} %collective-permute-done.12.block), channel_id=1, source_target_pairs={{0,4},{1,5},{2,6},{3,7},{4,8},{5,9},{6,10},{7,11},{8,12},{9,13},{1... | collective-permute-start | bytes 1572872 | tf_op jit(solution)/shard_map/ppermute | solution.py:240
  55.4 24.0 %collective-permute-start.7 = (bf16[128,2048]{1,0:T(8,128)(2,1)S(1)}, bf16[128,2048]{1,0:T(8,128)(2,1)S(1)}, u32[]{:S(2)}, u32[]{:S(2)}) collective-permute-start(bf16[128,2048]{1,0:T(8,128)(2,1)S(1)} %collective-permute-done.6.block), channel_id=1, source_target_pairs={{0,4},{1,5},{2,6},{3,7},{4,8},{5,9},{6,10},{7,11},{8,12},{9,13},{1... | collective-permute-start | bytes 1572872 | tf_op jit(solution)/shard_map/ppermute | solution.py:240
  78.6 12.5 %collective-permute-start.22 = (bf16[48,2048]{1,0:T(8,128)(2,1)S(1)}, bf16[48,2048]{1,0:T(8,128)(2,1)S(1)}, u32[]{:S(2)}, u32[]{:S(2)}) collective-permute-start(bf16[48,2048]{1,0:T(8,128)(2,1)S(1)} %get-tuple-element.119), channel_id=1, source_target_pairs={{0,2},{1,3},{2,0},{3,1},{4,6},{5,7},{6,4},{7,5},{8,10},{9,11},{10,... | collective-permute-start | bytes 589832 | tf_op jit(solution)/shard_map/ppermute | solution.py:240
  79.4 16.0 %collective-permute-start.23 = (bf16[48,2048]{1,0:T(8,128)(2,1)S(1)}, bf16[48,2048]{1,0:T(8,128)(2,1)S(1)}, u32[]{:S(2)}, u32[]{:S(2)}) collective-permute-start(bf16[48,2048]{1,0:T(8,128)(2,1)S(1)} %get-tuple-element.120), channel_id=1, source_target_pairs={{0,3},{1,2},{2,1},{3,0},{4,7},{5,6},{6,5},{7,4},{8,11},{9,10},{10,... | collective-permute-start | bytes 589832 | tf_op jit(solution)/shard_map/ppermute | solution.py:240
  82.7 14.3 %collective-permute-start.51 = (bf16[48,2048]{1,0:T(8,128)(2,1)S(1)}, bf16[48,2048]{1,0:T(8,128)(2,1)S(1)}, u32[]{:S(2)}, u32[]{:S(2)}) collective-permute-start(bf16[48,2048]{1,0:T(8,128)(2,1)S(1)} %get-tuple-element.161), channel_id=1, source_target_pairs={{0,1},{1,0},{2,3},{3,2},{4,5},{5,4},{6,7},{7,6},{8,9},{9,8},{10,11... | collective-permute-start | bytes 589832 | tf_op jit(solution)/shard_map/ppermute | solution.py:240
  86.9 12.6 %collective-permute-start.52 = (bf16[48,2048]{1,0:T(8,128)(2,1)S(1)}, bf16[48,2048]{1,0:T(8,128)(2,1)S(1)}, u32[]{:S(2)}, u32[]{:S(2)}) collective-permute-start(bf16[48,2048]{1,0:T(8,128)(2,1)S(1)} %get-tuple-element.162), channel_id=1, source_target_pairs={{0,2},{1,3},{2,0},{3,1},{4,6},{5,7},{6,4},{7,5},{8,10},{9,11},{10,... | collective-permute-start | bytes 589832 | tf_op jit(solution)/shard_map/ppermute | solution.py:240
  91.1 12.7 %collective-permute-start.53 = (bf16[48,2048]{1,0:T(8,128)(2,1)S(1)}, bf16[48,2048]{1,0:T(8,128)(2,1)S(1)}, u32[]{:S(2)}, u32[]{:S(2)}) collective-permute-start(bf16[48,2048]{1,0:T(8,128)(2,1)S(1)} %get-tuple-element.163), channel_id=1, source_target_pairs={{0,3},{1,2},{2,1},{3,0},{4,7},{5,6},{6,5},{7,4},{8,11},{9,10},{10,... | collective-permute-start | bytes 589832 | tf_op jit(solution)/shard_map/ppermute | solution.py:240
  95.3 19.1 %collective-permute-start.14 = (bf16[128,2048]{1,0:T(8,128)(2,1)S(1)}, bf16[128,2048]{1,0:T(8,128)(2,1)S(1)}, u32[]{:S(2)}, u32[]{:S(2)}) collective-permute-start(bf16[128,2048]{1,0:T(8,128)(2,1)S(1)} %collective-permute-done.13.block), channel_id=1, source_target_pairs={{0,4},{1,5},{2,6},{3,7},{4,8},{5,9},{6,10},{7,11},{8,12},{9,13},{1... | collective-permute-start | bytes 1572872 | tf_op jit(solution)/shard_map/ppermute | solution.py:240
  99.5 12.7 %collective-permute-start.26 = (bf16[48,2048]{1,0:T(8,128)(2,1)S(1)}, bf16[48,2048]{1,0:T(8,128)(2,1)S(1)}, u32[]{:S(2)}, u32[]{:S(2)}) collective-permute-start(bf16[48,2048]{1,0:T(8,128)(2,1)S(1)} %get-tuple-element.124), channel_id=1, source_target_pairs={{0,3},{1,2},{2,1},{3,0},{4,7},{5,6},{6,5},{7,4},{8,11},{9,10},{10,... | collective-permute-start | bytes 589832 | tf_op jit(solution)/shard_map/ppermute | solution.py:240
  103.8 21.0 %collective-permute-start.33 = (bf16[128,2048]{1,0:T(8,128)(2,1)S(1)}, bf16[128,2048]{1,0:T(8,128)(2,1)S(1)}, u32[]{:S(2)}, u32[]{:S(2)}) collective-permute-start(bf16[128,2048]{1,0:T(8,128)(2,1)S(1)} %get-tuple-element.133), channel_id=1, source_target_pairs={{0,4},{1,5},{2,6},{3,7},{4,8},{5,9},{6,10},{7,11},{8,12},{9,13},{1... | collective-permute-start | bytes 1572872 | tf_op jit(solution)/shard_map/ppermute | solution.py:240
  104.8 41.0 %collective-permute-start.63 = (bf16[128,2048]{1,0:T(8,128)(2,1)S(1)}, bf16[128,2048]{1,0:T(8,128)(2,1)S(1)}, u32[]{:S(2)}, u32[]{:S(2)}) collective-permute-start(bf16[128,2048]{1,0:T(8,128)(2,1)S(1)} %shard_map.139), channel_id=1, source_target_pairs={{0,4},{1,5},{2,6},{3,7},{4,8},{5,9},{6,10},{7,11},{8,12},{9,13},{1... | collective-permute-start | bytes 1572872 | tf_op jit(solution)/shard_map/ppermute | solution.py:240
  108.0 36.8 %collective-permute-start.8 = (bf16[128,2048]{1,0:T(8,128)(2,1)S(1)}, bf16[128,2048]{1,0:T(8,128)(2,1)S(1)}, u32[]{:S(2)}, u32[]{:S(2)}) collective-permute-start(bf16[128,2048]{1,0:T(8,128)(2,1)S(1)} %collective-permute-done.7.block), channel_id=1, source_target_pairs={{0,4},{1,5},{2,6},{3,7},{4,8},{5,9},{6,10},{7,11},{8,12},{9,13},{1... | collective-permute-start | bytes 1572872 | tf_op jit(solution)/shard_map/ppermute | solution.py:240
  121.4 24.5 %collective-permute-start.15 = (bf16[48,2048]{1,0:T(8,128)(2,1)S(1)}, bf16[48,2048]{1,0:T(8,128)(2,1)S(1)}, u32[]{:S(2)}, u32[]{:S(2)}) collective-permute-start(bf16[48,2048]{1,0:T(8,128)(2,1)S(1)} %get-tuple-element.110), channel_id=1, source_target_pairs={{0,1},{1,0},{2,3},{3,2},{4,5},{5,4},{6,7},{7,6},{8,9},{9,8},{10,11... | collective-permute-start | bytes 589832 | tf_op jit(solution)/shard_map/ppermute | solution.py:240
  123.9 22.7 %collective-permute-start.16 = (bf16[48,2048]{1,0:T(8,128)(2,1)S(1)}, bf16[48,2048]{1,0:T(8,128)(2,1)S(1)}, u32[]{:S(2)}, u32[]{:S(2)}) collective-permute-start(bf16[48,2048]{1,0:T(8,128)(2,1)S(1)} %get-tuple-element.111), channel_id=1, source_target_pairs={{0,2},{1,3},{2,0},{3,1},{4,6},{5,7},{6,4},{7,5},{8,10},{9,11},{10,... | collective-permute-start | bytes 589832 | tf_op jit(solution)/shard_map/ppermute | solution.py:240
  124.7 23.0 %collective-permute-start.17 = (bf16[48,2048]{1,0:T(8,128)(2,1)S(1)}, bf16[48,2048]{1,0:T(8,128)(2,1)S(1)}, u32[]{:S(2)}, u32[]{:S(2)}) collective-permute-start(bf16[48,2048]{1,0:T(8,128)(2,1)S(1)} %get-tuple-element.112), channel_id=1, source_target_pairs={{0,3},{1,2},{2,1},{3,0},{4,7},{5,6},{6,5},{7,4},{8,11},{9,10},{10,... | collective-permute-start | bytes 589832 | tf_op jit(solution)/shard_map/ppermute | solution.py:240
  144.8 27.8 %collective-permute-start.35 = (bf16[128,2048]{1,0:T(8,128)(2,1)S(1)}, bf16[128,2048]{1,0:T(8,128)(2,1)S(1)}, u32[]{:S(2)}, u32[]{:S(2)}) collective-permute-start(bf16[128,2048]{1,0:T(8,128)(2,1)S(1)} %get-tuple-element.135), channel_id=1, source_target_pairs={{0,4},{1,5},{2,6},{3,7},{4,8},{5,9},{6,10},{7,11},{8,12},{9,13},{1... | collective-permute-start | bytes 1572872 | tf_op jit(solution)/shard_map/ppermute | solution.py:240
  145.8 14.9 %collective-permute-start.45 = (bf16[48,2048]{1,0:T(8,128)(2,1)S(1)}, bf16[48,2048]{1,0:T(8,128)(2,1)S(1)}, u32[]{:S(2)}, u32[]{:S(2)}) collective-permute-start(bf16[48,2048]{1,0:T(8,128)(2,1)S(1)} %get-tuple-element.151), channel_id=1, source_target_pairs={{0,1},{1,0},{2,3},{3,2},{4,5},{5,4},{6,7},{7,6},{8,9},{9,8},{10,11... | collective-permute-start | bytes 589832 | tf_op jit(solution)/shard_map/ppermute | solution.py:240
  145.9 14.9 %collective-permute-start.46 = (bf16[48,2048]{1,0:T(8,128)(2,1)S(1)}, bf16[48,2048]{1,0:T(8,128)(2,1)S(1)}, u32[]{:S(2)}, u32[]{:S(2)}) collective-permute-start(bf16[48,2048]{1,0:T(8,128)(2,1)S(1)} %get-tuple-element.152), channel_id=1, source_target_pairs={{0,2},{1,3},{2,0},{3,1},{4,6},{5,7},{6,4},{7,5},{8,10},{9,11},{10,... | collective-permute-start | bytes 589832 | tf_op jit(solution)/shard_map/ppermute | solution.py:240
  146.7 14.8 %collective-permute-start.47 = (bf16[48,2048]{1,0:T(8,128)(2,1)S(1)}, bf16[48,2048]{1,0:T(8,128)(2,1)S(1)}, u32[]{:S(2)}, u32[]{:S(2)}) collective-permute-start(bf16[48,2048]{1,0:T(8,128)(2,1)S(1)} %get-tuple-element.153), channel_id=1, source_target_pairs={{0,3},{1,2},{2,1},{3,0},{4,7},{5,6},{6,5},{7,4},{8,11},{9,10},{10,... | collective-permute-start | bytes 589832 | tf_op jit(solution)/shard_map/ppermute | solution.py:240
  147.7 12.0 %collective-permute-start.36 = (f32[8,128]{1,0:T(8,128)S(1)}, f32[8,128]{1,0:T(8,128)S(1)}, u32[]{:S(2)}, u32[]{:S(2)}) collective-permute-start(f32[8,128]{1,0:T(8,128)S(1)} %get-tuple-element.136), channel_id=1, source_target_pairs={{0,4},{1,5},{2,6},{3,7},{4,8},{5,9},{6,10},{7,11},{8,12},{9,13},{1... | collective-permute-start | bytes 12296 | tf_op jit(solution)/shard_map/ppermute | solution.py:240
  160.8 23.5 %collective-permute-start.64 = (bf16[128,2048]{1,0:T(8,128)(2,1)S(1)}, bf16[128,2048]{1,0:T(8,128)(2,1)S(1)}, u32[]{:S(2)}, u32[]{:S(2)}) collective-permute-start(bf16[128,2048]{1,0:T(8,128)(2,1)S(1)} %shard_map.140), channel_id=1, source_target_pairs={{0,4},{1,5},{2,6},{3,7},{4,8},{5,9},{6,10},{7,11},{8,12},{9,13},{1... | collective-permute-start | bytes 1572872 | tf_op jit(solution)/shard_map/ppermute | solution.py:240
  168.7 16.6 %collective-permute-start.3 = (bf16[48,2048]{1,0:T(8,128)(2,1)S(1)}, bf16[48,2048]{1,0:T(8,128)(2,1)S(1)}, u32[]{:S(2)}, u32[]{:S(2)}) collective-permute-start(bf16[48,2048]{1,0:T(8,128)(2,1)S(1)} %get-tuple-element.106), channel_id=1, source_target_pairs={{0,1},{1,0},{2,3},{3,2},{4,5},{5,4},{6,7},{7,6},{8,9},{9,8},{10,11... | collective-permute-start | bytes 589832 | tf_op jit(solution)/shard_map/ppermute | solution.py:240
  175.5 16.9 %collective-permute-start.37 = (bf16[128,2048]{1,0:T(8,128)(2,1)S(1)}, bf16[128,2048]{1,0:T(8,128)(2,1)S(1)}, u32[]{:S(2)}, u32[]{:S(2)}) collective-permute-start(bf16[128,2048]{1,0:T(8,128)(2,1)S(1)} %get-tuple-element.137), channel_id=1, source_target_pairs={{0,4},{1,5},{2,6},{3,7},{4,8},{5,9},{6,10},{7,11},{8,12},{9,13},{1... | collective-permute-start | bytes 1572872 | tf_op jit(solution)/shard_map/ppermute | solution.py:240
  179.7 12.6 %collective-permute-start.4 = (bf16[48,2048]{1,0:T(8,128)(2,1)S(1)}, bf16[48,2048]{1,0:T(8,128)(2,1)S(1)}, u32[]{:S(2)}, u32[]{:S(2)}) collective-permute-start(bf16[48,2048]{1,0:T(8,128)(2,1)S(1)} %get-tuple-element.107), channel_id=1, source_target_pairs={{0,2},{1,3},{2,0},{3,1},{4,6},{5,7},{6,4},{7,5},{8,10},{9,11},{10,... | collective-permute-start | bytes 589832 | tf_op jit(solution)/shard_map/ppermute | solution.py:240
  185.3 17.4 %collective-permute-start.65 = (bf16[128,2048]{1,0:T(8,128)(2,1)S(1)}, bf16[128,2048]{1,0:T(8,128)(2,1)S(1)}, u32[]{:S(2)}, u32[]{:S(2)}) collective-permute-start(bf16[128,2048]{1,0:T(8,128)(2,1)S(1)} %shard_map.141), channel_id=1, source_target_pairs={{0,4},{1,5},{2,6},{3,7},{4,8},{5,9},{6,10},{7,11},{8,12},{9,13},{1... | collective-permute-start | bytes 1572872 | tf_op jit(solution)/shard_map/ppermute | solution.py:240
  (45 other events, 307.8 us)

commit v5 on v4

--- a/solution.py
+++ b/solution.py
@@ -86,8 +86,9 @@
 def forward_kernel(plane, *refs):
     rows = refs[:plane]
     gate_w, up_w, down_w = refs[plane : plane + 3]
-    outs = refs[plane + 3 : 2 * plane + 3]
-    hidden_out, gate_out, up_out = refs[2 * plane + 3 :]
+    outs = refs[plane + 3 : -3]
+    hidden_out, gate_out, up_out = refs[-3:]
+    span = outs[0].shape[1]
     width = gate_w.shape[0]
     depth = rows[0].shape[0]
     row_x = jnp.concatenate([r[...] for r in rows], axis=0)
@@ -101,8 +102,9 @@
     for start in range(0, width, TILE):
         cols = pl.ds(start, TILE)
         y = nn(hidden, down_w[:, cols]).astype(BF16)
+        part = outs[start // span * plane :]
         for e in range(plane):
-            outs[e][:, cols] = y[e * depth : (e + 1) * depth]
+            part[e][:, pl.ds(start % span, TILE)] = y[e * depth : (e + 1) * depth]
 
 
 def backward_kernel(plane, *refs):
@@ -128,62 +130,60 @@
             outs[e][:, cols] = dx[e * depth : (e + 1) * depth]
 
 
-def combine_out_kernel(plane, ring, depth, step, has_running, place, ids, block, *refs):
+def maps_kernel(plane, ring, depth, step, place, ids, probs, high, low, spread, picked):
+    route_count = ids.shape[0]
+    ids = block_ids(place, ids, probs.shape[1], step, plane, ring)
+    pick, gate = slots_of(place, ids, probs[...], plane, depth, route_count)
+    weighted = pick * gate
+    weight_high = rounded(weighted)
+    high[...] = jnp.transpose(weight_high).astype(BF16)
+    low[...] = jnp.transpose(weighted - weight_high).astype(BF16)
+    spread[...] = jnp.transpose(pick).astype(BF16)
+    picked[...] = pick
+
+
+def combine_kernel(plane, maps, runs, offset, *refs):
+    weights = [r[...] for r in refs[:maps]]
+    near = refs[maps : maps + plane]
+    running = refs[maps + plane : maps + plane + runs]
+    out = refs[-1]
+    for start in range(0, near[0].shape[1], TILE):
+        cols = pl.ds(start, TILE)
+        rows = jnp.concatenate([n[:, cols] for n in near], axis=0)
+        part = sum(nn(w, rows) for w in weights)
+        if runs:
+            span = running[0].shape[1]
+            at = offset + start
+            part = part + running[at // span][:, pl.ds(at % span, TILE)].astype(F32)
+        out[:, cols] = part.astype(out.dtype)
+
+
+def gates_kernel(plane, ring, depth, step, has_running, place, ids, picked, block, *refs):
+    near = refs[: len(refs) - 1 - has_running]
+    span = near[0].shape[1]
+    out = refs[-1]
     tokens = block.shape[0]
     route_count = ids.shape[0]
-    probs, refs = refs[0][...], refs[1:]
-    near = refs[:plane]
-    refs = refs[plane:]
-    running = None
-    if has_running:
-        running, run_gates, refs = refs[0], refs[1], refs[2:]
-    width = near[0].shape[1]
-    ids_now = block_ids(place, ids, tokens, step, plane, ring)
-    pick, gate = slots_of(place, ids_now, probs, plane, depth, route_count)
-    weighted = pick * gate
-    weight_high = rounded(weighted)
-    high = jnp.transpose(weight_high).astype(BF16)
-    low = jnp.transpose(weighted - weight_high).astype(BF16)
+    ids = block_ids(place, ids, tokens, step, plane, ring)
     dots = jnp.zeros((plane * depth, tokens), F32)
-    for start in range(0, width, TILE):
-        cols = pl.ds(start, TILE)
-        y = jnp.concatenate([n[:, cols] for n in near], axis=0)
-        part_y = nn(high, y) + nn(low, y)
-        dots = dots + nt(y, block[:, cols])
-        if has_running:
-            part_y = part_y + running[:, cols].astype(F32)
-        refs[0][:, cols] = part_y.astype(BF16)
-    dots = pick * dots
+    for start in range(0, block.shape[1], TILE):
+        cols = pl.ds(start % span, TILE)
+        part = near[start // span * plane :][:plane]
+        rows = jnp.concatenate([n[:, cols] for n in part], axis=0)
+        dots = dots + nt(rows, block[:, pl.ds(start, TILE)])
+    dots = picked[...] * dots
     found = [jnp.sum(dots[e * depth : (e + 1) * depth], axis=0, keepdims=True) for e in range(plane)]
     gates = []
     for k in range(route_count):
-        mine = ids_now[k : k + 1]
         total = jnp.zeros((1, tokens), F32)
         for eid, value in zip(expert_ids(place, plane), found):
-            total = total + jnp.where(mine == eid, value, 0.0)
+            total = total + jnp.where(ids[k : k + 1] == eid, value, 0.0)
         gates.append(total)
     pad = jnp.zeros((8 - route_count, tokens), F32)
     total = jnp.concatenate(gates + [pad], axis=0)
     if has_running:
-        total = total + run_gates[...]
-    refs[1][...] = total
-
-
-def combine_back_kernel(plane, ring, depth, step, has_running, place, ids, *refs):
-    near = refs[:plane]
-    out = refs[-1]
-    route_count = ids.shape[0]
-    ids = block_ids(place, ids, out.shape[0], step, plane, ring)
-    width = near[0].shape[1]
-    pick, _ = slots_of(place, ids, None, plane, depth, route_count)
-    spread = jnp.transpose(pick).astype(BF16)
-    for start in range(0, width, TILE):
-        cols = pl.ds(start, TILE)
-        dx = jnp.concatenate([n[:, cols] for n in near], axis=0)
-        part_dx = nn(spread, dx)
-        if has_running:
-            part_dx = part_dx + refs[plane][:, cols].astype(F32)
-        out[:, cols] = part_dx.astype(out.dtype)
+        total = total + refs[-2][...]
+    out[...] = total
 
 
 def grads_kernel(ring, plane, *refs):
@@ -271,9 +271,11 @@
                 [place, ids, blocks[s]] + extra,
             )
             got.append(exchange(picked))
+        parts = 2 if ring > 1 and s == ring - 1 and width % (2 * TILE) == 0 else 1
+        count = plane * parts
         ahead = call(
             functools.partial(forward_kernel, plane),
-            slots + [shape(rows, hidden_width)] + [shape(rows, hidden_width, kind=F32)] * 2,
+            [shape(depth, width // parts)] * count + [shape(rows, hidden_width)] + [shape(rows, hidden_width, kind=F32)] * 2,
             3 * dense_flops,
             got_x[s] + weights,
         )
@@ -281,36 +283,49 @@
             functools.partial(backward_kernel, plane),
             slots + [shape(rows, hidden_width)] * 2,
             3 * dense_flops,
-            got_c[s] + list(ahead[plane + 1 :]) + weights,
-        )
-        small += [ahead[plane], back[plane], back[plane + 1]]
-        back_y.append(exchange(ahead[:plane]))
+            got_c[s] + list(ahead[count + 1 :]) + weights,
+        )
+        small += [ahead[count], back[plane], back[plane + 1]]
+        back_y.append([exchange(ahead[p * plane : (p + 1) * plane]) for p in range(parts)])
         back_d.append(exchange(back[:plane]))
 
     run_y, run_d, run_gates = [], [], []
     for s in list(range(1, ring)) + [0]:
         last = s == 0
-        row = shape(token_rows, width)
-        done_y = call(
-            functools.partial(
-                combine_out_kernel, plane, ring, depth, s, bool(run_y)
-            ),
-            [row, shape(8, token_rows, kind=F32)],
-            3 * move_flops,
-            [place, ids, block_c[s], probs[s]] + back_y[s] + run_y + run_gates,
+        high, low, spread, picked = call(
+            functools.partial(maps_kernel, plane, ring, depth, s),
+            [shape(token_rows, rows)] * 3 + [shape(rows, token_rows, kind=F32)],
+            2 * 8 * token_rows * token_rows,
+            [place, ids, probs[s]],
+        )
+        span = width // len(back_y[s])
+        done_y = [
+            call(
+                functools.partial(combine_kernel, plane, 2, len(run_y), p * span),
+                [shape(token_rows, span)],
+                2 * move_flops * span // width,
+                [high, low] + near + run_y,
+            )[0]
+            for p, near in enumerate(back_y[s])
+        ]
+        gates = call(
+            functools.partial(gates_kernel, plane, ring, depth, s, bool(run_gates)),
+            [shape(8, token_rows, kind=F32)],
+            move_flops,
+            [place, ids, picked, block_c[s]] + sum(back_y[s], []) + run_gates,
         )
         before = [] if last else run_d
         done_d = call(
-            functools.partial(combine_back_kernel, plane, ring, depth, s, bool(before)),
-            [shape(token_rows, width, kind=F32) if last else row],
+            functools.partial(combine_kernel, plane, 1, len(before), 0),
+            [shape(token_rows, width, kind=F32 if last else BF16)],
             move_flops,
-            [place, ids] + back_d[s] + before,
+            [spread] + back_d[s] + before,
         )
         if not last:
-            run_y = [hop(done_y[0], ring_up)]
+            run_y = [hop(y, ring_up) for y in done_y]
             run_d = [hop(done_d[0], ring_up)]
-            run_gates = [hop(done_y[1], ring_up)]
-    expert_out, gates = done_y
+            run_gates = [hop(gates[0], ring_up)]
+    expert_out, gates = done_y[0], gates[0]
     grad_tokens = done_d[0]
     if run_d:
         grad_tokens = grad_tokens + run_d[0].astype(F32)

time: 204 us -> 206 us (level)
  the two profiles are of different devices: /device:TPU:0 before, /device:TPU:13 now
where the time goes in v5:
time: 206 us; the launch traced here: 203 us
  waiting for transfers between devices  83.1 us (40%)
  starting transfers between devices  69.8 us (34%)
  Pallas kernels  39.6 us (19%)
  local copies, waits for them, and re-layouts  8.35 us (4%)
    ppermute x70, waiting for transfers between devices, hop(): return lax.ppermute(value, 'owner', pairs)  83.1 us
    ppermute x70, starting transfers between devices, hop(): return lax.ppermute(value, 'owner', pairs)  69.8 us
    pallas_call x34, Pallas kernels, call(): pl.pallas_call(body, out_shape=tuple(outs), in_specs=specs, out_specs=tup...  39.6 us
    unnamed x22, local copies, waits for them, and re-layouts  7.08 us
  transfers between devices with their start and end apart: 70, of which 29 were waited for; matrix products, arithmetic and copies ran while one was open for 1% of the time, Pallas kernels for 20%

profile of v5, /device:TPU:13, one launch (start us, length us, event | category | flops | bytes accessed | tf_op | source)
XLA Modules:
  0.0 202.9 jit_solution(10338736346762665006)
XLA Ops:
  12.5 5.1 %collective-permute-done.2.refs_3_ = bf16[48,2048]{1,0:T(8,128)(2,1)S(1)} collective-permute-done((bf16[48,2048]{1,0:T(8,128)(2,1)S(1)}, bf16[48,2048]{1,0:T(8,128)(2,1)S(1)}, u32[]{:S(2)}, u32[]{:S(2)}) %collective-permute-start.2) | collective-permute-done | bytes 196640 | tf_op jit(solution)/shard_map/ppermute | solution.py:240
  23.3 2.1 %collective-permute-done.39.refs_3_.refs_19_ = bf16[48,2048]{1,0:T(8,128)(2,1)S(1)} collective-permute-done((bf16[48,2048]{1,0:T(8,128)(2,1)S(1)}, bf16[48,2048]{1,0:T(8,128)(2,1)S(1)}, u32[]{:S(2)}, u32[]{:S(2)}) %collective-permute-start.39) | collective-permute-done | bytes 196640 | tf_op jit(solution)/shard_map/ppermute | solution.py:240
  25.5 1.8 shard_map.136
  36.0 3.2 %collective-permute-done.8.probs.outs_0_ = f32[8,128]{1,0:T(8,128)S(1)} collective-permute-done((f32[8,128]{1,0:T(8,128)S(1)}, f32[8,128]{1,0:T(8,128)S(1)}, u32[]{:S(2)}, u32[]{:S(2)}) %collective-permute-start.8) | collective-permute-done | bytes 4128 | tf_op jit(solution)/shard_map/ppermute | solution.py:240
  40.4 3.6 %collective-permute-start.26 = (bf16[48,2048]{1,0:T(8,128)(2,1)S(1)}, bf16[48,2048]{1,0:T(8,128)(2,1)S(1)}, u32[]{:S(2)}, u32[]{:S(2)}) collective-permute-start(bf16[48,2048]{1,0:T(8,128)(2,1)S(1)} %get-tuple-element.148), channel_id=1, source_target_pairs={{0,3},{1,2},{2,1},{3,0},{4,7},{5,6},{6,5},{7,4},{8,11},{9,10},{10,... | collective-permute-start | bytes 589832 | tf_op jit(solution)/shard_map/ppermute | solution.py:240
  46.5 2.1 %collective-permute-start.44 = (bf16[128,2048]{1,0:T(8,128)(2,1)S(1)}, bf16[128,2048]{1,0:T(8,128)(2,1)S(1)}, u32[]{:S(2)}, u32[]{:S(2)}) collective-permute-start(bf16[128,2048]{1,0:T(8,128)(2,1)S(1)} %collective-permute-done.43.block), channel_id=1, source_target_pairs={{0,4},{1,5},{2,6},{3,7},{4,8},{5,9},{6,10},{7,11},{8,12},{9,13},{1... | collective-permute-start | bytes 1572872 | tf_op jit(solution)/shard_map/ppermute | solution.py:240
  48.6 4.5 %collective-permute-done.26.refs_3_.refs_7_ = bf16[48,2048]{1,0:T(8,128)(2,1)S(1)} collective-permute-done((bf16[48,2048]{1,0:T(8,128)(2,1)S(1)}, bf16[48,2048]{1,0:T(8,128)(2,1)S(1)}, u32[]{:S(2)}, u32[]{:S(2)}) %collective-permute-start.26) | collective-permute-done | bytes 196640 | tf_op jit(solution)/shard_map/ppermute | solution.py:240
  57.2 3.2 %collective-permute-done.60.refs_3_.refs_23_ = bf16[48,2048]{1,0:T(8,128)(2,1)S(1)} collective-permute-done((bf16[48,2048]{1,0:T(8,128)(2,1)S(1)}, bf16[48,2048]{1,0:T(8,128)(2,1)S(1)}, u32[]{:S(2)}, u32[]{:S(2)}) %collective-permute-start.60) | collective-permute-done | bytes 196640 | tf_op jit(solution)/shard_map/ppermute | solution.py:240
  60.5 2.5 %collective-permute-start.28 = (bf16[48,2048]{1,0:T(8,128)(2,1)S(1)}, bf16[48,2048]{1,0:T(8,128)(2,1)S(1)}, u32[]{:S(2)}, u32[]{:S(2)}) collective-permute-start(bf16[48,2048]{1,0:T(8,128)(2,1)S(1)} %get-tuple-element.151), channel_id=1, source_target_pairs={{0,2},{1,3},{2,0},{3,1},{4,6},{5,7},{6,4},{7,5},{8,10},{9,11},{10,... | collective-permute-start | bytes 589832 | tf_op jit(solution)/shard_map/ppermute | solution.py:240
  63.0 1.8 shard_map.143
  66.1 2.9 %collective-permute-done.28.refs_4_.refs_2_ = bf16[48,2048]{1,0:T(8,128)(2,1)S(1)} collective-permute-done((bf16[48,2048]{1,0:T(8,128)(2,1)S(1)}, bf16[48,2048]{1,0:T(8,128)(2,1)S(1)}, u32[]{:S(2)}, u32[]{:S(2)}) %collective-permute-start.28) | collective-permute-done | bytes 196640 | tf_op jit(solution)/shard_map/ppermute | solution.py:240
  77.7 3.8 %collective-permute-done.63.refs_4_ = bf16[48,2048]{1,0:T(8,128)(2,1)S(1)} collective-permute-done((bf16[48,2048]{1,0:T(8,128)(2,1)S(1)}, bf16[48,2048]{1,0:T(8,128)(2,1)S(1)}, u32[]{:S(2)}, u32[]{:S(2)}) %collective-permute-start.63) | collective-permute-done | bytes 196640 | tf_op jit(solution)/shard_map/ppermute | solution.py:240
  87.0 2.9 %collective-permute-done.20.refs_3_.refs_11_ = bf16[48,2048]{1,0:T(8,128)(2,1)S(1)} collective-permute-done((bf16[48,2048]{1,0:T(8,128)(2,1)S(1)}, bf16[48,2048]{1,0:T(8,128)(2,1)S(1)}, u32[]{:S(2)}, u32[]{:S(2)}) %collective-permute-start.20) | collective-permute-done | bytes 196640 | tf_op jit(solution)/shard_map/ppermute | solution.py:240
  95.9 2.5 %collective-permute-done.54.refs_3_.refs_27_ = bf16[48,2048]{1,0:T(8,128)(2,1)S(1)} collective-permute-done((bf16[48,2048]{1,0:T(8,128)(2,1)S(1)}, bf16[48,2048]{1,0:T(8,128)(2,1)S(1)}, u32[]{:S(2)}, u32[]{:S(2)}) %collective-permute-start.54) | collective-permute-done | bytes 196640 | tf_op jit(solution)/shard_map/ppermute | solution.py:240
  98.7 2.3 %collective-permute-start.64 = (bf16[128,2048]{1,0:T(8,128)(2,1)S(1)}, bf16[128,2048]{1,0:T(8,128)(2,1)S(1)}, u32[]{:S(2)}, u32[]{:S(2)}) collective-permute-start(bf16[128,2048]{1,0:T(8,128)(2,1)S(1)} %shard_map.144), channel_id=1, source_target_pairs={{0,4},{1,5},{2,6},{3,7},{4,8},{5,9},{6,10},{7,11},{8,12},{9,13},{1... | collective-permute-start | bytes 1572872 | tf_op jit(solution)/shard_map/ppermute | solution.py:240
  102.8 1.9 collective-permute-start.45
  104.7 1.8 shard_map.141
  112.1 3.1 %collective-permute-done.56.refs_3_ = bf16[48,2048]{1,0:T(8,128)(2,1)S(1)} collective-permute-done((bf16[48,2048]{1,0:T(8,128)(2,1)S(1)}, bf16[48,2048]{1,0:T(8,128)(2,1)S(1)}, u32[]{:S(2)}, u32[]{:S(2)}) %collective-permute-start.56) | collective-permute-done | bytes 196640 | tf_op jit(solution)/shard_map/ppermute | solution.py:240
  115.1 2.1 %collective-permute-start.12 = (bf16[48,2048]{1,0:T(8,128)(2,1)S(1)}, bf16[48,2048]{1,0:T(8,128)(2,1)S(1)}, u32[]{:S(2)}, u32[]{:S(2)}) collective-permute-start(bf16[48,2048]{1,0:T(8,128)(2,1)S(1)} %get-tuple-element.126), channel_id=1, source_target_pairs={{0,1},{1,0},{2,3},{3,2},{4,5},{5,4},{6,7},{7,6},{8,9},{9,8},{10,11... | collective-permute-start | bytes 589832 | tf_op jit(solution)/shard_map/ppermute | solution.py:240
  117.2 3.0 %collective-permute-done.57.refs_4_ = bf16[48,2048]{1,0:T(8,128)(2,1)S(1)} collective-permute-done((bf16[48,2048]{1,0:T(8,128)(2,1)S(1)}, bf16[48,2048]{1,0:T(8,128)(2,1)S(1)}, u32[]{:S(2)}, u32[]{:S(2)}) %collective-permute-start.57) | collective-permute-done | bytes 196640 | tf_op jit(solution)/shard_map/ppermute | solution.py:240
  123.3 4.4 %collective-permute-done.64.refs_5_ = bf16[128,2048]{1,0:T(8,128)(2,1)S(1)} collective-permute-done((bf16[128,2048]{1,0:T(8,128)(2,1)S(1)}, bf16[128,2048]{1,0:T(8,128)(2,1)S(1)}, u32[]{:S(2)}, u32[]{:S(2)}) %collective-permute-start.64) | collective-permute-done | bytes 524320 | tf_op jit(solution)/shard_map/ppermute | solution.py:240
  128.1 10.9 %collective-permute-done.68.refs_8_ = f32[8,128]{1,0:T(8,128)S(1)} collective-permute-done((f32[8,128]{1,0:T(8,128)S(1)}, f32[8,128]{1,0:T(8,128)S(1)}, u32[]{:S(2)}, u32[]{:S(2)}) %collective-permute-start.68) | collective-permute-done | bytes 4128 | tf_op jit(solution)/shard_map/ppermute | solution.py:240
  141.8 2.0 %collective-permute-start.46 = (bf16[48,2048]{1,0:T(8,128)(2,1)S(1)}, bf16[48,2048]{1,0:T(8,128)(2,1)S(1)}, u32[]{:S(2)}, u32[]{:S(2)}) collective-permute-start(bf16[48,2048]{1,0:T(8,128)(2,1)S(1)} %get-tuple-element.170), channel_id=1, source_target_pairs={{0,1},{1,0},{2,3},{3,2},{4,5},{5,4},{6,7},{7,6},{8,9},{9,8},{10,11... | collective-permute-start | bytes 589832 | tf_op jit(solution)/shard_map/ppermute | solution.py:240
  147.2 2.9 %collective-permute-done.47.refs_2_.refs_30_ = bf16[48,2048]{1,0:T(8,128)(2,1)S(1)} collective-permute-done((bf16[48,2048]{1,0:T(8,128)(2,1)S(1)}, bf16[48,2048]{1,0:T(8,128)(2,1)S(1)}, u32[]{:S(2)}, u32[]{:S(2)}) %collective-permute-start.47) | collective-permute-done | bytes 196640 | tf_op jit(solution)/shard_map/ppermute | solution.py:240
  151.2 4.3 %collective-permute-done.48.refs_3_.refs_31_ = bf16[48,2048]{1,0:T(8,128)(2,1)S(1)} collective-permute-done((bf16[48,2048]{1,0:T(8,128)(2,1)S(1)}, bf16[48,2048]{1,0:T(8,128)(2,1)S(1)}, u32[]{:S(2)}, u32[]{:S(2)}) %collective-permute-start.48) | collective-permute-done | bytes 196640 | tf_op jit(solution)/shard_map/ppermute | solution.py:240
  157.5 2.6 %collective-permute-done.17.refs_5_.refs_3_ = bf16[48,1024]{1,0:T(8,128)(2,1)S(1)} collective-permute-done((bf16[48,1024]{1,0:T(8,128)(2,1)S(1)}, bf16[48,1024]{1,0:T(8,128)(2,1)S(1)}, u32[]{:S(2)}, u32[]{:S(2)}) %collective-permute-start.17) | collective-permute-done | bytes 98336 | tf_op jit(solution)/shard_map/ppermute | solution.py:240
  160.1 1.8 shard_map.139
  171.8 3.6 %collective-permute-start.69 = (f32[8,128]{1,0:T(8,128)S(1)}, f32[8,128]{1,0:T(8,128)S(1)}, u32[]{:S(2)}, u32[]{:S(2)}) collective-permute-start(f32[8,128]{1,0:T(8,128)S(1)} %shard_map.149), channel_id=1, source_target_pairs={{0,4},{1,5},{2,6},{3,7},{4,8},{5,9},{6,10},{7,11},{8,12},{9,13},{1... | collective-permute-start | bytes 12296 | tf_op jit(solution)/shard_map/ppermute | solution.py:240
  175.4 3.6 %collective-permute-start.32 = (bf16[128,1024]{1,0:T(8,128)(2,1)S(1)}, bf16[128,1024]{1,0:T(8,128)(2,1)S(1)}, u32[]{:S(2)}, u32[]{:S(2)}) collective-permute-start(bf16[128,1024]{1,0:T(8,128)(2,1)S(1)} %shard_map.132), channel_id=1, source_target_pairs={{0,4},{1,5},{2,6},{3,7},{4,8},{5,9},{6,10},{7,11},{8,12},{9,13},{1... | collective-permute-start | bytes 786440 | tf_op jit(solution)/shard_map/ppermute | solution.py:240
  179.5 3.0 %collective-permute-start.66 = (bf16[128,2048]{1,0:T(8,128)(2,1)S(1)}, bf16[128,2048]{1,0:T(8,128)(2,1)S(1)}, u32[]{:S(2)}, u32[]{:S(2)}) collective-permute-start(bf16[128,2048]{1,0:T(8,128)(2,1)S(1)} %shard_map.146), channel_id=1, source_target_pairs={{0,4},{1,5},{2,6},{3,7},{4,8},{5,9},{6,10},{7,11},{8,12},{9,13},{1... | collective-permute-start | bytes 1572872 | tf_op jit(solution)/shard_map/ppermute | solution.py:240
  182.5 6.7 %shard_map.151 = (bf16[2048,384]{1,0:T(8,128)(2,1)}, bf16[2048,384]{1,0:T(8,128)(2,1)}, bf16[384,2048]{1,0:T(8,128)(2,1)}) custom-call(bf16[48,2048]{1,0:T(8,128)(2,1)S(1)} %get-tuple-element.115.refs_0_, bf16[48,2048]{1,0:T(8,128)(2,1)S(1)} %collective-permute-done.refs_1_, bf16[48,2048]{1,0:T(8,128)(2,1)S(1)} %collective-permute-done.1.refs_2_, ...), custom_call_target="tpu_custom_call" | custom-call | flops 3623878656 | bytes 12779520 | tf_op jit(solution)/shard_map/pallas_call | solution.py:212
  192.0 10.0 %collective-permute-done.66 = bf16[128,2048]{1,0:T(8,128)(2,1)S(1)} collective-permute-done((bf16[128,2048]{1,0:T(8,128)(2,1)S(1)}, bf16[128,2048]{1,0:T(8,128)(2,1)S(1)}, u32[]{:S(2)}, u32[]{:S(2)}) %collective-permute-start.66) | collective-permute-done | bytes 524320 | tf_op jit(solution)/shard_map/ppermute | solution.py:240
  (168 shorter events, 89.5 us)
Async XLA Ops:
  0.6 27.3 %collective-permute-start.9 = (bf16[128,2048]{1,0:T(8,128)(2,1)}, bf16[128,2048]{1,0:T(8,128)(2,1)S(1)}, u32[]{:S(2)}, u32[]{:S(2)}) collective-permute-start(bf16[128,2048]{1,0:T(8,128)(2,1)} %block.3), channel_id=1, source_target_pairs={{0,4},{1,5},{2,6},{3,7},{4,8},{5,9},{6,10},{7,11},{8,12},{9,13},{1... | collective-permute-start | bytes 1572872 | tf_op jit(solution)/shard_map/ppermute | solution.py:240
  6.1 11.4 %collective-permute-start.2 = (bf16[48,2048]{1,0:T(8,128)(2,1)S(1)}, bf16[48,2048]{1,0:T(8,128)(2,1)S(1)}, u32[]{:S(2)}, u32[]{:S(2)}) collective-permute-start(bf16[48,2048]{1,0:T(8,128)(2,1)S(1)} %get-tuple-element.118), channel_id=1, source_target_pairs={{0,3},{1,2},{2,1},{3,0},{4,7},{5,6},{6,5},{7,4},{8,11},{9,10},{10,... | collective-permute-start | bytes 589832 | tf_op jit(solution)/shard_map/ppermute | solution.py:240
  7.6 32.8 %collective-permute-start.43 = (bf16[128,2048]{1,0:T(8,128)(2,1)}, bf16[128,2048]{1,0:T(8,128)(2,1)S(1)}, u32[]{:S(2)}, u32[]{:S(2)}) collective-permute-start(bf16[128,2048]{1,0:T(8,128)(2,1)} %block.5), channel_id=1, source_target_pairs={{0,4},{1,5},{2,6},{3,7},{4,8},{5,9},{6,10},{7,11},{8,12},{9,13},{1... | collective-permute-start | bytes 1572872 | tf_op jit(solution)/shard_map/ppermute | solution.py:240
  11.7 11.6 %collective-permute-start.37 = (bf16[48,2048]{1,0:T(8,128)(2,1)S(1)}, bf16[48,2048]{1,0:T(8,128)(2,1)S(1)}, u32[]{:S(2)}, u32[]{:S(2)}) collective-permute-start(bf16[48,2048]{1,0:T(8,128)(2,1)S(1)} %get-tuple-element.159), channel_id=1, source_target_pairs={{0,1},{1,0},{2,3},{3,2},{4,5},{5,4},{6,7},{7,6},{8,9},{9,8},{10,11... | collective-permute-start | bytes 589832 | tf_op jit(solution)/shard_map/ppermute | solution.py:240
  27.3 17.7 %collective-permute-start.40 = (bf16[48,2048]{1,0:T(8,128)(2,1)S(1)}, bf16[48,2048]{1,0:T(8,128)(2,1)S(1)}, u32[]{:S(2)}, u32[]{:S(2)}) collective-permute-start(bf16[48,2048]{1,0:T(8,128)(2,1)S(1)} %get-tuple-element.165), channel_id=1, source_target_pairs={{0,1},{1,0},{2,3},{3,2},{4,5},{5,4},{6,7},{7,6},{8,9},{9,8},{10,11... | collective-permute-start | bytes 589832 | tf_op jit(solution)/shard_map/ppermute | solution.py:240
  27.4 17.8 %collective-permute-start.41 = (bf16[48,2048]{1,0:T(8,128)(2,1)S(1)}, bf16[48,2048]{1,0:T(8,128)(2,1)S(1)}, u32[]{:S(2)}, u32[]{:S(2)}) collective-permute-start(bf16[48,2048]{1,0:T(8,128)(2,1)S(1)} %get-tuple-element.166), channel_id=1, source_target_pairs={{0,2},{1,3},{2,0},{3,1},{4,6},{5,7},{6,4},{7,5},{8,10},{9,11},{10,... | collective-permute-start | bytes 589832 | tf_op jit(solution)/shard_map/ppermute | solution.py:240
  29.0 17.5 %collective-permute-start.24 = (bf16[48,2048]{1,0:T(8,128)(2,1)S(1)}, bf16[48,2048]{1,0:T(8,128)(2,1)S(1)}, u32[]{:S(2)}, u32[]{:S(2)}) collective-permute-start(bf16[48,2048]{1,0:T(8,128)(2,1)S(1)} %get-tuple-element.146), channel_id=1, source_target_pairs={{0,1},{1,0},{2,3},{3,2},{4,5},{5,4},{6,7},{7,6},{8,9},{9,8},{10,11... | collective-permute-start | bytes 589832 | tf_op jit(solution)/shard_map/ppermute | solution.py:240
  40.4 12.6 %collective-permute-start.26 = (bf16[48,2048]{1,0:T(8,128)(2,1)S(1)}, bf16[48,2048]{1,0:T(8,128)(2,1)S(1)}, u32[]{:S(2)}, u32[]{:S(2)}) collective-permute-start(bf16[48,2048]{1,0:T(8,128)(2,1)S(1)} %get-tuple-element.148), channel_id=1, source_target_pairs={{0,3},{1,2},{2,1},{3,0},{4,7},{5,6},{6,5},{7,4},{8,11},{9,10},{10,... | collective-permute-start | bytes 589832 | tf_op jit(solution)/shard_map/ppermute | solution.py:240
  46.5 23.5 %collective-permute-start.10 = (bf16[128,2048]{1,0:T(8,128)(2,1)S(1)}, bf16[128,2048]{1,0:T(8,128)(2,1)S(1)}, u32[]{:S(2)}, u32[]{:S(2)}) collective-permute-start(bf16[128,2048]{1,0:T(8,128)(2,1)S(1)} %collective-permute-done.9.block), channel_id=1, source_target_pairs={{0,4},{1,5},{2,6},{3,7},{4,8},{5,9},{6,10},{7,11},{8,12},{9,13},{1... | collective-permute-start | bytes 1572872 | tf_op jit(solution)/shard_map/ppermute | solution.py:240
  46.5 28.1 %collective-permute-start.44 = (bf16[128,2048]{1,0:T(8,128)(2,1)S(1)}, bf16[128,2048]{1,0:T(8,128)(2,1)S(1)}, u32[]{:S(2)}, u32[]{:S(2)}) collective-permute-start(bf16[128,2048]{1,0:T(8,128)(2,1)S(1)} %collective-permute-done.43.block), channel_id=1, source_target_pairs={{0,4},{1,5},{2,6},{3,7},{4,8},{5,9},{6,10},{7,11},{8,12},{9,13},{1... | collective-permute-start | bytes 1572872 | tf_op jit(solution)/shard_map/ppermute | solution.py:240
  69.9 11.6 %collective-permute-start.63 = (bf16[48,2048]{1,0:T(8,128)(2,1)S(1)}, bf16[48,2048]{1,0:T(8,128)(2,1)S(1)}, u32[]{:S(2)}, u32[]{:S(2)}) collective-permute-start(bf16[48,2048]{1,0:T(8,128)(2,1)S(1)} %get-tuple-element.200), channel_id=1, source_target_pairs={{0,3},{1,2},{2,1},{3,0},{4,7},{5,6},{6,5},{7,4},{8,11},{9,10},{10,... | collective-permute-start | bytes 589832 | tf_op jit(solution)/shard_map/ppermute | solution.py:240
  73.7 12.1 %collective-permute-start.19 = (bf16[48,2048]{1,0:T(8,128)(2,1)S(1)}, bf16[48,2048]{1,0:T(8,128)(2,1)S(1)}, u32[]{:S(2)}, u32[]{:S(2)}) collective-permute-start(bf16[48,2048]{1,0:T(8,128)(2,1)S(1)} %get-tuple-element.137), channel_id=1, source_target_pairs={{0,2},{1,3},{2,0},{3,1},{4,6},{5,7},{6,4},{7,5},{8,10},{9,11},{10,... | collective-permute-start | bytes 589832 | tf_op jit(solution)/shard_map/ppermute | solution.py:240
  74.5 15.4 %collective-permute-start.20 = (bf16[48,2048]{1,0:T(8,128)(2,1)S(1)}, bf16[48,2048]{1,0:T(8,128)(2,1)S(1)}, u32[]{:S(2)}, u32[]{:S(2)}) collective-permute-start(bf16[48,2048]{1,0:T(8,128)(2,1)S(1)} %get-tuple-element.138), channel_id=1, source_target_pairs={{0,3},{1,2},{2,1},{3,0},{4,7},{5,6},{6,5},{7,4},{8,11},{9,10},{10,... | collective-permute-start | bytes 589832 | tf_op jit(solution)/shard_map/ppermute | solution.py:240
  77.3 14.8 %collective-permute-start.52 = (bf16[48,2048]{1,0:T(8,128)(2,1)S(1)}, bf16[48,2048]{1,0:T(8,128)(2,1)S(1)}, u32[]{:S(2)}, u32[]{:S(2)}) collective-permute-start(bf16[48,2048]{1,0:T(8,128)(2,1)S(1)} %get-tuple-element.181), channel_id=1, source_target_pairs={{0,1},{1,0},{2,3},{3,2},{4,5},{5,4},{6,7},{7,6},{8,9},{9,8},{10,11... | collective-permute-start | bytes 589832 | tf_op jit(solution)/shard_map/ppermute | solution.py:240
  81.5 12.6 %collective-permute-start.53 = (bf16[48,2048]{1,0:T(8,128)(2,1)S(1)}, bf16[48,2048]{1,0:T(8,128)(2,1)S(1)}, u32[]{:S(2)}, u32[]{:S(2)}) collective-permute-start(bf16[48,2048]{1,0:T(8,128)(2,1)S(1)} %get-tuple-element.182), channel_id=1, source_target_pairs={{0,2},{1,3},{2,0},{3,1},{4,6},{5,7},{6,4},{7,5},{8,10},{9,11},{10,... | collective-permute-start | bytes 589832 | tf_op jit(solution)/shard_map/ppermute | solution.py:240
  85.7 12.6 %collective-permute-start.54 = (bf16[48,2048]{1,0:T(8,128)(2,1)S(1)}, bf16[48,2048]{1,0:T(8,128)(2,1)S(1)}, u32[]{:S(2)}, u32[]{:S(2)}) collective-permute-start(bf16[48,2048]{1,0:T(8,128)(2,1)S(1)} %get-tuple-element.183), channel_id=1, source_target_pairs={{0,3},{1,2},{2,1},{3,0},{4,7},{5,6},{6,5},{7,4},{8,11},{9,10},{10,... | collective-permute-start | bytes 589832 | tf_op jit(solution)/shard_map/ppermute | solution.py:240
  90.0 20.0 %collective-permute-start.11 = (bf16[128,2048]{1,0:T(8,128)(2,1)S(1)}, bf16[128,2048]{1,0:T(8,128)(2,1)S(1)}, u32[]{:S(2)}, u32[]{:S(2)}) collective-permute-start(bf16[128,2048]{1,0:T(8,128)(2,1)S(1)} %collective-permute-done.10.block), channel_id=1, source_target_pairs={{0,4},{1,5},{2,6},{3,7},{4,8},{5,9},{6,10},{7,11},{8,12},{9,13},{1... | collective-permute-start | bytes 1572872 | tf_op jit(solution)/shard_map/ppermute | solution.py:240
  94.2 12.6 %collective-permute-start.23 = (bf16[48,2048]{1,0:T(8,128)(2,1)S(1)}, bf16[48,2048]{1,0:T(8,128)(2,1)S(1)}, u32[]{:S(2)}, u32[]{:S(2)}) collective-permute-start(bf16[48,2048]{1,0:T(8,128)(2,1)S(1)} %get-tuple-element.142), channel_id=1, source_target_pairs={{0,3},{1,2},{2,1},{3,0},{4,7},{5,6},{6,5},{7,4},{8,11},{9,10},{10,... | collective-permute-start | bytes 589832 | tf_op jit(solution)/shard_map/ppermute | solution.py:240
  98.4 22.7 %collective-permute-start.30 = (bf16[128,2048]{1,0:T(8,128)(2,1)S(1)}, bf16[128,2048]{1,0:T(8,128)(2,1)S(1)}, u32[]{:S(2)}, u32[]{:S(2)}) collective-permute-start(bf16[128,2048]{1,0:T(8,128)(2,1)S(1)} %shard_map.130), channel_id=1, source_target_pairs={{0,4},{1,5},{2,6},{3,7},{4,8},{5,9},{6,10},{7,11},{8,12},{9,13},{1... | collective-permute-start | bytes 1572872 | tf_op jit(solution)/shard_map/ppermute | solution.py:240
  98.7 29.0 %collective-permute-start.64 = (bf16[128,2048]{1,0:T(8,128)(2,1)S(1)}, bf16[128,2048]{1,0:T(8,128)(2,1)S(1)}, u32[]{:S(2)}, u32[]{:S(2)}) collective-permute-start(bf16[128,2048]{1,0:T(8,128)(2,1)S(1)} %shard_map.144), channel_id=1, source_target_pairs={{0,4},{1,5},{2,6},{3,7},{4,8},{5,9},{6,10},{7,11},{8,12},{9,13},{1... | collective-permute-start | bytes 1572872 | tf_op jit(solution)/shard_map/ppermute | solution.py:240
  102.8 36.6 %collective-permute-start.45 = (bf16[128,2048]{1,0:T(8,128)(2,1)S(1)}, bf16[128,2048]{1,0:T(8,128)(2,1)S(1)}, u32[]{:S(2)}, u32[]{:S(2)}) collective-permute-start(bf16[128,2048]{1,0:T(8,128)(2,1)S(1)} %collective-permute-done.44.block), channel_id=1, source_target_pairs={{0,4},{1,5},{2,6},{3,7},{4,8},{5,9},{6,10},{7,11},{8,12},{9,13},{1... | collective-permute-start | bytes 1572872 | tf_op jit(solution)/shard_map/ppermute | solution.py:240
  115.1 26.6 %collective-permute-start.12 = (bf16[48,2048]{1,0:T(8,128)(2,1)S(1)}, bf16[48,2048]{1,0:T(8,128)(2,1)S(1)}, u32[]{:S(2)}, u32[]{:S(2)}) collective-permute-start(bf16[48,2048]{1,0:T(8,128)(2,1)S(1)} %get-tuple-element.126), channel_id=1, source_target_pairs={{0,1},{1,0},{2,3},{3,2},{4,5},{5,4},{6,7},{7,6},{8,9},{9,8},{10,11... | collective-permute-start | bytes 589832 | tf_op jit(solution)/shard_map/ppermute | solution.py:240
  120.2 23.7 %collective-permute-start.13 = (bf16[48,2048]{1,0:T(8,128)(2,1)S(1)}, bf16[48,2048]{1,0:T(8,128)(2,1)S(1)}, u32[]{:S(2)}, u32[]{:S(2)}) collective-permute-start(bf16[48,2048]{1,0:T(8,128)(2,1)S(1)} %get-tuple-element.127), channel_id=1, source_target_pairs={{0,2},{1,3},{2,0},{3,1},{4,6},{5,7},{6,4},{7,5},{8,10},{9,11},{10,... | collective-permute-start | bytes 589832 | tf_op jit(solution)/shard_map/ppermute | solution.py:240
  121.1 23.8 %collective-permute-start.14 = (bf16[48,2048]{1,0:T(8,128)(2,1)S(1)}, bf16[48,2048]{1,0:T(8,128)(2,1)S(1)}, u32[]{:S(2)}, u32[]{:S(2)}) collective-permute-start(bf16[48,2048]{1,0:T(8,128)(2,1)S(1)} %get-tuple-element.128), channel_id=1, source_target_pairs={{0,3},{1,2},{2,1},{3,0},{4,7},{5,6},{6,5},{7,4},{8,11},{9,10},{10,... | collective-permute-start | bytes 589832 | tf_op jit(solution)/shard_map/ppermute | solution.py:240
  139.0 26.5 %collective-permute-start.31 = (bf16[128,2048]{1,0:T(8,128)(2,1)S(1)}, bf16[128,2048]{1,0:T(8,128)(2,1)S(1)}, u32[]{:S(2)}, u32[]{:S(2)}) collective-permute-start(bf16[128,2048]{1,0:T(8,128)(2,1)S(1)} %shard_map.131), channel_id=1, source_target_pairs={{0,4},{1,5},{2,6},{3,7},{4,8},{5,9},{6,10},{7,11},{8,12},{9,13},{1... | collective-permute-start | bytes 1572872 | tf_op jit(solution)/shard_map/ppermute | solution.py:240
  139.4 26.9 %collective-permute-start.65 = (bf16[128,2048]{1,0:T(8,128)(2,1)S(1)}, bf16[128,2048]{1,0:T(8,128)(2,1)S(1)}, u32[]{:S(2)}, u32[]{:S(2)}) collective-permute-start(bf16[128,2048]{1,0:T(8,128)(2,1)S(1)} %shard_map.145), channel_id=1, source_target_pairs={{0,4},{1,5},{2,6},{3,7},{4,8},{5,9},{6,10},{7,11},{8,12},{9,13},{1... | collective-permute-start | bytes 1572872 | tf_op jit(solution)/shard_map/ppermute | solution.py:240
  165.5 13.9 %collective-permute-start.3 = (bf16[48,2048]{1,0:T(8,128)(2,1)S(1)}, bf16[48,2048]{1,0:T(8,128)(2,1)S(1)}, u32[]{:S(2)}, u32[]{:S(2)}) collective-permute-start(bf16[48,2048]{1,0:T(8,128)(2,1)S(1)} %get-tuple-element.120), channel_id=1, source_target_pairs={{0,1},{1,0},{2,3},{3,2},{4,5},{5,4},{6,7},{7,6},{8,9},{9,8},{10,11... | collective-permute-start | bytes 589832 | tf_op jit(solution)/shard_map/ppermute | solution.py:240
  166.2 13.2 %collective-permute-start.4 = (bf16[48,2048]{1,0:T(8,128)(2,1)S(1)}, bf16[48,2048]{1,0:T(8,128)(2,1)S(1)}, u32[]{:S(2)}, u32[]{:S(2)}) collective-permute-start(bf16[48,2048]{1,0:T(8,128)(2,1)S(1)} %get-tuple-element.121), channel_id=1, source_target_pairs={{0,2},{1,3},{2,0},{3,1},{4,6},{5,7},{6,4},{7,5},{8,10},{9,11},{10,... | collective-permute-start | bytes 589832 | tf_op jit(solution)/shard_map/ppermute | solution.py:240
  170.5 18.7 %collective-permute-start.5 = (bf16[48,2048]{1,0:T(8,128)(2,1)S(1)}, bf16[48,2048]{1,0:T(8,128)(2,1)S(1)}, u32[]{:S(2)}, u32[]{:S(2)}) collective-permute-start(bf16[48,2048]{1,0:T(8,128)(2,1)S(1)} %get-tuple-element.122), channel_id=1, source_target_pairs={{0,3},{1,2},{2,1},{3,0},{4,7},{5,6},{6,5},{7,4},{8,11},{9,10},{10,... | collective-permute-start | bytes 589832 | tf_op jit(solution)/shard_map/ppermute | solution.py:240
  171.8 17.4 %collective-permute-start.69 = (f32[8,128]{1,0:T(8,128)S(1)}, f32[8,128]{1,0:T(8,128)S(1)}, u32[]{:S(2)}, u32[]{:S(2)}) collective-permute-start(f32[8,128]{1,0:T(8,128)S(1)} %shard_map.149), channel_id=1, source_target_pairs={{0,4},{1,5},{2,6},{3,7},{4,8},{5,9},{6,10},{7,11},{8,12},{9,13},{1... | collective-permute-start | bytes 12296 | tf_op jit(solution)/shard_map/ppermute | solution.py:240
  175.4 15.3 %collective-permute-start.32 = (bf16[128,1024]{1,0:T(8,128)(2,1)S(1)}, bf16[128,1024]{1,0:T(8,128)(2,1)S(1)}, u32[]{:S(2)}, u32[]{:S(2)}) collective-permute-start(bf16[128,1024]{1,0:T(8,128)(2,1)S(1)} %shard_map.132), channel_id=1, source_target_pairs={{0,4},{1,5},{2,6},{3,7},{4,8},{5,9},{6,10},{7,11},{8,12},{9,13},{1... | collective-permute-start | bytes 786440 | tf_op jit(solution)/shard_map/ppermute | solution.py:240
  179.5 22.5 %collective-permute-start.66 = (bf16[128,2048]{1,0:T(8,128)(2,1)S(1)}, bf16[128,2048]{1,0:T(8,128)(2,1)S(1)}, u32[]{:S(2)}, u32[]{:S(2)}) collective-permute-start(bf16[128,2048]{1,0:T(8,128)(2,1)S(1)} %shard_map.146), channel_id=1, source_target_pairs={{0,4},{1,5},{2,6},{3,7},{4,8},{5,9},{6,10},{7,11},{8,12},{9,13},{1... | collective-permute-start | bytes 1572872 | tf_op jit(solution)/shard_map/ppermute | solution.py:240
  (49 other events, 321.7 us)

commit v6 on v5

--- a/solution.py
+++ b/solution.py
@@ -110,8 +110,9 @@
 def backward_kernel(plane, *refs):
     rows = refs[:plane]
     gate_pre, up_pre, gate_w, up_w, down_w = refs[plane : plane + 5]
-    outs = refs[plane + 5 : 2 * plane + 5]
-    ggp_out, gup_out = refs[2 * plane + 5 :]
+    outs = refs[plane + 5 : -2]
+    ggp_out, gup_out = refs[-2:]
+    span = outs[0].shape[1]
     width = gate_w.shape[0]
     depth = rows[0].shape[0]
     row_c = jnp.concatenate([r[...] for r in rows], axis=0)
@@ -126,8 +127,9 @@
     for start in range(0, width, TILE):
         cols = pl.ds(start, TILE)
         dx = (nt(ggp, gate_w[cols, :]) + nt(gup, up_w[cols, :])).astype(BF16)
+        part = outs[start // span * plane :]
         for e in range(plane):
-            outs[e][:, cols] = dx[e * depth : (e + 1) * depth]
+            part[e][:, pl.ds(start % span, TILE)] = dx[e * depth : (e + 1) * depth]
 
 
 def maps_kernel(plane, ring, depth, step, place, ids, probs, high, low, spread, picked):
@@ -281,13 +283,13 @@
         )
         back = call(
             functools.partial(backward_kernel, plane),
-            slots + [shape(rows, hidden_width)] * 2,
+            [shape(depth, width // parts)] * count + [shape(rows, hidden_width)] * 2,
             3 * dense_flops,
             got_c[s] + list(ahead[count + 1 :]) + weights,
         )
-        small += [ahead[count], back[plane], back[plane + 1]]
+        small += [ahead[count], back[count], back[count + 1]]
         back_y.append([exchange(ahead[p * plane : (p + 1) * plane]) for p in range(parts)])
-        back_d.append(exchange(back[:plane]))
+        back_d.append([exchange(back[p * plane : (p + 1) * plane]) for p in range(parts)])
 
     run_y, run_d, run_gates = [], [], []
     for s in list(range(1, ring)) + [0]:
@@ -315,20 +317,23 @@
             [place, ids, picked, block_c[s]] + sum(back_y[s], []) + run_gates,
         )
         before = [] if last else run_d
-        done_d = call(
-            functools.partial(combine_kernel, plane, 1, len(before), 0),
-            [shape(token_rows, width, kind=F32 if last else BF16)],
-            move_flops,
-            [spread] + back_d[s] + before,
-        )
+        done_d = [
+            call(
+                functools.partial(combine_kernel, plane, 1, len(before), p * span),
+                [shape(token_rows, span, kind=F32 if last else BF16)],
+                move_flops * span // width,
+                [spread] + near + before,
+            )[0]
+            for p, near in enumerate(back_d[s])
+        ]
         if not last:
             run_y = [hop(y, ring_up) for y in done_y]
-            run_d = [hop(done_d[0], ring_up)]
+            run_d = [hop(d, ring_up) for d in done_d]
             run_gates = [hop(gates[0], ring_up)]
     expert_out, gates = done_y[0], gates[0]
     grad_tokens = done_d[0]
     if run_d:
-        grad_tokens = grad_tokens + run_d[0].astype(F32)
+        grad_tokens = grad_tokens + jnp.concatenate(run_d, axis=1).astype(F32)
     grad_tokens = grad_tokens.astype(BF16)
 
     grads = call(

time: 206 us -> 213 us (1.034)
  the two profiles are of different devices: /device:TPU:13 before, /device:TPU:0 now
where the time goes in v6:
time: 213 us
  waiting for transfers between devices  113 us (53%)
  starting transfers between devices  50.2 us (24%)
  Pallas kernels  40.2 us (19%)
  local copies, waits for them, and re-layouts  7.72 us (4%)
    ppermute x74, waiting for transfers between devices, hop(): return lax.ppermute(value, 'owner', pairs)  113 us
    ppermute x74, starting transfers between devices, hop(): return lax.ppermute(value, 'owner', pairs)  50.2 us
    pallas_call x35, Pallas kernels, call(): pl.pallas_call(body, out_shape=tuple(outs), in_specs=specs, out_specs=tup...  40.2 us
    unnamed x20, local copies, waits for them, and re-layouts  6.45 us
  transfers between devices with their start and end apart: 74, of which 37 were waited for; matrix products, arithmetic and copies ran while one was open for 1% of the time, Pallas kernels for 18%

profile of v6, /device:TPU:0, one launch (start us, length us, event | category | flops | bytes accessed | tf_op | source)
XLA Modules:
  0.0 212.8 jit_solution(8977830064463615776)
XLA Ops:
  3.6 2.6 %collective-permute-start.1 = (bf16[48,2048]{1,0:T(8,128)(2,1)S(1)}, bf16[48,2048]{1,0:T(8,128)(2,1)S(1)}, u32[]{:S(2)}, u32[]{:S(2)}) collective-permute-start(bf16[48,2048]{1,0:T(8,128)(2,1)S(1)} %get-tuple-element.121), channel_id=1, source_target_pairs={{0,2},{1,3},{2,0},{3,1},{4,6},{5,7},{6,4},{7,5},{8,10},{9,11},{10,... | collective-permute-start | bytes 589832 | tf_op jit(solution)/shard_map/ppermute | solution.py:242
  6.2 1.8 collective-permute-start.9
  15.7 2.2 %collective-permute-start.39 = (bf16[48,2048]{1,0:T(8,128)(2,1)S(1)}, bf16[48,2048]{1,0:T(8,128)(2,1)S(1)}, u32[]{:S(2)}, u32[]{:S(2)}) collective-permute-start(bf16[48,2048]{1,0:T(8,128)(2,1)S(1)} %get-tuple-element.165), channel_id=1, source_target_pairs={{0,3},{1,2},{2,1},{3,0},{4,7},{5,6},{6,5},{7,4},{8,11},{9,10},{10,... | collective-permute-start | bytes 589832 | tf_op jit(solution)/shard_map/ppermute | solution.py:242
  24.4 1.8 shard_map.136
  29.7 4.4 %collective-permute-done.6.probs.outs_0_ = f32[8,128]{1,0:T(8,128)S(1)} collective-permute-done((f32[8,128]{1,0:T(8,128)S(1)}, f32[8,128]{1,0:T(8,128)S(1)}, u32[]{:S(2)}, u32[]{:S(2)}) %collective-permute-start.6) | collective-permute-done | bytes 4128 | tf_op jit(solution)/shard_map/ppermute | solution.py:242
  34.0 5.4 %collective-permute-done.7.probs.outs_0_ = f32[8,128]{1,0:T(8,128)S(1)} collective-permute-done((f32[8,128]{1,0:T(8,128)S(1)}, f32[8,128]{1,0:T(8,128)S(1)}, u32[]{:S(2)}, u32[]{:S(2)}) %collective-permute-start.7) | collective-permute-done | bytes 4128 | tf_op jit(solution)/shard_map/ppermute | solution.py:242
  40.5 4.4 %collective-permute-done.8.probs.outs_0_ = f32[8,128]{1,0:T(8,128)S(1)} collective-permute-done((f32[8,128]{1,0:T(8,128)S(1)}, f32[8,128]{1,0:T(8,128)S(1)}, u32[]{:S(2)}, u32[]{:S(2)}) %collective-permute-start.8) | collective-permute-done | bytes 4128 | tf_op jit(solution)/shard_map/ppermute | solution.py:242
  48.6 4.4 %collective-permute-done.25.refs_2_.refs_6_ = bf16[48,2048]{1,0:T(8,128)(2,1)S(1)} collective-permute-done((bf16[48,2048]{1,0:T(8,128)(2,1)S(1)}, bf16[48,2048]{1,0:T(8,128)(2,1)S(1)}, u32[]{:S(2)}, u32[]{:S(2)}) %collective-permute-start.25) | collective-permute-done | bytes 196640 | tf_op jit(solution)/shard_map/ppermute | solution.py:242
  55.9 2.2 %collective-permute-start.60 = (bf16[48,2048]{1,0:T(8,128)(2,1)S(1)}, bf16[48,2048]{1,0:T(8,128)(2,1)S(1)}, u32[]{:S(2)}, u32[]{:S(2)}) collective-permute-start(bf16[48,2048]{1,0:T(8,128)(2,1)S(1)} %get-tuple-element.198), channel_id=1, source_target_pairs={{0,3},{1,2},{2,1},{3,0},{4,7},{5,6},{6,5},{7,4},{8,11},{9,10},{10,... | collective-permute-start | bytes 589832 | tf_op jit(solution)/shard_map/ppermute | solution.py:242
  59.6 1.9 collective-permute-done.59.refs_2_.refs_22_
  62.6 1.7 collective-permute-done.60.refs_3_.refs_23_
  64.3 2.2 %collective-permute-start.29 = (bf16[48,2048]{1,0:T(8,128)(2,1)S(1)}, bf16[48,2048]{1,0:T(8,128)(2,1)S(1)}, u32[]{:S(2)}, u32[]{:S(2)}) collective-permute-start(bf16[48,2048]{1,0:T(8,128)(2,1)S(1)} %get-tuple-element.156), channel_id=1, source_target_pairs={{0,3},{1,2},{2,1},{3,0},{4,7},{5,6},{6,5},{7,4},{8,11},{9,10},{10,... | collective-permute-start | bytes 589832 | tf_op jit(solution)/shard_map/ppermute | solution.py:242
  66.5 1.8 shard_map.143
  78.4 2.8 %collective-permute-done.63.refs_4_ = bf16[48,2048]{1,0:T(8,128)(2,1)S(1)} collective-permute-done((bf16[48,2048]{1,0:T(8,128)(2,1)S(1)}, bf16[48,2048]{1,0:T(8,128)(2,1)S(1)}, u32[]{:S(2)}, u32[]{:S(2)}) %collective-permute-start.63) | collective-permute-done | bytes 196640 | tf_op jit(solution)/shard_map/ppermute | solution.py:242
  82.7 4.1 %collective-permute-done.19.refs_2_.refs_10_ = bf16[48,2048]{1,0:T(8,128)(2,1)S(1)} collective-permute-done((bf16[48,2048]{1,0:T(8,128)(2,1)S(1)}, bf16[48,2048]{1,0:T(8,128)(2,1)S(1)}, u32[]{:S(2)}, u32[]{:S(2)}) %collective-permute-start.19) | collective-permute-done | bytes 196640 | tf_op jit(solution)/shard_map/ppermute | solution.py:242
  91.1 7.8 %collective-permute-done.71.refs_4_ = f32[8,128]{1,0:T(8,128)S(1)} collective-permute-done((f32[8,128]{1,0:T(8,128)S(1)}, f32[8,128]{1,0:T(8,128)S(1)}, u32[]{:S(2)}, u32[]{:S(2)}) %collective-permute-start.71) | collective-permute-done | bytes 4128 | tf_op jit(solution)/shard_map/ppermute | solution.py:242
  101.1 1.8 shard_map.141
  103.3 3.3 %collective-permute-done.22.refs_4_.refs_2_ = bf16[48,2048]{1,0:T(8,128)(2,1)S(1)} collective-permute-done((bf16[48,2048]{1,0:T(8,128)(2,1)S(1)}, bf16[48,2048]{1,0:T(8,128)(2,1)S(1)}, u32[]{:S(2)}, u32[]{:S(2)}) %collective-permute-start.22) | collective-permute-done | bytes 196640 | tf_op jit(solution)/shard_map/ppermute | solution.py:242
  107.1 2.8 %collective-permute-done.23.refs_5_.refs_3_ = bf16[48,2048]{1,0:T(8,128)(2,1)S(1)} collective-permute-done((bf16[48,2048]{1,0:T(8,128)(2,1)S(1)}, bf16[48,2048]{1,0:T(8,128)(2,1)S(1)}, u32[]{:S(2)}, u32[]{:S(2)}) %collective-permute-start.23) | collective-permute-done | bytes 196640 | tf_op jit(solution)/shard_map/ppermute | solution.py:242
  112.9 4.8 %collective-permute-done.56.refs_3_ = bf16[48,2048]{1,0:T(8,128)(2,1)S(1)} collective-permute-done((bf16[48,2048]{1,0:T(8,128)(2,1)S(1)}, bf16[48,2048]{1,0:T(8,128)(2,1)S(1)}, u32[]{:S(2)}, u32[]{:S(2)}) %collective-permute-start.56) | collective-permute-done | bytes 196640 | tf_op jit(solution)/shard_map/ppermute | solution.py:242
  117.7 3.4 %collective-permute-done.57.refs_4_ = bf16[48,2048]{1,0:T(8,128)(2,1)S(1)} collective-permute-done((bf16[48,2048]{1,0:T(8,128)(2,1)S(1)}, bf16[48,2048]{1,0:T(8,128)(2,1)S(1)}, u32[]{:S(2)}, u32[]{:S(2)}) %collective-permute-start.57) | collective-permute-done | bytes 196640 | tf_op jit(solution)/shard_map/ppermute | solution.py:242
  124.3 4.6 %collective-permute-done.45.block = bf16[128,2048]{1,0:T(8,128)(2,1)S(1)} collective-permute-done((bf16[128,2048]{1,0:T(8,128)(2,1)S(1)}, bf16[128,2048]{1,0:T(8,128)(2,1)S(1)}, u32[]{:S(2)}, u32[]{:S(2)}) %collective-permute-start.45) | collective-permute-done | bytes 524320 | tf_op jit(solution)/shard_map/ppermute | solution.py:242
  130.0 10.2 %collective-permute-done.30.refs_6_ = bf16[128,2048]{1,0:T(8,128)(2,1)S(1)} collective-permute-done((bf16[128,2048]{1,0:T(8,128)(2,1)S(1)}, bf16[128,2048]{1,0:T(8,128)(2,1)S(1)}, u32[]{:S(2)}, u32[]{:S(2)}) %collective-permute-start.30) | collective-permute-done | bytes 524320 | tf_op jit(solution)/shard_map/ppermute | solution.py:242
  144.5 6.3 %collective-permute-done.72.refs_8_ = f32[8,128]{1,0:T(8,128)S(1)} collective-permute-done((f32[8,128]{1,0:T(8,128)S(1)}, f32[8,128]{1,0:T(8,128)S(1)}, u32[]{:S(2)}, u32[]{:S(2)}) %collective-permute-start.72) | collective-permute-done | bytes 4128 | tf_op jit(solution)/shard_map/ppermute | solution.py:242
  154.1 1.8 shard_map.139
  174.9 3.8 %collective-permute-start.66 = (bf16[128,1024]{1,0:T(8,128)(2,1)S(1)}, bf16[128,1024]{1,0:T(8,128)(2,1)S(1)}, u32[]{:S(2)}, u32[]{:S(2)}) collective-permute-start(bf16[128,1024]{1,0:T(8,128)(2,1)S(1)} %shard_map.146), channel_id=1, source_target_pairs={{0,4},{1,5},{2,6},{3,7},{4,8},{5,9},{6,10},{7,11},{8,12},{9,13},{1... | collective-permute-start | bytes 786440 | tf_op jit(solution)/shard_map/ppermute | solution.py:242
  178.6 6.7 %shard_map.152 = (bf16[2048,384]{1,0:T(8,128)(2,1)}, bf16[2048,384]{1,0:T(8,128)(2,1)}, bf16[384,2048]{1,0:T(8,128)(2,1)}) custom-call(bf16[48,2048]{1,0:T(8,128)(2,1)S(1)} %get-tuple-element.119.refs_0_, bf16[48,2048]{1,0:T(8,128)(2,1)S(1)} %collective-permute-done.refs_1_, bf16[48,2048]{1,0:T(8,128)(2,1)S(1)} %collective-permute-done.1.refs_2_, ...), custom_call_target="tpu_custom_call" | custom-call | flops 3623878656 | bytes 12779520 | tf_op jit(solution)/shard_map/pallas_call | solution.py:214
  185.3 4.7 %collective-permute-done.73.refs_4_ = f32[8,128]{1,0:T(8,128)S(1)} collective-permute-done((f32[8,128]{1,0:T(8,128)S(1)}, f32[8,128]{1,0:T(8,128)S(1)}, u32[]{:S(2)}, u32[]{:S(2)}) %collective-permute-start.73) | collective-permute-done | bytes 4128 | tf_op jit(solution)/shard_map/ppermute | solution.py:242
  192.3 3.4 %collective-permute-done.70 = bf16[128,1024]{1,0:T(8,128)(2,1)S(1)} collective-permute-done((bf16[128,1024]{1,0:T(8,128)(2,1)S(1)}, bf16[128,1024]{1,0:T(8,128)(2,1)S(1)}, u32[]{:S(2)}, u32[]{:S(2)}) %collective-permute-start.70) | collective-permute-done | bytes 262176 | tf_op jit(solution)/shard_map/ppermute | solution.py:242
  195.7 5.6 %collective-permute-done.66 = bf16[128,1024]{1,0:T(8,128)(2,1)S(1)} collective-permute-done((bf16[128,1024]{1,0:T(8,128)(2,1)S(1)}, bf16[128,1024]{1,0:T(8,128)(2,1)S(1)}, u32[]{:S(2)}, u32[]{:S(2)}) %collective-permute-start.66) | collective-permute-done | bytes 262176 | tf_op jit(solution)/shard_map/ppermute | solution.py:242
  202.2 4.7 %collective-permute-done.32.refs_6_ = bf16[128,1024]{1,0:T(8,128)(2,1)S(1)} collective-permute-done((bf16[128,1024]{1,0:T(8,128)(2,1)S(1)}, bf16[128,1024]{1,0:T(8,128)(2,1)S(1)}, u32[]{:S(2)}, u32[]{:S(2)}) %collective-permute-start.32) | collective-permute-done | bytes 262176 | tf_op jit(solution)/shard_map/ppermute | solution.py:242
  206.9 4.6 %collective-permute-done.36.refs_7_ = bf16[128,1024]{1,0:T(8,128)(2,1)S(1)} collective-permute-done((bf16[128,1024]{1,0:T(8,128)(2,1)S(1)}, bf16[128,1024]{1,0:T(8,128)(2,1)S(1)}, u32[]{:S(2)}, u32[]{:S(2)}) %collective-permute-start.36) | collective-permute-done | bytes 262176 | tf_op jit(solution)/shard_map/ppermute | solution.py:242
  (175 shorter events, 87.4 us)
Async XLA Ops:
  6.2 33.2 %collective-permute-start.9 = (bf16[128,2048]{1,0:T(8,128)(2,1)}, bf16[128,2048]{1,0:T(8,128)(2,1)S(1)}, u32[]{:S(2)}, u32[]{:S(2)}) collective-permute-start(bf16[128,2048]{1,0:T(8,128)(2,1)} %block.3), channel_id=1, source_target_pairs={{0,4},{1,5},{2,6},{3,7},{4,8},{5,9},{6,10},{7,11},{8,12},{9,13},{1... | collective-permute-start | bytes 1572872 | tf_op jit(solution)/shard_map/ppermute | solution.py:242
  8.0 38.4 %collective-permute-start.43 = (bf16[128,2048]{1,0:T(8,128)(2,1)}, bf16[128,2048]{1,0:T(8,128)(2,1)S(1)}, u32[]{:S(2)}, u32[]{:S(2)}) collective-permute-start(bf16[128,2048]{1,0:T(8,128)(2,1)} %block.5), channel_id=1, source_target_pairs={{0,4},{1,5},{2,6},{3,7},{4,8},{5,9},{6,10},{7,11},{8,12},{9,13},{1... | collective-permute-start | bytes 1572872 | tf_op jit(solution)/shard_map/ppermute | solution.py:242
  12.4 11.2 %collective-permute-start.37 = (bf16[48,2048]{1,0:T(8,128)(2,1)S(1)}, bf16[48,2048]{1,0:T(8,128)(2,1)S(1)}, u32[]{:S(2)}, u32[]{:S(2)}) collective-permute-start(bf16[48,2048]{1,0:T(8,128)(2,1)S(1)} %get-tuple-element.163), channel_id=1, source_target_pairs={{0,1},{1,0},{2,3},{3,2},{4,5},{5,4},{6,7},{7,6},{8,9},{9,8},{10,11... | collective-permute-start | bytes 589832 | tf_op jit(solution)/shard_map/ppermute | solution.py:242
  26.3 19.0 %collective-permute-start.40 = (bf16[48,2048]{1,0:T(8,128)(2,1)S(1)}, bf16[48,2048]{1,0:T(8,128)(2,1)S(1)}, u32[]{:S(2)}, u32[]{:S(2)}) collective-permute-start(bf16[48,2048]{1,0:T(8,128)(2,1)S(1)} %get-tuple-element.169), channel_id=1, source_target_pairs={{0,1},{1,0},{2,3},{3,2},{4,5},{5,4},{6,7},{7,6},{8,9},{9,8},{10,11... | collective-permute-start | bytes 589832 | tf_op jit(solution)/shard_map/ppermute | solution.py:242
  26.4 21.4 %collective-permute-start.41 = (bf16[48,2048]{1,0:T(8,128)(2,1)S(1)}, bf16[48,2048]{1,0:T(8,128)(2,1)S(1)}, u32[]{:S(2)}, u32[]{:S(2)}) collective-permute-start(bf16[48,2048]{1,0:T(8,128)(2,1)S(1)} %get-tuple-element.170), channel_id=1, source_target_pairs={{0,2},{1,3},{2,0},{3,1},{4,6},{5,7},{6,4},{7,5},{8,10},{9,11},{10,... | collective-permute-start | bytes 589832 | tf_op jit(solution)/shard_map/ppermute | solution.py:242
  47.7 11.8 %collective-permute-start.58 = (bf16[48,2048]{1,0:T(8,128)(2,1)S(1)}, bf16[48,2048]{1,0:T(8,128)(2,1)S(1)}, u32[]{:S(2)}, u32[]{:S(2)}) collective-permute-start(bf16[48,2048]{1,0:T(8,128)(2,1)S(1)} %get-tuple-element.196), channel_id=1, source_target_pairs={{0,1},{1,0},{2,3},{3,2},{4,5},{5,4},{6,7},{7,6},{8,9},{9,8},{10,11... | collective-permute-start | bytes 589832 | tf_op jit(solution)/shard_map/ppermute | solution.py:242
  48.6 22.4 %collective-permute-start.10 = (bf16[128,2048]{1,0:T(8,128)(2,1)S(1)}, bf16[128,2048]{1,0:T(8,128)(2,1)S(1)}, u32[]{:S(2)}, u32[]{:S(2)}) collective-permute-start(bf16[128,2048]{1,0:T(8,128)(2,1)S(1)} %collective-permute-done.9.block), channel_id=1, source_target_pairs={{0,4},{1,5},{2,6},{3,7},{4,8},{5,9},{6,10},{7,11},{8,12},{9,13},{1... | collective-permute-start | bytes 1572872 | tf_op jit(solution)/shard_map/ppermute | solution.py:242
  48.6 26.9 %collective-permute-start.44 = (bf16[128,2048]{1,0:T(8,128)(2,1)S(1)}, bf16[128,2048]{1,0:T(8,128)(2,1)S(1)}, u32[]{:S(2)}, u32[]{:S(2)}) collective-permute-start(bf16[128,2048]{1,0:T(8,128)(2,1)S(1)} %collective-permute-done.43.block), channel_id=1, source_target_pairs={{0,4},{1,5},{2,6},{3,7},{4,8},{5,9},{6,10},{7,11},{8,12},{9,13},{1... | collective-permute-start | bytes 1572872 | tf_op jit(solution)/shard_map/ppermute | solution.py:242
  74.3 12.5 %collective-permute-start.19 = (bf16[48,2048]{1,0:T(8,128)(2,1)S(1)}, bf16[48,2048]{1,0:T(8,128)(2,1)S(1)}, u32[]{:S(2)}, u32[]{:S(2)}) collective-permute-start(bf16[48,2048]{1,0:T(8,128)(2,1)S(1)} %get-tuple-element.141), channel_id=1, source_target_pairs={{0,2},{1,3},{2,0},{3,1},{4,6},{5,7},{6,4},{7,5},{8,10},{9,11},{10,... | collective-permute-start | bytes 589832 | tf_op jit(solution)/shard_map/ppermute | solution.py:242
  75.5 14.1 %collective-permute-start.20 = (bf16[48,2048]{1,0:T(8,128)(2,1)S(1)}, bf16[48,2048]{1,0:T(8,128)(2,1)S(1)}, u32[]{:S(2)}, u32[]{:S(2)}) collective-permute-start(bf16[48,2048]{1,0:T(8,128)(2,1)S(1)} %get-tuple-element.142), channel_id=1, source_target_pairs={{0,3},{1,2},{2,1},{3,0},{4,7},{5,6},{6,5},{7,4},{8,11},{9,10},{10,... | collective-permute-start | bytes 589832 | tf_op jit(solution)/shard_map/ppermute | solution.py:242
  78.4 20.5 %collective-permute-start.52 = (bf16[48,2048]{1,0:T(8,128)(2,1)S(1)}, bf16[48,2048]{1,0:T(8,128)(2,1)S(1)}, u32[]{:S(2)}, u32[]{:S(2)}) collective-permute-start(bf16[48,2048]{1,0:T(8,128)(2,1)S(1)} %get-tuple-element.185), channel_id=1, source_target_pairs={{0,1},{1,0},{2,3},{3,2},{4,5},{5,4},{6,7},{7,6},{8,9},{9,8},{10,11... | collective-permute-start | bytes 589832 | tf_op jit(solution)/shard_map/ppermute | solution.py:242
  81.1 18.8 %collective-permute-start.53 = (bf16[48,2048]{1,0:T(8,128)(2,1)S(1)}, bf16[48,2048]{1,0:T(8,128)(2,1)S(1)}, u32[]{:S(2)}, u32[]{:S(2)}) collective-permute-start(bf16[48,2048]{1,0:T(8,128)(2,1)S(1)} %get-tuple-element.186), channel_id=1, source_target_pairs={{0,2},{1,3},{2,0},{3,1},{4,6},{5,7},{6,4},{7,5},{8,10},{9,11},{10,... | collective-permute-start | bytes 589832 | tf_op jit(solution)/shard_map/ppermute | solution.py:242
  82.7 28.1 %collective-permute-start.11 = (bf16[128,2048]{1,0:T(8,128)(2,1)S(1)}, bf16[128,2048]{1,0:T(8,128)(2,1)S(1)}, u32[]{:S(2)}, u32[]{:S(2)}) collective-permute-start(bf16[128,2048]{1,0:T(8,128)(2,1)S(1)} %collective-permute-done.10.block), channel_id=1, source_target_pairs={{0,4},{1,5},{2,6},{3,7},{4,8},{5,9},{6,10},{7,11},{8,12},{9,13},{1... | collective-permute-start | bytes 1572872 | tf_op jit(solution)/shard_map/ppermute | solution.py:242
  86.8 14.3 %collective-permute-start.54 = (bf16[48,2048]{1,0:T(8,128)(2,1)S(1)}, bf16[48,2048]{1,0:T(8,128)(2,1)S(1)}, u32[]{:S(2)}, u32[]{:S(2)}) collective-permute-start(bf16[48,2048]{1,0:T(8,128)(2,1)S(1)} %get-tuple-element.187), channel_id=1, source_target_pairs={{0,3},{1,2},{2,1},{3,0},{4,7},{5,6},{6,5},{7,4},{8,11},{9,10},{10,... | collective-permute-start | bytes 589832 | tf_op jit(solution)/shard_map/ppermute | solution.py:242
  101.1 21.2 %collective-permute-start.64 = (bf16[128,2048]{1,0:T(8,128)(2,1)S(1)}, bf16[128,2048]{1,0:T(8,128)(2,1)S(1)}, u32[]{:S(2)}, u32[]{:S(2)}) collective-permute-start(bf16[128,2048]{1,0:T(8,128)(2,1)S(1)} %shard_map.144), channel_id=1, source_target_pairs={{0,4},{1,5},{2,6},{3,7},{4,8},{5,9},{6,10},{7,11},{8,12},{9,13},{1... | collective-permute-start | bytes 1572872 | tf_op jit(solution)/shard_map/ppermute | solution.py:242
  106.7 22.3 %collective-permute-start.45 = (bf16[128,2048]{1,0:T(8,128)(2,1)S(1)}, bf16[128,2048]{1,0:T(8,128)(2,1)S(1)}, u32[]{:S(2)}, u32[]{:S(2)}) collective-permute-start(bf16[128,2048]{1,0:T(8,128)(2,1)S(1)} %collective-permute-done.44.block), channel_id=1, source_target_pairs={{0,4},{1,5},{2,6},{3,7},{4,8},{5,9},{6,10},{7,11},{8,12},{9,13},{1... | collective-permute-start | bytes 1572872 | tf_op jit(solution)/shard_map/ppermute | solution.py:242
  109.9 30.2 %collective-permute-start.30 = (bf16[128,2048]{1,0:T(8,128)(2,1)S(1)}, bf16[128,2048]{1,0:T(8,128)(2,1)S(1)}, u32[]{:S(2)}, u32[]{:S(2)}) collective-permute-start(bf16[128,2048]{1,0:T(8,128)(2,1)S(1)} %shard_map.130), channel_id=1, source_target_pairs={{0,4},{1,5},{2,6},{3,7},{4,8},{5,9},{6,10},{7,11},{8,12},{9,13},{1... | collective-permute-start | bytes 1572872 | tf_op jit(solution)/shard_map/ppermute | solution.py:242
  117.7 22.5 %collective-permute-start.12 = (bf16[48,2048]{1,0:T(8,128)(2,1)S(1)}, bf16[48,2048]{1,0:T(8,128)(2,1)S(1)}, u32[]{:S(2)}, u32[]{:S(2)}) collective-permute-start(bf16[48,2048]{1,0:T(8,128)(2,1)S(1)} %get-tuple-element.130), channel_id=1, source_target_pairs={{0,1},{1,0},{2,3},{3,2},{4,5},{5,4},{6,7},{7,6},{8,9},{9,8},{10,11... | collective-permute-start | bytes 589832 | tf_op jit(solution)/shard_map/ppermute | solution.py:242
  121.2 20.0 %collective-permute-start.13 = (bf16[48,2048]{1,0:T(8,128)(2,1)S(1)}, bf16[48,2048]{1,0:T(8,128)(2,1)S(1)}, u32[]{:S(2)}, u32[]{:S(2)}) collective-permute-start(bf16[48,2048]{1,0:T(8,128)(2,1)S(1)} %get-tuple-element.131), channel_id=1, source_target_pairs={{0,2},{1,3},{2,0},{3,1},{4,6},{5,7},{6,4},{7,5},{8,10},{9,11},{10,... | collective-permute-start | bytes 589832 | tf_op jit(solution)/shard_map/ppermute | solution.py:242
  122.2 20.7 %collective-permute-start.14 = (bf16[48,2048]{1,0:T(8,128)(2,1)S(1)}, bf16[48,2048]{1,0:T(8,128)(2,1)S(1)}, u32[]{:S(2)}, u32[]{:S(2)}) collective-permute-start(bf16[48,2048]{1,0:T(8,128)(2,1)S(1)} %get-tuple-element.132), channel_id=1, source_target_pairs={{0,3},{1,2},{2,1},{3,0},{4,7},{5,6},{6,5},{7,4},{8,11},{9,10},{10,... | collective-permute-start | bytes 589832 | tf_op jit(solution)/shard_map/ppermute | solution.py:242
  128.9 38.2 %collective-permute-start.65 = (bf16[128,2048]{1,0:T(8,128)(2,1)S(1)}, bf16[128,2048]{1,0:T(8,128)(2,1)S(1)}, u32[]{:S(2)}, u32[]{:S(2)}) collective-permute-start(bf16[128,2048]{1,0:T(8,128)(2,1)S(1)} %shard_map.145), channel_id=1, source_target_pairs={{0,4},{1,5},{2,6},{3,7},{4,8},{5,9},{6,10},{7,11},{8,12},{9,13},{1... | collective-permute-start | bytes 1572872 | tf_op jit(solution)/shard_map/ppermute | solution.py:242
  140.2 11.7 %collective-permute-start.47 = (bf16[48,2048]{1,0:T(8,128)(2,1)S(1)}, bf16[48,2048]{1,0:T(8,128)(2,1)S(1)}, u32[]{:S(2)}, u32[]{:S(2)}) collective-permute-start(bf16[48,2048]{1,0:T(8,128)(2,1)S(1)} %get-tuple-element.175), channel_id=1, source_target_pairs={{0,2},{1,3},{2,0},{3,1},{4,6},{5,7},{6,4},{7,5},{8,10},{9,11},{10,... | collective-permute-start | bytes 589832 | tf_op jit(solution)/shard_map/ppermute | solution.py:242
  141.2 11.5 %collective-permute-start.48 = (bf16[48,2048]{1,0:T(8,128)(2,1)S(1)}, bf16[48,2048]{1,0:T(8,128)(2,1)S(1)}, u32[]{:S(2)}, u32[]{:S(2)}) collective-permute-start(bf16[48,2048]{1,0:T(8,128)(2,1)S(1)} %get-tuple-element.176), channel_id=1, source_target_pairs={{0,3},{1,2},{2,1},{3,0},{4,7},{5,6},{6,5},{7,4},{8,11},{9,10},{10,... | collective-permute-start | bytes 589832 | tf_op jit(solution)/shard_map/ppermute | solution.py:242
  161.9 12.9 %collective-permute-start.3 = (bf16[48,2048]{1,0:T(8,128)(2,1)S(1)}, bf16[48,2048]{1,0:T(8,128)(2,1)S(1)}, u32[]{:S(2)}, u32[]{:S(2)}) collective-permute-start(bf16[48,2048]{1,0:T(8,128)(2,1)S(1)} %get-tuple-element.124), channel_id=1, source_target_pairs={{0,1},{1,0},{2,3},{3,2},{4,5},{5,4},{6,7},{7,6},{8,9},{9,8},{10,11... | collective-permute-start | bytes 589832 | tf_op jit(solution)/shard_map/ppermute | solution.py:242
  162.7 12.2 %collective-permute-start.4 = (bf16[48,2048]{1,0:T(8,128)(2,1)S(1)}, bf16[48,2048]{1,0:T(8,128)(2,1)S(1)}, u32[]{:S(2)}, u32[]{:S(2)}) collective-permute-start(bf16[48,2048]{1,0:T(8,128)(2,1)S(1)} %get-tuple-element.125), channel_id=1, source_target_pairs={{0,2},{1,3},{2,0},{3,1},{4,6},{5,7},{6,4},{7,5},{8,10},{9,11},{10,... | collective-permute-start | bytes 589832 | tf_op jit(solution)/shard_map/ppermute | solution.py:242
  172.1 13.2 %collective-permute-start.5 = (bf16[48,2048]{1,0:T(8,128)(2,1)S(1)}, bf16[48,2048]{1,0:T(8,128)(2,1)S(1)}, u32[]{:S(2)}, u32[]{:S(2)}) collective-permute-start(bf16[48,2048]{1,0:T(8,128)(2,1)S(1)} %get-tuple-element.126), channel_id=1, source_target_pairs={{0,3},{1,2},{2,1},{3,0},{4,7},{5,6},{6,5},{7,4},{8,11},{9,10},{10,... | collective-permute-start | bytes 589832 | tf_op jit(solution)/shard_map/ppermute | solution.py:242
  173.4 18.2 %collective-permute-start.31 = (bf16[128,2048]{1,0:T(8,128)(2,1)S(1)}, bf16[128,2048]{1,0:T(8,128)(2,1)S(1)}, u32[]{:S(2)}, u32[]{:S(2)}) collective-permute-start(bf16[128,2048]{1,0:T(8,128)(2,1)S(1)} %shard_map.131), channel_id=1, source_target_pairs={{0,4},{1,5},{2,6},{3,7},{4,8},{5,9},{6,10},{7,11},{8,12},{9,13},{1... | collective-permute-start | bytes 1572872 | tf_op jit(solution)/shard_map/ppermute | solution.py:242
  174.5 15.5 %collective-permute-start.73 = (f32[8,128]{1,0:T(8,128)S(1)}, f32[8,128]{1,0:T(8,128)S(1)}, u32[]{:S(2)}, u32[]{:S(2)}) collective-permute-start(f32[8,128]{1,0:T(8,128)S(1)} %shard_map.150), channel_id=1, source_target_pairs={{0,4},{1,5},{2,6},{3,7},{4,8},{5,9},{6,10},{7,11},{8,12},{9,13},{1... | collective-permute-start | bytes 12296 | tf_op jit(solution)/shard_map/ppermute | solution.py:242
  174.8 20.9 %collective-permute-start.70 = (bf16[128,1024]{1,0:T(8,128)(2,1)S(1)}, bf16[128,1024]{1,0:T(8,128)(2,1)S(1)}, u32[]{:S(2)}, u32[]{:S(2)}) collective-permute-start(bf16[128,1024]{1,0:T(8,128)(2,1)S(1)} %shard_map.147), channel_id=1, source_target_pairs={{0,4},{1,5},{2,6},{3,7},{4,8},{5,9},{6,10},{7,11},{8,12},{9,13},{1... | collective-permute-start | bytes 786440 | tf_op jit(solution)/shard_map/ppermute | solution.py:242
  174.9 26.4 %collective-permute-start.66 = (bf16[128,1024]{1,0:T(8,128)(2,1)S(1)}, bf16[128,1024]{1,0:T(8,128)(2,1)S(1)}, u32[]{:S(2)}, u32[]{:S(2)}) collective-permute-start(bf16[128,1024]{1,0:T(8,128)(2,1)S(1)} %shard_map.146), channel_id=1, source_target_pairs={{0,4},{1,5},{2,6},{3,7},{4,8},{5,9},{6,10},{7,11},{8,12},{9,13},{1... | collective-permute-start | bytes 786440 | tf_op jit(solution)/shard_map/ppermute | solution.py:242
  191.8 15.1 %collective-permute-start.32 = (bf16[128,1024]{1,0:T(8,128)(2,1)S(1)}, bf16[128,1024]{1,0:T(8,128)(2,1)S(1)}, u32[]{:S(2)}, u32[]{:S(2)}) collective-permute-start(bf16[128,1024]{1,0:T(8,128)(2,1)S(1)} %shard_map.132), channel_id=1, source_target_pairs={{0,4},{1,5},{2,6},{3,7},{4,8},{5,9},{6,10},{7,11},{8,12},{9,13},{1... | collective-permute-start | bytes 786440 | tf_op jit(solution)/shard_map/ppermute | solution.py:242
  192.2 19.3 %collective-permute-start.36 = (bf16[128,1024]{1,0:T(8,128)(2,1)S(1)}, bf16[128,1024]{1,0:T(8,128)(2,1)S(1)}, u32[]{:S(2)}, u32[]{:S(2)}) collective-permute-start(bf16[128,1024]{1,0:T(8,128)(2,1)S(1)} %shard_map.133), channel_id=1, source_target_pairs={{0,4},{1,5},{2,6},{3,7},{4,8},{5,9},{6,10},{7,11},{8,12},{9,13},{1... | collective-permute-start | bytes 786440 | tf_op jit(solution)/shard_map/ppermute | solution.py:242
  (52 other events, 355.6 us)
